TPU v7x, 32 devices: a whole 2x2x4 slice. The times are simulated.
32 devices in a mesh: facet: 16 (over z, x, core), chan: 2 (over y).
Axes of the slice: x: 2, y: 2, z: 4, core: 2. Of those that a mesh axis runs over, the one named last changes fastest.
Arguments:
- x_start: float32 [256, 256, 128], P('chan', 'facet'), may hold values from 0 to 2
- dirty: float32 [256, 256, 128], P('chan', 'facet'), may hold values from -6 to 6
- weights: float32 [8, 256, 128], P(None, 'facet'), may hold values from 1 to 16
- filters: float32 [8, 16], replicated, may hold values from -1.5 to 1.5
- basis: float32 [16, 256, 32], P('facet', 'chan'), may hold values from -1 to 1
- bounds: float32 [32], replicated, may hold values from 0.1 to 3
- margin_rows: int32 [16], replicated, may hold values from 1 to 15, as said below
Outputs:
- image: float32 [256, 256, 128], P('chan', 'facet')
- wavelet_dual: float32 [8, 256, 256, 128], P(None, 'chan', 'facet')
- spectral_dual: float32 [256, 256, 128], P('chan', 'facet')
Inputs may be any that keep to these rules, and one draw needn't show every extreme that they name: `margin_rows`: each facet borrows 1 to 15 rows; some facet after the first borrows 15.
All inputs are finite; a program needn't handle non-finite values.
Results may differ from a plain program's by a relative error of at most 0.0001.
Values sent between devices are 32-bit elements; how exact they have to be, the bound alone decides.
No kernel may reach another device: no remote copies, remote signals or barrier semaphores. Data moves between devices by JAX's collectives and lax.ppermute only.
A program may use at most 128 MiB of HBM per device.

v0:
```python
import jax
import jax.numpy as jnp
from jax import lax
from jax.sharding import PartitionSpec as P

ITERS = 2


primal_step = 0.5
dual_step = 0.5


def from_behind(value, axis, steps):
    count = lax.axis_size(axis)
    initial, last = (max(0, -steps), min(count, count - steps))
    return lax.ppermute(value, axis, [(source, source + steps) for source in range(initial, last)])


def build_toeplitz(filters, height):
    bases, tap_count = filters.shape
    reach_rows = tap_count - 1
    tap_mask = jnp.arange(tap_count)[None, :] < 2 * (jnp.arange(bases)[:, None] + 1)
    tap_values = jnp.where(tap_mask, filters, jnp.zeros_like(filters))
    tap_index = jnp.arange(height)[:, None] - jnp.arange(height + reach_rows)[None, :] + reach_rows
    one_hot = (tap_index[None, :, :] == jnp.arange(tap_count)[:, None, None]).astype(filters.dtype)
    return jnp.einsum("bk,krs->brs", tap_values, one_hot, precision=lax.Precision.HIGHEST)


def body(x_start, dirty, weights, filters, basis, bounds, margin_rows):
    height = x_start.shape[1]
    bases, tap_count = filters.shape
    reach_rows = tap_count - 1
    toeplitz = build_toeplitz(filters, height)
    facet_index = lax.axis_index("facet")
    facet_count = lax.axis_size("facet")
    offsets = jnp.arange(reach_rows)
    own_margin = lax.dynamic_index_in_dim(margin_rows, facet_index, 0, keepdims=False)
    next_margin = lax.dynamic_index_in_dim(
        margin_rows, jnp.minimum(facet_index + 1, facet_count - 1), 0, keepdims=False
    )
    own_edge = (reach_rows - offsets <= own_margin).astype(jnp.float32)
    next_edge = (reach_rows - offsets <= next_margin).astype(jnp.float32)
    loading = basis[0]
    limits = bounds[:, None, None]
    image = x_start
    wavelet = jnp.zeros((bases,) + x_start.shape, jnp.float32)
    spectral = jnp.zeros_like(x_start)
    for iteration in range(ITERS):
        gradient = image - dirty + spectral
        if iteration > 0:
            interior = jnp.einsum(
                "brs,bcrn->csn",
                toeplitz[:, :, reach_rows:],
                wavelet,
                precision=lax.Precision.HIGHEST,
            )
            states = from_behind(wavelet[:, :, :reach_rows, :], "facet", -1)
            border_sum = (
                jnp.einsum(
                    "brs,bcrn->csn",
                    toeplitz[:, :reach_rows, :reach_rows],
                    states,
                    precision=lax.Precision.HIGHEST,
                )
                * next_edge[None, :, None]
            )
            gradient = gradient + (
                interior + jnp.pad(border_sum, ((0, 0), (height - reach_rows, 0), (0, 0)))
            )
        updated = jnp.maximum(image - primal_step * gradient, 0.0)
        reflected = 2.0 * updated - image
        above_rows = from_behind(reflected[:, height - reach_rows :, :], "facet", 1)
        extended = jnp.concatenate([above_rows * own_edge[None, :, None], reflected], axis=1)
        lifted = wavelet + dual_step * jnp.einsum(
            "brs,csn->bcrn", toeplitz, extended, precision=lax.Precision.HIGHEST
        )
        spectral_lift = spectral + dual_step * reflected
        coeff_part = jnp.einsum(
            "cq,cpn->qpn", loading, spectral_lift, precision=lax.Precision.HIGHEST
        )
        squares = jnp.sum(lifted * lifted, axis=1)
        coeff_total, square_total = lax.psum((coeff_part, squares), "chan")
        clipped = jnp.clip(coeff_total, -limits, limits)
        magnitudes = jnp.sqrt(square_total)
        wavelet = lifted * (weights / jnp.maximum(magnitudes, weights))[:, None]
        spectral = jnp.einsum("cq,qpn->cpn", loading, clipped, precision=lax.Precision.HIGHEST)
        image = updated
    return (image, wavelet, spectral)


def solution(mesh):
    in_specs = (
        P("chan", "facet", None),
        P("chan", "facet", None),
        P(None, "facet", None),
        P(),
        P("facet", "chan", None),
        P(),
        P(),
    )
    out_specs = (P("chan", "facet", None), P(None, "chan", "facet", None), P("chan", "facet", None))
    return jax.shard_map(body, mesh=mesh, in_specs=in_specs, out_specs=out_specs, check_vma=False)
```

profile of v0, /device:TPU:16, one launch (start us, length us, event | category | flops | bytes accessed | tf_op | source)
XLA Modules:
  0.0 268.0 jit_solution(2970434713724990739)
XLA Ops:
  8.8 1.6 copy.28
  11.7 1.9 collective-permute-start
  15.1 1.9 convolution_bitcast_fusion.4
  17.0 11.3 %collective-permute-done = f32[128,15,128]{0,2,1:T(8,128)} collective-permute-done((f32[128,15,128]{0,2,1:T(8,128)}, f32[128,15,128]{0,2,1:T(8,128)}, u32[]{:S(2)}, u32[]{:S(2)}) %collective-permute-start) | collective-permute-done | bytes 983072 | tf_op jit(solution)/shard_map/ppermute | solution.py:16
  31.0 3.2 %copy.44 = f32[128,31,128,1]{2,1,3,0:T(8,128)} copy(f32[128,31,128,1]{0,2,1,3:T(8,128)} %maximum_bitcast_fusion) | data formatting | bytes 4063232 | tf_op jit(solution)/shard_map/concatenate | solution.py:73
  34.2 11.1 %fusion.1 = (f32[8,16,128]{2,1,0:T(8,128)}, f32[128,128,8,16]{1,3,2,0:T(8,128)}) fusion(f32[128,31,128,1]{2,1,3,0:T(8,128)} %copy.44, f32[8,16,31]{2,0,1:T(8,128)S(1)} %fusion.24), kind=kOutput, calls=%fused_computation.4 | convolution fusion | flops 786415616 | bytes 10501632 | tf_op jit(solution)/shard_map/brs,csn->bcrn/dot_general | solution.py:74
  45.6 24.6 %all-reduce.8.cloned.1.call-done = (f32[8,16,128]{2,1,0:T(8,128)}, f32[32,16,128]{2,0,1:T(8,128)}) async-done(((f32[8,16,128]{2,1,0:T(8,128)}, f32[32,16,128]{2,0,1:T(8,128)}), (f32[8,16,128]{2,1,0:T(8,128)}, f32[32,16,128]{2,0,1:T(8,128)})) %all-reduce.8.cloned.1.call-update) | async-done | bytes 327696 | tf_op jit(solution)/shard_map/psum | solution.py:82
  71.0 4.2 %bitcast_multiply_fusion = f32[8,128,16,128]{3,2,0,1:T(8,128)S(1)} fusion(f32[128,128,8,16]{1,3,2,0:T(8,128)} %get-tuple-element.18, f32[8,16,128]{2,1,0:T(8,128)S(1)} %fusion.25), kind=kLoop, calls=%fused_computation.1 | loop fusion | flops 2097152 | bytes 16842752 | tf_op jit(solution)/shard_map/mul | solution.py:85
  75.3 3.4 %copy-done.1 = f32[8,128,16,128]{3,2,0,1:T(8,128)} copy-done((f32[8,128,16,128]{3,2,0,1:T(8,128)}, f32[8,128,16,128]{3,2,0,1:T(8,128)S(1)}, u32[]{:S(2)}) %copy-start.1) | copy-done | bytes 8388632
  78.7 7.6 %copy.35 = f32[8,128,15,128]{3,1,2,0:T(8,128)} copy(f32[8,128,15,128]{3,2,0,1:T(8,128)S(1)} %bitcast.77) | data formatting | bytes 15728640 | tf_op jit(solution)/shard_map/slice | solution.py:57
  86.3 3.0 %collective-permute-start.1 = (f32[8,128,15,128]{3,1,2,0:T(8,128)}, f32[8,128,15,128]{3,1,2,0:T(8,128)}, u32[]{:S(2)}, u32[]{:S(2)}) collective-permute-start(f32[8,128,15,128]{3,1,2,0:T(8,128)} %copy.35), channel_id=1, source_target_pairs={{2,0},{4,2},{6,4},{8,6},{10,8},{12,10},{14,12},{16,14},{18,16},{20... | collective-permute-start | bytes 23592968 | tf_op jit(solution)/shard_map/ppermute | solution.py:16
  91.2 6.8 %convolution_bitcast_fusion.1 = f32[128,128,16]{1,2,0:T(8,128)S(1)} fusion(f32[8,128,16,128]{3,2,0,1:T(8,128)} %copy-done.1, f32[8,16,16]{1,2,0:T(8,128)S(1)} %copy.33), kind=kOutput, calls=%fused_computation.13 | convolution fusion | flops 402653184 | bytes 9445376 | tf_op jit(solution)/shard_map/brs,bcrn->csn/dot_general | solution.py:51
  99.4 75.3 %collective-permute-done.1 = f32[8,128,15,128]{3,1,2,0:T(8,128)} collective-permute-done((f32[8,128,15,128]{3,1,2,0:T(8,128)}, f32[8,128,15,128]{3,1,2,0:T(8,128)}, u32[]{:S(2)}, u32[]{:S(2)}) %collective-permute-start.1) | collective-permute-done | bytes 7864352 | tf_op jit(solution)/shard_map/ppermute | solution.py:16
  174.7 11.6 %fusion.4 = f32[128,128,15]{1,2,0:T(8,128)S(1)} fusion(f32[8,128,15,128]{3,1,2,0:T(8,128)} %collective-permute-done.1, f32[8,16,31]{2,0,1:T(8,128)S(1)} %fusion.24), kind=kOutput, calls=%fused_computation.11 | convolution fusion | flops 353894400 | bytes 8908800 | tf_op jit(solution)/shard_map/brs,bcrn->csn/dot_general | solution.py:59
  189.0 3.4 %multiply_subtract_fusion = (f32[128,16,128]{0,2,1:T(8,128)S(1)}, f32[128,16,128]{0,2,1:T(8,128)S(1)}, f32[128,16,128]{0,2,1:T(8,128)S(1)}) fusion(f32[128,16,128]{0,2,1:T(8,128)S(1)} %copy.28, f32[128,16,128]{0,2,1:T(8,128)S(1)} %copy.27, f32[128,15,128]{0,2,1:T(8,128)S(1)} %multiply_bitcast_fusion, f32[128,128,16]{0,1,2:T(8,128)} %copy.34, ...), kind=kOutput, calls=%fused_computation.24 | convolution fusion | flops 104202240 | bytes 7553280 | tf_op jit(solution)/shard_map/cq,qpn->cpn/dot_general | solution.py:86
  192.5 3.0 %collective-permute-start.2 = (f32[128,15,128]{0,2,1:T(8,128)S(1)}, f32[128,15,128]{0,2,1:T(8,128)S(1)}, u32[]{:S(2)}, u32[]{:S(2)}) collective-permute-start(f32[128,15,128]{0,2,1:T(8,128)S(1)} %slice.24), channel_id=1, source_target_pairs={{0,2},{2,4},{4,6},{6,8},{8,10},{10,12},{12,14},{14,16},{16,18},{18... | collective-permute-start | bytes 2949128 | tf_op jit(solution)/shard_map/ppermute | solution.py:16
  195.5 1.9 convolution_bitcast_fusion.3
  197.4 11.6 %collective-permute-done.2 = f32[128,15,128]{0,2,1:T(8,128)S(1)} collective-permute-done((f32[128,15,128]{0,2,1:T(8,128)S(1)}, f32[128,15,128]{0,2,1:T(8,128)S(1)}, u32[]{:S(2)}, u32[]{:S(2)}) %collective-permute-start.2) | collective-permute-done | bytes 983072 | tf_op jit(solution)/shard_map/ppermute | solution.py:16
  210.6 2.4 copy.49
  213.0 11.9 %multiply_reduce_fusion = (f32[8,16,128]{2,1,0:T(8,128)}, f32[8,128,16,128]{3,2,0,1:T(8,128)}) fusion(f32[8,128,16,128]{3,2,0,1:T(8,128)} %copy-done.1, f32[128,31,128,1]{2,1,3,0:T(8,128)S(1)} %copy.49, f32[8,16,31]{2,0,1:T(8,128)S(1)} %fusion.24), kind=kOutput, calls=%fused_computation.5 | convolution fusion | flops 788512768 | bytes 18890240 | tf_op jit(solution)/shard_map/brs,csn->bcrn/dot_general | solution.py:74
  226.3 22.4 %all-reduce.6.cloned.1.call-done = (f32[8,16,128]{2,1,0:T(8,128)}, f32[32,16,128]{2,0,1:T(8,128)}) async-done(((f32[8,16,128]{2,1,0:T(8,128)}, f32[32,16,128]{2,0,1:T(8,128)}), (f32[8,16,128]{2,1,0:T(8,128)}, f32[32,16,128]{2,0,1:T(8,128)})) %all-reduce.6.cloned.1.call-update) | async-done | bytes 327696 | tf_op jit(solution)/shard_map/psum | solution.py:82
  249.5 4.2 %broadcast_multiply_fusion = f32[8,128,16,128]{3,2,0,1:T(8,128)S(1)} fusion(f32[8,128,16,128]{3,2,0,1:T(8,128)} %get-tuple-element.21, f32[8,16,128]{2,1,0:T(8,128)S(1)} %maximum_divide_fusion), kind=kLoop, calls=%fused_computation.8 | loop fusion | flops 2097152 | bytes 16842752 | tf_op jit(solution)/shard_map/mul | solution.py:85
  253.8 4.1 %copy.42 = f32[8,128,16,128]{3,2,1,0:T(8,128)} copy(f32[8,128,16,128]{3,2,0,1:T(8,128)S(1)} %broadcast_multiply_fusion) | data formatting | bytes 16777216
  257.9 1.9 convolution_bitcast_fusion
  (51 shorter events, 19.6 us)
Async XLA Ops:
  7.2 7.9 %copy-start = (f32[1,128,32]{1,2,0:T(8,128)S(1)}, f32[1,128,32]{1,2,0:T(8,128)}, u32[]{:S(2)}) copy-start(f32[1,128,32]{1,2,0:T(8,128)} %param.11) | copy-start | bytes 49156
  7.2 6.4 %copy-start.11 = (s32[16]{0:T(128)S(1)}, s32[16]{0:T(128)}, u32[]{:S(2)}) copy-start(s32[16]{0:T(128)} %param.13) | copy-start | bytes 196
  7.2 7.7 %copy-start.5 = (f32[8,16]{1,0:T(8,128)S(1)}, f32[8,16]{1,0:T(8,128)}, u32[]{:S(2)}) copy-start(f32[8,16]{1,0:T(8,128)} %param.10) | copy-start | bytes 1540
  7.2 62.9 %all-reduce.8.cloned.1.call-start = ((), (), s32[]{:S(2)}) async-start(), calls=%async_computation.1 | async-start | bytes 655360 | tf_op jit(solution)/shard_map/psum | solution.py:82
  11.7 16.6 %collective-permute-start = (f32[128,15,128]{0,2,1:T(8,128)}, f32[128,15,128]{0,2,1:T(8,128)}, u32[]{:S(2)}, u32[]{:S(2)}) collective-permute-start(f32[128,15,128]{0,2,1:T(8,128)} %slice.20), channel_id=1, source_target_pairs={{0,2},{2,4},{4,6},{6,8},{8,10},{10,12},{12,14},{14,16},{16,18},{18... | collective-permute-start | bytes 2949128 | tf_op jit(solution)/shard_map/ppermute | solution.py:16
  14.8 13.4 %copy-start.8 = (f32[15]{0:T(128)}, f32[15]{0:T(128)S(1)}, u32[]{:S(2)}) copy-start(f32[15]{0:T(128)S(1)} %compare_convert_fusion.1) | copy-start | bytes 184
  31.0 39.1 %copy-start.3 = (f32[8,16,128]{2,1,0:T(8,128)S(1)}, f32[8,16,128]{2,1,0:T(8,128)}, u32[]{:S(2)}) copy-start(f32[8,16,128]{2,1,0:T(8,128)} %param.9) | copy-start | bytes 196612
  45.3 203.3 %all-reduce.6.cloned.1.call-start = ((), (), s32[]{:S(2)}) async-start(), calls=%async_computation | async-start | bytes 655360 | tf_op jit(solution)/shard_map/psum | solution.py:82
  75.3 3.4 %copy-start.1 = (f32[8,128,16,128]{3,2,0,1:T(8,128)}, f32[8,128,16,128]{3,2,0,1:T(8,128)S(1)}, u32[]{:S(2)}) copy-start(f32[8,128,16,128]{3,2,0,1:T(8,128)S(1)} %bitcast_multiply_fusion) | copy-start | bytes 25165828
  75.3 14.2 %copy-start.6 = (f32[32]{0:T(128)S(1)}, f32[32]{0:T(128)}, u32[]{:S(2)}) copy-start(f32[32]{0:T(128)} %param.12) | copy-start | bytes 388
  86.3 88.5 %collective-permute-start.1 = (f32[8,128,15,128]{3,1,2,0:T(8,128)}, f32[8,128,15,128]{3,1,2,0:T(8,128)}, u32[]{:S(2)}, u32[]{:S(2)}) collective-permute-start(f32[8,128,15,128]{3,1,2,0:T(8,128)} %copy.35), channel_id=1, source_target_pairs={{2,0},{4,2},{6,4},{8,6},{10,8},{12,10},{14,12},{16,14},{18,16},{20... | collective-permute-start | bytes 23592968 | tf_op jit(solution)/shard_map/ppermute | solution.py:16
  98.0 91.0 %copy-start.2 = (f32[32,16,128]{2,0,1:T(8,128)S(1)}, f32[32,16,128]{2,0,1:T(8,128)}, u32[]{:S(2)}) copy-start(f32[32,16,128]{2,0,1:T(8,128)} %get-tuple-element.12) | copy-start | bytes 786436
  187.7 21.3 %copy-start.9 = (f32[15]{0:T(128)S(1)}, f32[15]{0:T(128)}, u32[]{:S(2)}) copy-start(f32[15]{0:T(128)} %copy-done.8) | copy-start | bytes 184
  192.5 16.5 %collective-permute-start.2 = (f32[128,15,128]{0,2,1:T(8,128)S(1)}, f32[128,15,128]{0,2,1:T(8,128)S(1)}, u32[]{:S(2)}, u32[]{:S(2)}) collective-permute-start(f32[128,15,128]{0,2,1:T(8,128)S(1)} %slice.24), channel_id=1, source_target_pairs={{0,2},{2,4},{4,6},{6,8},{8,10},{10,12},{12,14},{14,16},{16,18},{18... | collective-permute-start | bytes 2949128 | tf_op jit(solution)/shard_map/ppermute | solution.py:16
  253.7 4.1 %copy-start.4 = (f32[32,16,128]{2,0,1:T(8,128)S(1)}, f32[32,16,128]{2,0,1:T(8,128)}, u32[]{:S(2)}) copy-start(f32[32,16,128]{2,0,1:T(8,128)} %get-tuple-element.10) | copy-start | bytes 786436
  253.8 4.1 %copy-start.7 = (f32[32]{0:T(128)S(1)}, f32[32]{0:T(128)}, u32[]{:S(2)}) copy-start(f32[32]{0:T(128)} %param.12) | copy-start | bytes 388
  253.8 4.1 %copy-start.10 = (f32[32]{0:T(128)S(1)}, f32[32]{0:T(128)}, u32[]{:S(2)}) copy-start(f32[32]{0:T(128)} %neg.5) | copy-start | bytes 388
Sparse Core Ops, SparseCore 0:
  45.4 24.6 all-reduce.7
  225.0 23.5 all-reduce.5
where the time goes:
time: 270 us; the launch traced here: 268 us
  waiting for transfers between devices  145 us (54%)
  matrix products  50.5 us (19%)
  local copies, waits for them, and re-layouts  31.2 us (12%)
  other arithmetic  18.6 us (7%)
  between operations  14.3 us (5%)
  starting transfers between devices  8.24 us (3%)
    ppermute x3, waiting for transfers between devices, from_behind(): lax.ppermute(value, axis, [(source, source + steps) for source in range(i...  98.2 us
    psum x2, waiting for transfers between devices, body(): coeff_total, square_total = lax.psum((coeff_part, squares), 'chan')  46.9 us
    dot_general x2, matrix products, body(): jnp.einsum('brs,csn->bcrn', toeplitz, extended, precision=lax.Precision.H...  23 us
    unnamed x29, local copies, waits for them, and re-layouts  13.5 us
    dot_general x1, matrix products, body(): jnp.einsum('brs,bcrn->csn', toeplitz[:, :reach_rows, :reach_rows], states...  11.6 us
    mul x3, other arithmetic, body(): wavelet = lifted * (weights / jnp.maximum(magnitudes, weights))[:, None]  9.37 us
    ppermute x3, starting transfers between devices, from_behind(): lax.ppermute(value, axis, [(source, source + steps) for source in range(i...  7.98 us
    slice x1, local copies, waits for them, and re-layouts, body(): states = from_behind(wavelet[:, :, :reach_rows, :], 'facet', -1)  7.6 us
  transfers between devices with their start and end apart: 5, of which 5 were waited for; matrix products, arithmetic and copies ran while one was open for 6% of the time, Pallas kernels for 0%

commit v1 on v0

v1 whole, which is shorter than its diff:
```python
import functools

import jax
import jax.numpy as jnp
from jax import lax
from jax.experimental import pallas as pl
from jax.experimental.pallas import tpu as pltpu
from jax.sharding import PartitionSpec as P

PRIMAL = 0.5
DUAL = 0.5
F32 = jnp.float32
BF16 = jnp.bfloat16
CHUNKS = 2
GROUP = 4
VMEM_LIMIT = 24 << 20


def shift(value, axis, steps):
    count = lax.axis_size(axis)
    initial, last = (max(0, -steps), min(count, count - steps))
    return lax.ppermute(value, axis, [(source, source + steps) for source in range(initial, last)])


def chan_pairs(value, stride):
    count = lax.axis_size("chan")
    return lax.ppermute(value, "chan", [(source, source ^ stride) for source in range(count)])


def chan_terms(value):
    count = lax.axis_size("chan")
    if count & (count - 1):
        return lax.psum(value, "chan"), jnp.zeros_like(value)
    stride = 1
    other = jnp.zeros_like(value)
    while stride < count:
        if stride > 1:
            value = value + other
        other = chan_pairs(value, stride)
        stride *= 2
    return value, other


def high_low(value):
    high = lax.reduce_precision(value, 8, 7)
    low = value - high
    return high.astype(BF16), low.astype(BF16)


def split(value):
    high = value.astype(BF16)
    low = (value - high.astype(F32)).astype(BF16)
    return high, low


def three_lhs(matrix):
    high, low = high_low(matrix)
    return jnp.concatenate([high, high, low], axis=1)


def three_rhs(value):
    high, low = split(value)
    return jnp.concatenate([high, low, high], axis=0)


def two_lhs(matrix):
    high, low = high_low(matrix)
    top = jnp.concatenate([high, high], axis=1)
    bottom = jnp.concatenate([low, jnp.zeros_like(low)], axis=1)
    return jnp.concatenate([top, bottom], axis=0)


def two_rhs(value):
    high, low = split(value)
    return jnp.concatenate([high, low], axis=0)


def dot(lhs, rhs):
    return jnp.dot(lhs, rhs, preferred_element_type=F32)


def edge_toeplitz(filters, height, margin):
    bases, taps = filters.shape
    tap_mask = jnp.arange(taps)[None, :] < 2 * (jnp.arange(bases)[:, None] + 1)
    taps_of = jnp.where(tap_mask, filters, jnp.zeros_like(filters))
    rows = jnp.arange(height)[:, None]
    columns = jnp.arange(2 * height)[None, :]
    index = rows - columns + height
    allowed = (columns >= height) | (height - columns <= margin)
    result = jnp.zeros((bases, height, 2 * height), F32)
    for tap in range(taps):
        hit = (index == tap) & allowed
        result = jnp.where(hit[None], taps_of[:, tap][:, None, None], result)
    return result.reshape(bases * height, 2 * height)


def reflect_kernel(x_ref, d_ref, *r_refs):
    block = r_refs[0].shape[0]
    for index, r_ref in enumerate(r_refs):
        rows = pl.ds(index * block, block)
        x = x_ref[rows, :]
        updated = jnp.maximum(x - PRIMAL * (x - d_ref[rows, :]), 0.0)
        r_ref[...] = 2.0 * updated - x


def coef_kernel(height, spectral, lhs_ref, *refs):
    out_ref = refs[-1]
    s_ref = refs[0] if spectral else None
    r_refs = refs[1 if spectral else 0 : -1]
    rank = out_ref.shape[0]

    def pixels(row):
        parts = [r[pl.ds(row, r.shape[0] // height, stride=height), :] for r in r_refs]
        value = DUAL * jnp.concatenate(parts, axis=0)
        if spectral:
            value = value + s_ref[pl.ds(row, s_ref.shape[0] // height, stride=height), :]
        return value

    lhs = lhs_ref[...]
    lanes = out_ref.shape[1] // height
    for row in range(0, height, 2):
        value = jnp.concatenate([pixels(row), pixels(row + 1)], axis=1)
        both = dot(lhs, two_rhs(value))
        out_ref[:, row * lanes : (row + 2) * lanes] = both[:rank] + both[rank:]


def spectral_kernel(height, lhs_ref, own_ref, other_ref, bounds_ref, out_ref):
    lanes = out_ref.shape[1]
    channels = out_ref.shape[0] // height
    limit = bounds_ref[...]
    lhs = lhs_ref[...]
    for row in range(0, height, 2):
        span = slice(row * lanes, (row + 2) * lanes)
        total = own_ref[:, span] + other_ref[:, span]
        clipped = jnp.minimum(jnp.maximum(total, -limit), limit)
        both = dot(lhs, three_rhs(clipped))
        out_ref[pl.ds(row, channels, stride=height), :] = both[:, :lanes]
        out_ref[pl.ds(row + 1, channels, stride=height), :] = both[:, lanes:]


def scale_of(weights_ref, own_ref, other_ref):
    weights = weights_ref[...]
    return weights / jnp.maximum(jnp.sqrt(own_ref[...] + other_ref[...]), weights)


def extended(halo_ref, own_ref, height, channel):
    rows = pl.ds(pl.multiple_of(channel * height, height), height)
    return jnp.concatenate([halo_ref[rows, :], own_ref[rows, :]], axis=0)


def lift_kernel(height, first, *refs):
    if first:
        halo_ref, own_ref, lhs_ref, before_ref, out_ref, squares_ref = refs
    else:
        (halo_ref, own_ref, lhs_ref, before_ref, dual_ref, weights_ref, mine_ref, other_ref, out_ref, squares_ref) = refs
        scale = scale_of(weights_ref, mine_ref, other_ref)
    size = squares_ref.shape[0]
    lanes = own_ref.shape[1]
    channels = own_ref.shape[0] // height
    lhs = lhs_ref[...]

    def step(group, total):
        for pair in range(0, GROUP, 2):
            channel = group * GROUP + pair
            value = jnp.concatenate(
                [extended(halo_ref, own_ref, height, channel), extended(halo_ref, own_ref, height, channel + 1)], axis=1
            )
            both = dot(lhs, three_rhs(value))
            for half in range(2):
                rows = pl.ds(pl.multiple_of((channel + half) * size, size), size)
                lifted = both[:, half * lanes : (half + 1) * lanes]
                if not first:
                    lifted = lifted + dual_ref[rows, :] * scale
                out_ref[rows, :] = lifted
                total = total + lifted * lifted
        return total

    squares_ref[...] = lax.fori_loop(0, channels // GROUP, step, before_ref[...])


def adjoint_kernel(height, start, dual_ref, lhs_ref, weights_ref, mine_ref, other_ref, x_ref, d_ref, s_ref, border_ref, partial_ref):
    size, lanes = weights_ref.shape
    channels = border_ref.shape[0] // height
    scale = scale_of(weights_ref, mine_ref, other_ref)
    lhs = lhs_ref[...]

    def step(group, carry):
        for pair in range(0, GROUP, 2):
            channel = group * GROUP + pair
            duals = [
                dual_ref[pl.ds(pl.multiple_of((channel + half) * size, size), size), :] * scale for half in range(2)
            ]
            both = dot(lhs, two_rhs(jnp.concatenate(duals, axis=1)))
            spread = both[: 2 * height] + both[2 * height :]
            for half in range(2):
                rows = pl.ds(pl.multiple_of((channel + half) * height, height), height)
                mine = spread[:, half * lanes : (half + 1) * lanes]
                border_ref[rows, :] = mine[:height]
                cube = pl.ds(pl.multiple_of(start + (channel + half) * height, height), height)
                x, d = x_ref[cube, :], d_ref[cube, :]
                updated = jnp.maximum(x - PRIMAL * (x - d), 0.0)
                gradient = (updated - d) + s_ref[cube, :] + mine[height:]
                partial_ref[rows, :] = updated - PRIMAL * gradient
        return carry

    lax.fori_loop(0, channels // GROUP, step, 0)


def update_kernel(start, partial_ref, border_ref, x_ref, d_ref, u_ref, r_ref):
    cube = pl.ds(start, u_ref.shape[0])
    x = x_ref[cube, :]
    before = jnp.maximum(x - PRIMAL * (x - d_ref[cube, :]), 0.0)
    updated = jnp.maximum(partial_ref[...] - PRIMAL * border_ref[...], 0.0)
    u_ref[...] = updated
    r_ref[...] = 2.0 * updated - before


def wavelet_kernel(chunks, height, *refs):
    dual_refs = refs[:chunks]
    weights_ref, mine_ref, other_ref, out_ref, buffer, sems = refs[chunks:]
    size = weights_ref.shape[0]
    bases = size // height
    scale = scale_of(weights_ref, mine_ref, other_ref)
    block = buffer.shape[2]
    slots = buffer.shape[0]
    pending = [None] * slots
    turn = 0
    for index, dual_ref in enumerate(dual_refs):
        channels = dual_ref.shape[0] // size
        for start in range(0, channels, block):
            slot = turn % slots
            if pending[slot] is not None:
                pending[slot].wait()

            def step(channel, carry):
                rows = pl.ds(pl.multiple_of((start + channel) * size, size), size)
                value = dual_ref[rows, :] * scale
                for basis in range(bases):
                    buffer[slot, basis, channel] = value[basis * height : (basis + 1) * height]
                return carry

            lax.fori_loop(0, block, step, 0, unroll=2)
            copy = pltpu.make_async_copy(
                buffer.at[slot], out_ref.at[:, pl.ds(index * channels + start, block)], sems.at[slot]
            )
            copy.start()
            pending[slot] = copy
            turn += 1
    for copy in pending:
        if copy is not None:
            copy.wait()


def whole():
    return pl.BlockSpec(memory_space=pltpu.VMEM)


def call(kernel, outs, ins, operands, flops, nbytes, scratch=(), out_specs=None):
    return pl.pallas_call(
        kernel,
        out_shape=outs,
        in_specs=ins,
        out_specs=out_specs if out_specs is not None else jax.tree.map(lambda _: whole(), outs),
        scratch_shapes=scratch,
        compiler_params=pltpu.CompilerParams(vmem_limit_bytes=VMEM_LIMIT),
        cost_estimate=pl.CostEstimate(flops=flops, bytes_accessed=nbytes, transcendentals=0),
    )(*operands)


def body(x_start, dirty, weights, filters, basis, bounds, margin_rows):
    channels, height, lanes = x_start.shape
    bases, taps = filters.shape
    rank = bounds.shape[0]
    assert taps == height
    size = bases * height
    chunks = CHUNKS if channels >= 8 * CHUNKS else 1
    per = channels // chunks
    block = per * height
    rows = channels * height

    def flat(extent):
        return jax.ShapeDtypeStruct((extent, lanes), F32)

    x = x_start.reshape(rows, lanes)
    d = dirty.reshape(rows, lanes)
    w = weights.reshape(size, lanes)
    margin = lax.dynamic_index_in_dim(margin_rows, lax.axis_index("facet"), 0, keepdims=False)
    matrix = edge_toeplitz(filters, height, margin)
    lift_lhs = three_lhs(DUAL * matrix)
    adjoint_lhs = two_lhs(matrix.T)
    loading = basis[0]
    coef_lhs = two_lhs(loading.T)
    spectral_lhs = three_lhs(loading)
    limits = bounds[:, None]
    cubes = rows * lanes * 4
    duals = per * size * lanes * 4

    reflected = call(
        reflect_kernel, [flat(block)] * chunks, [whole()] * 2, (x, d), 4 * rows * lanes, 3 * cubes
    )
    halos = [shift(r, "facet", 1) for r in reflected]

    def coefficients(parts, spectral):
        operands = (coef_lhs,) + ((spectral,) if spectral is not None else ()) + tuple(parts)
        return call(
            functools.partial(coef_kernel, height, spectral is not None),
            jax.ShapeDtypeStruct((rank, height * lanes), F32),
            [whole()] * len(operands), operands, 6 * rank * rows * lanes, 2 * cubes,
        )

    def synthesis(own, other):
        return call(
            functools.partial(spectral_kernel, height), flat(rows), [whole()] * 4,
            (spectral_lhs, own, other, limits), 6 * rank * rows * lanes, 2 * cubes,
        )

    spectral = synthesis(*chan_terms(coefficients(reflected, None)))

    squares = jnp.zeros((size, lanes), F32)
    lifted = []
    for index in range(chunks):
        out, squares = call(
            functools.partial(lift_kernel, height, True), [flat(per * size), flat(size)], [whole()] * 4,
            (halos[index], reflected[index], lift_lhs, squares), 6 * 32 * per * size * lanes, duals,
        )
        lifted.append(out)
    own, other = chan_terms(squares)

    image, reflected, halos = [], [], []
    for index in range(chunks):
        borders, partial = call(
            functools.partial(adjoint_kernel, height, index * block), [flat(block)] * 2,
            [whole()] * 8,
            (lifted[index], adjoint_lhs, w, own, other, x, d, spectral), 6 * 32 * per * size * lanes, duals,
        )
        received = shift(borders, "facet", -1)
        updated, r = call(
            functools.partial(update_kernel, index * block), [flat(block)] * 2, [whole()] * 4,
            (partial, received, x, d), 5 * block * lanes, 6 * block * lanes * 4,
        )
        image.append(updated)
        reflected.append(r)
        halos.append(shift(r, "facet", 1))

    terms = chan_terms(coefficients(reflected, spectral))

    squares = jnp.zeros((size, lanes), F32)
    final = []
    for index in range(chunks):
        out, squares = call(
            functools.partial(lift_kernel, height, False), [flat(per * size), flat(size)], [whole()] * 8,
            (halos[index], reflected[index], lift_lhs, squares, lifted[index], w, own, other),
            6 * 32 * per * size * lanes, 2 * duals,
        )
        final.append(out)
    own, other = chan_terms(squares)
    spectral = synthesis(*terms)

    slab = min(per, 16)
    wavelet = call(
        functools.partial(wavelet_kernel, chunks, height),
        jax.ShapeDtypeStruct((bases, channels, height, lanes), F32),
        [whole()] * (chunks + 3), (*final, w, own, other), rows * lanes * bases, 2 * cubes * bases,
        scratch=[pltpu.VMEM((3, bases, slab, height, lanes), F32), pltpu.SemaphoreType.DMA((3,))],
        out_specs=pl.BlockSpec(memory_space=pl.ANY),
    )
    return (
        jnp.concatenate(image, axis=0).reshape(channels, height, lanes),
        wavelet,
        spectral.reshape(channels, height, lanes),
    )


def solution(mesh):
    in_specs = (
        P("chan", "facet", None),
        P("chan", "facet", None),
        P(None, "facet", None),
        P(),
        P("facet", "chan", None),
        P(),
        P(),
    )
    out_specs = (P("chan", "facet", None), P(None, "chan", "facet", None), P("chan", "facet", None))
    return jax.shard_map(body, mesh=mesh, in_specs=in_specs, out_specs=out_specs, check_vma=False)
```

time: 270 us -> 96.2 us (0.36)
  the two profiles are of different devices: /device:TPU:16 before, /device:TPU:10 now
where the time goes in v1:
time: 96.2 us; the launch traced here: 95.4 us
  Pallas kernels  28.1 us (29%)
  waiting for transfers between devices  21.9 us (23%)
  starting transfers between devices  18.9 us (20%)
  local copies, waits for them, and re-layouts  18.2 us (19%)
  other arithmetic  7.48 us (8%)
    pallas_call x14, Pallas kernels, call(): pl.pallas_call(kernel, out_shape=outs, in_specs=ins, out_specs=out_specs...  28.1 us
    ppermute x6, waiting for transfers between devices, shift(): lax.ppermute(value, axis, [(source, source + steps) for source in range(i...  18.6 us
    ppermute x6, starting transfers between devices, shift(): lax.ppermute(value, axis, [(source, source + steps) for source in range(i...  15.6 us
    broadcast_in_dim x32, local copies, waits for them, and re-layouts, edge_toeplitz(): result = jnp.where(hit[None], taps_of[:, tap][:, None, None], result)  9.86 us
    unnamed x15, local copies, waits for them, and re-layouts  4.39 us
    ppermute x4, waiting for transfers between devices, chan_pairs(): lax.ppermute(value, 'chan', [(source, source ^ stride) for source in rang...  3.37 us
    ppermute x4, starting transfers between devices, chan_pairs(): lax.ppermute(value, 'chan', [(source, source ^ stride) for source in rang...  3.26 us
    convert_element_type x5, other arithmetic, high_low(): return (high.astype(BF16), low.astype(BF16))  2.84 us
  transfers between devices with their start and end apart: 10, of which 5 were waited for; matrix products, arithmetic and copies ran while one was open for 23% of the time, Pallas kernels for 22%

profile of v1, /device:TPU:10, one launch (start us, length us, event | category | flops | bytes accessed | tf_op | source)
XLA Modules:
  0.0 95.4 jit_solution(10526875458413749053)
XLA Ops:
  0.6 1.2 %copy-done = f32[128,16,128]{2,1,0:T(8,128)S(1)} copy-done((f32[128,16,128]{2,1,0:T(8,128)S(1)}, f32[128,16,128]{2,1,0:T(8,128)}, u32[]{:S(2)}) %copy-start) | copy-done | bytes 1048600
  1.9 1.2 %copy-done.2 = f32[128,16,128]{2,1,0:T(8,128)S(1)} copy-done((f32[128,16,128]{2,1,0:T(8,128)S(1)}, f32[128,16,128]{2,1,0:T(8,128)}, u32[]{:S(2)}) %copy-start.2) | copy-done | bytes 1048600
  3.3 2.1 %collective-permute-start = (f32[1024,128]{1,0:T(8,128)S(1)}, f32[1024,128]{1,0:T(8,128)}, u32[]{:S(2)}, u32[]{:S(2)}) collective-permute-start(f32[1024,128]{1,0:T(8,128)S(1)} %get-tuple-element.21.refs_1_.refs_0_), channel_id=1, source_target_pairs={{0,2},{2,4},{4,6},{6,8},{8,10},{10,12},{12,14},{14,16},{16,18},{18... | collective-permute-start | bytes 1572872 | tf_op jit(solution)/shard_map/ppermute | solution.py:22
  5.4 3.6 %collective-permute-start.1 = (f32[1024,128]{1,0:T(8,128)S(1)}, f32[1024,128]{1,0:T(8,128)}, u32[]{:S(2)}, u32[]{:S(2)}) collective-permute-start(f32[1024,128]{1,0:T(8,128)S(1)} %get-tuple-element.23.refs_1_), channel_id=1, source_target_pairs={{0,2},{2,4},{4,6},{6,8},{8,10},{10,12},{12,14},{14,16},{16,18},{18... | collective-permute-start | bytes 1572872 | tf_op jit(solution)/shard_map/ppermute | solution.py:22
  11.0 1.6 %collective-permute-start.3 = (f32[32,2048]{1,0:T(8,128)S(1)}, f32[32,2048]{1,0:T(8,128)}, u32[]{:S(2)}, u32[]{:S(2)}) collective-permute-start(f32[32,2048]{1,0:T(8,128)S(1)} %shard_map.97.own_ref), channel_id=1, source_target_pairs={{0,1},{1,0},{2,3},{3,2},{4,5},{5,4},{6,7},{7,6},{8,9},{9,8},{10,11... | collective-permute-start | bytes 786440 | tf_op jit(solution)/shard_map/ppermute | solution.py:27
  12.6 1.2 %dynamic_slice.4 = s32[1]{0:T(128)} dynamic-slice(s32[16]{0:T(128)} %param.13, s32[]{:T(128)S(6)} %select_n.73), dynamic_slice_sizes={1} | dynamic-slice | bytes 12 | tf_op jit(solution)/shard_map/jit(dynamic_index_in_dim)/dynamic_slice | solution.py:287
  13.8 1.2 %compare_or_fusion = pred[32]{0:T(512)(128)(4,1)} fusion(s32[]{:T(128)} %bitcast.2), kind=kLoop, calls=%fused_computation.72 | loop fusion | flops 128 | bytes 36 | tf_op jit(solution)/shard_map/or | solution.py:89
  33.2 3.9 %shard_map.95 = (f32[8192,128]{1,0:T(8,128)S(1)}, f32[128,128]{1,0:T(8,128)S(1)}) custom-call(f32[1024,128]{1,0:T(8,128)} %collective-permute-done.refs_0_, f32[1024,128]{1,0:T(8,128)S(1)} %get-tuple-element.21.refs_1_.refs_0_, bf16[128,96]{1,0:T(8,128)(2,1)S(1)} %pad_maximum_fusion.1.refs_2_, f32[128,128]{1,0:T(8,128)S(1)} %broadcast_5_refs_3_.2.refs_3_), custom_call_target="tpu_custom_call" | custom-call | flops 201326592 | bytes 4194304 | tf_op jit(solution)/shard_map/pallas_call | solution.py:259
  37.1 3.9 %shard_map.96 = (f32[8192,128]{1,0:T(8,128)S(1)}, f32[128,128]{1,0:T(8,128)S(1)}) custom-call(f32[1024,128]{1,0:T(8,128)} %collective-permute-done.1.refs_0_, f32[1024,128]{1,0:T(8,128)S(1)} %get-tuple-element.23.refs_1_, bf16[128,96]{1,0:T(8,128)(2,1)S(1)} %pad_maximum_fusion.1.refs_2_, f32[128,128]{1,0:T(8,128)S(1)} %get-tuple-element.24.refs_3_), custom_call_target="tpu_custom_call" | custom-call | flops 201326592 | bytes 4194304 | tf_op jit(solution)/shard_map/pallas_call | solution.py:259
  41.6 1.5 %shard_map.98.s_ref.refs_0_ = f32[2048,128]{1,0:T(8,128)S(1)} custom-call(bf16[128,96]{1,0:T(8,128)(2,1)S(1)} %pad_maximum_fusion.2.lhs_ref, f32[32,2048]{1,0:T(8,128)S(1)} %shard_map.97.own_ref, f32[32,2048]{1,0:T(8,128)} %collective-permute-done.3.other_ref, f32[32,1]{1,0:T(8,128)S(1)} %copy.40.bounds_ref), custom_call_target="tpu_custom_call" | custom-call | flops 50331648 | bytes 2097152 | tf_op jit(solution)/shard_map/pallas_call | solution.py:259
  43.1 2.2 %collective-permute-done.2.other_ref.refs_7_ = f32[128,128]{1,0:T(8,128)S(1)} collective-permute-done((f32[128,128]{1,0:T(8,128)S(1)}, f32[128,128]{1,0:T(8,128)S(1)}, u32[]{:S(2)}, u32[]{:S(2)}) %collective-permute-start.2) | collective-permute-done | bytes 65568 | tf_op jit(solution)/shard_map/ppermute | solution.py:27
  45.3 3.0 %shard_map.99 = (f32[1024,128]{1,0:T(8,128)S(1)}, f32[1024,128]{1,0:T(8,128)S(1)}) custom-call(f32[8192,128]{1,0:T(8,128)S(1)} %get-tuple-element.22.dual_ref.refs_4_, bf16[64,256]{1,0:T(8,128)(2,1)S(1)} %copy.41.lhs_ref, f32[128,128]{1,0:T(8,128)S(1)} %bitcast.75, f32[128,128]{1,0:T(8,128)S(1)} %get-tuple-element.25.mine_ref.refs_6_, ...), custom_call_target="tpu_custom_call" | custom-call | flops 201326592 | bytes 4194304 | tf_op jit(solution)/shard_map/pallas_call | solution.py:259
  48.3 1.9 %collective-permute-start.4 = (f32[1024,128]{1,0:T(8,128)S(1)}, f32[1024,128]{1,0:T(8,128)S(1)}, u32[]{:S(2)}, u32[]{:S(2)}) collective-permute-start(f32[1024,128]{1,0:T(8,128)S(1)} %get-tuple-element.27), channel_id=1, source_target_pairs={{2,0},{4,2},{6,4},{8,6},{10,8},{12,10},{14,12},{16,14},{18,16},{20... | collective-permute-start | bytes 1572872 | tf_op jit(solution)/shard_map/ppermute | solution.py:22
  50.3 3.0 %shard_map.101 = (f32[1024,128]{1,0:T(8,128)S(1)}, f32[1024,128]{1,0:T(8,128)S(1)}) custom-call(f32[8192,128]{1,0:T(8,128)S(1)} %get-tuple-element.29.dual_ref.refs_4_, bf16[64,256]{1,0:T(8,128)(2,1)S(1)} %copy.41.lhs_ref, f32[128,128]{1,0:T(8,128)S(1)} %bitcast.76, f32[128,128]{1,0:T(8,128)S(1)} %get-tuple-element.25.mine_ref.refs_6_, ...), custom_call_target="tpu_custom_call" | custom-call | flops 201326592 | bytes 4194304 | tf_op jit(solution)/shard_map/pallas_call | solution.py:259
  53.3 2.5 %collective-permute-start.5 = (f32[1024,128]{1,0:T(8,128)S(1)}, f32[1024,128]{1,0:T(8,128)S(1)}, u32[]{:S(2)}, u32[]{:S(2)}) collective-permute-start(f32[1024,128]{1,0:T(8,128)S(1)} %get-tuple-element.31), channel_id=1, source_target_pairs={{2,0},{4,2},{6,4},{8,6},{10,8},{12,10},{14,12},{16,14},{18,16},{20... | collective-permute-start | bytes 1572872 | tf_op jit(solution)/shard_map/ppermute | solution.py:22
  57.1 3.7 %collective-permute-start.6 = (f32[1024,128]{1,0:T(8,128)S(1)}, f32[1024,128]{1,0:T(8,128)S(1)}, u32[]{:S(2)}, u32[]{:S(2)}) collective-permute-start(f32[1024,128]{1,0:T(8,128)S(1)} %get-tuple-element.33.refs_1_), channel_id=1, source_target_pairs={{0,2},{2,4},{4,6},{6,8},{8,10},{10,12},{12,14},{14,16},{16,18},{18... | collective-permute-start | bytes 1572872 | tf_op jit(solution)/shard_map/ppermute | solution.py:22
  60.8 13.0 %collective-permute-done.5.border_ref = f32[1024,128]{1,0:T(8,128)S(1)} collective-permute-done((f32[1024,128]{1,0:T(8,128)S(1)}, f32[1024,128]{1,0:T(8,128)S(1)}, u32[]{:S(2)}, u32[]{:S(2)}) %collective-permute-start.5) | collective-permute-done | bytes 524320 | tf_op jit(solution)/shard_map/ppermute | solution.py:22
  74.0 1.9 %collective-permute-start.7 = (f32[1024,128]{1,0:T(8,128)S(1)}, f32[1024,128]{1,0:T(8,128)S(1)}, u32[]{:S(2)}, u32[]{:S(2)}) collective-permute-start(f32[1024,128]{1,0:T(8,128)S(1)} %get-tuple-element.35.refs_1_.refs_2_), channel_id=1, source_target_pairs={{0,2},{2,4},{4,6},{6,8},{8,10},{10,12},{12,14},{14,16},{16,18},{18... | collective-permute-start | bytes 1572872 | tf_op jit(solution)/shard_map/ppermute | solution.py:22
  77.4 2.9 %shard_map.103 = (f32[8192,128]{1,0:T(8,128)S(1)}, f32[128,128]{1,0:T(8,128)S(1)}) custom-call(f32[1024,128]{1,0:T(8,128)S(1)} %collective-permute-done.6.refs_0_, f32[1024,128]{1,0:T(8,128)S(1)} %get-tuple-element.33.refs_1_, bf16[128,96]{1,0:T(8,128)(2,1)S(1)} %pad_maximum_fusion.1.refs_2_, f32[128,128]{1,0:T(8,128)S(1)} %broadcast_5_refs_3_.2.refs_3_, ...), custom_call_target="tpu_custom_call" | custom-call | flops 201326592 | bytes 8388608 | tf_op jit(solution)/shard_map/pallas_call | solution.py:259
  80.3 4.4 %collective-permute-done.7.refs_0_ = f32[1024,128]{1,0:T(8,128)S(1)} collective-permute-done((f32[1024,128]{1,0:T(8,128)S(1)}, f32[1024,128]{1,0:T(8,128)S(1)}, u32[]{:S(2)}, u32[]{:S(2)}) %collective-permute-start.7) | collective-permute-done | bytes 524320 | tf_op jit(solution)/shard_map/ppermute | solution.py:22
  84.6 2.9 %shard_map.104 = (f32[8192,128]{1,0:T(8,128)S(1)}, f32[128,128]{1,0:T(8,128)S(1)}) custom-call(f32[1024,128]{1,0:T(8,128)S(1)} %collective-permute-done.7.refs_0_, f32[1024,128]{1,0:T(8,128)S(1)} %get-tuple-element.35.refs_1_.refs_2_, bf16[128,96]{1,0:T(8,128)(2,1)S(1)} %pad_maximum_fusion.1.refs_2_, f32[128,128]{1,0:T(8,128)S(1)} %get-tuple-element.36.refs_3_, ...), custom_call_target="tpu_custom_call" | custom-call | flops 201326592 | bytes 8388608 | tf_op jit(solution)/shard_map/pallas_call | solution.py:259
  89.1 1.5 %shard_map.107 = f32[2048,128]{1,0:T(8,128)} custom-call(bf16[128,96]{1,0:T(8,128)(2,1)S(1)} %pad_maximum_fusion.2.lhs_ref, f32[32,2048]{1,0:T(8,128)S(1)} %shard_map.106.own_ref, f32[32,2048]{1,0:T(8,128)S(1)} %collective-permute-done.9.other_ref, f32[32,1]{1,0:T(8,128)S(1)} %copy.40.bounds_ref), custom_call_target="tpu_custom_call" | custom-call | flops 50331648 | bytes 2097152 | tf_op jit(solution)/shard_map/pallas_call | solution.py:259
  90.7 1.2 %collective-permute-done.8.refs_4_ = f32[128,128]{1,0:T(8,128)S(1)} collective-permute-done((f32[128,128]{1,0:T(8,128)S(1)}, f32[128,128]{1,0:T(8,128)S(1)}, u32[]{:S(2)}, u32[]{:S(2)}) %collective-permute-start.8) | collective-permute-done | bytes 65568 | tf_op jit(solution)/shard_map/ppermute | solution.py:27
  91.9 3.6 %shard_map.105 = f32[8,128,16,128]{3,2,1,0:T(8,128)} custom-call(f32[8192,128]{1,0:T(8,128)S(1)} %get-tuple-element.34.refs_0_, f32[8192,128]{1,0:T(8,128)S(1)} %get-tuple-element.37.refs_1_, f32[128,128]{1,0:T(8,128)S(1)} %bitcast.79, f32[128,128]{1,0:T(8,128)S(1)} %get-tuple-element.38.refs_3_, f32[128,128]{1,0:T(8,128)S(1)} %collective-permute-done.8.refs_4_), custom_call_target="tpu_custom_call" | custom-call | flops 2097152 | bytes 16777216 | tf_op jit(solution)/shard_map/pallas_call | solution.py:259
  (77 shorter events, 25.6 us)
Async XLA Ops:
  0.6 1.2 %copy-start = (f32[128,16,128]{2,1,0:T(8,128)S(1)}, f32[128,16,128]{2,1,0:T(8,128)}, u32[]{:S(2)}) copy-start(f32[128,16,128]{2,1,0:T(8,128)} %param.7) | copy-start | bytes 3145732
  1.9 1.2 %copy-start.2 = (f32[128,16,128]{2,1,0:T(8,128)S(1)}, f32[128,16,128]{2,1,0:T(8,128)}, u32[]{:S(2)}) copy-start(f32[128,16,128]{2,1,0:T(8,128)} %param.8) | copy-start | bytes 3145732
  3.1 42.2 %copy-start.1 = (f32[128,16,128]{2,1,0:T(8,128)S(1)}, f32[128,16,128]{2,1,0:T(8,128)}, u32[]{:S(2)}) copy-start(f32[128,16,128]{2,1,0:T(8,128)} %param.7) | copy-start | bytes 3145732
  3.1 42.2 %copy-start.3 = (f32[128,16,128]{2,1,0:T(8,128)S(1)}, f32[128,16,128]{2,1,0:T(8,128)}, u32[]{:S(2)}) copy-start(f32[128,16,128]{2,1,0:T(8,128)} %param.8) | copy-start | bytes 3145732
  3.1 42.2 %copy-start.4 = (f32[8,16,128]{2,1,0:T(8,128)S(1)}, f32[8,16,128]{2,1,0:T(8,128)}, u32[]{:S(2)}) copy-start(f32[8,16,128]{2,1,0:T(8,128)} %param.9) | copy-start | bytes 196612
  3.3 29.9 %collective-permute-start = (f32[1024,128]{1,0:T(8,128)S(1)}, f32[1024,128]{1,0:T(8,128)}, u32[]{:S(2)}, u32[]{:S(2)}) collective-permute-start(f32[1024,128]{1,0:T(8,128)S(1)} %get-tuple-element.21.refs_1_.refs_0_), channel_id=1, source_target_pairs={{0,2},{2,4},{4,6},{6,8},{8,10},{10,12},{12,14},{14,16},{16,18},{18... | collective-permute-start | bytes 1572872 | tf_op jit(solution)/shard_map/ppermute | solution.py:22
  5.4 31.7 %collective-permute-start.1 = (f32[1024,128]{1,0:T(8,128)S(1)}, f32[1024,128]{1,0:T(8,128)}, u32[]{:S(2)}, u32[]{:S(2)}) collective-permute-start(f32[1024,128]{1,0:T(8,128)S(1)} %get-tuple-element.23.refs_1_), channel_id=1, source_target_pairs={{0,2},{2,4},{4,6},{6,8},{8,10},{10,12},{12,14},{14,16},{16,18},{18... | collective-permute-start | bytes 1572872 | tf_op jit(solution)/shard_map/ppermute | solution.py:22
  9.7 0.6 copy-start.5
  11.0 30.6 %collective-permute-start.3 = (f32[32,2048]{1,0:T(8,128)S(1)}, f32[32,2048]{1,0:T(8,128)}, u32[]{:S(2)}, u32[]{:S(2)}) collective-permute-start(f32[32,2048]{1,0:T(8,128)S(1)} %shard_map.97.own_ref), channel_id=1, source_target_pairs={{0,1},{1,0},{2,3},{3,2},{4,5},{5,4},{6,7},{7,6},{8,9},{9,8},{10,11... | collective-permute-start | bytes 786440 | tf_op jit(solution)/shard_map/ppermute | solution.py:27
  29.1 0.6 copy-start.6
  41.0 4.3 %collective-permute-start.2 = (f32[128,128]{1,0:T(8,128)S(1)}, f32[128,128]{1,0:T(8,128)S(1)}, u32[]{:S(2)}, u32[]{:S(2)}) collective-permute-start(f32[128,128]{1,0:T(8,128)S(1)} %get-tuple-element.25.mine_ref.refs_6_), channel_id=1, source_target_pairs={{0,1},{1,0},{2,3},{3,2},{4,5},{5,4},{6,7},{7,6},{8,9},{9,8},{10,11... | collective-permute-start | bytes 196616 | tf_op jit(solution)/shard_map/ppermute | solution.py:27
  48.3 8.6 %collective-permute-start.4 = (f32[1024,128]{1,0:T(8,128)S(1)}, f32[1024,128]{1,0:T(8,128)S(1)}, u32[]{:S(2)}, u32[]{:S(2)}) collective-permute-start(f32[1024,128]{1,0:T(8,128)S(1)} %get-tuple-element.27), channel_id=1, source_target_pairs={{2,0},{4,2},{6,4},{8,6},{10,8},{12,10},{14,12},{16,14},{18,16},{20... | collective-permute-start | bytes 1572872 | tf_op jit(solution)/shard_map/ppermute | solution.py:22
  53.3 20.5 %collective-permute-start.5 = (f32[1024,128]{1,0:T(8,128)S(1)}, f32[1024,128]{1,0:T(8,128)S(1)}, u32[]{:S(2)}, u32[]{:S(2)}) collective-permute-start(f32[1024,128]{1,0:T(8,128)S(1)} %get-tuple-element.31), channel_id=1, source_target_pairs={{2,0},{4,2},{6,4},{8,6},{10,8},{12,10},{14,12},{16,14},{18,16},{20... | collective-permute-start | bytes 1572872 | tf_op jit(solution)/shard_map/ppermute | solution.py:22
  57.1 20.3 %collective-permute-start.6 = (f32[1024,128]{1,0:T(8,128)S(1)}, f32[1024,128]{1,0:T(8,128)S(1)}, u32[]{:S(2)}, u32[]{:S(2)}) collective-permute-start(f32[1024,128]{1,0:T(8,128)S(1)} %get-tuple-element.33.refs_1_), channel_id=1, source_target_pairs={{0,2},{2,4},{4,6},{6,8},{8,10},{10,12},{12,14},{14,16},{16,18},{18... | collective-permute-start | bytes 1572872 | tf_op jit(solution)/shard_map/ppermute | solution.py:22
  74.0 10.6 %collective-permute-start.7 = (f32[1024,128]{1,0:T(8,128)S(1)}, f32[1024,128]{1,0:T(8,128)S(1)}, u32[]{:S(2)}, u32[]{:S(2)}) collective-permute-start(f32[1024,128]{1,0:T(8,128)S(1)} %get-tuple-element.35.refs_1_.refs_2_), channel_id=1, source_target_pairs={{0,2},{2,4},{4,6},{6,8},{8,10},{10,12},{12,14},{14,16},{16,18},{18... | collective-permute-start | bytes 1572872 | tf_op jit(solution)/shard_map/ppermute | solution.py:22
  76.8 12.3 %collective-permute-start.9 = (f32[32,2048]{1,0:T(8,128)S(1)}, f32[32,2048]{1,0:T(8,128)S(1)}, u32[]{:S(2)}, u32[]{:S(2)}) collective-permute-start(f32[32,2048]{1,0:T(8,128)S(1)} %shard_map.106.own_ref), channel_id=1, source_target_pairs={{0,1},{1,0},{2,3},{3,2},{4,5},{5,4},{6,7},{7,6},{8,9},{9,8},{10,11... | collective-permute-start | bytes 786440 | tf_op jit(solution)/shard_map/ppermute | solution.py:27
  87.5 4.3 %collective-permute-start.8 = (f32[128,128]{1,0:T(8,128)S(1)}, f32[128,128]{1,0:T(8,128)S(1)}, u32[]{:S(2)}, u32[]{:S(2)}) collective-permute-start(f32[128,128]{1,0:T(8,128)S(1)} %get-tuple-element.38.refs_3_), channel_id=1, source_target_pairs={{0,1},{1,0},{2,3},{3,2},{4,5},{5,4},{6,7},{7,6},{8,9},{9,8},{10,11... | collective-permute-start | bytes 196616 | tf_op jit(solution)/shard_map/ppermute | solution.py:27

commit v2 on v1

--- a/solution.py
+++ b/solution.py
@@ -12,7 +12,7 @@
 F32 = jnp.float32
 BF16 = jnp.bfloat16
 CHUNKS = 2
-GROUP = 4
+GROUP = 32
 VMEM_LIMIT = 24 << 20
 
 
@@ -41,12 +41,6 @@
     return value, other
 
 
-def high_low(value):
-    high = lax.reduce_precision(value, 8, 7)
-    low = value - high
-    return high.astype(BF16), low.astype(BF16)
-
-
 def split(value):
     high = value.astype(BF16)
     low = (value - high.astype(F32)).astype(BF16)
@@ -54,7 +48,7 @@
 
 
 def three_lhs(matrix):
-    high, low = high_low(matrix)
+    high, low = split(matrix)
     return jnp.concatenate([high, high, low], axis=1)
 
 
@@ -64,7 +58,7 @@
 
 
 def two_lhs(matrix):
-    high, low = high_low(matrix)
+    high, low = split(matrix)
     top = jnp.concatenate([high, high], axis=1)
     bottom = jnp.concatenate([low, jnp.zeros_like(low)], axis=1)
     return jnp.concatenate([top, bottom], axis=0)
@@ -79,27 +73,53 @@
     return jnp.dot(lhs, rhs, preferred_element_type=F32)
 
 
-def edge_toeplitz(filters, height, margin):
-    bases, taps = filters.shape
-    tap_mask = jnp.arange(taps)[None, :] < 2 * (jnp.arange(bases)[:, None] + 1)
-    taps_of = jnp.where(tap_mask, filters, jnp.zeros_like(filters))
-    rows = jnp.arange(height)[:, None]
-    columns = jnp.arange(2 * height)[None, :]
-    index = rows - columns + height
-    allowed = (columns >= height) | (height - columns <= margin)
-    result = jnp.zeros((bases, height, 2 * height), F32)
+def setup_kernel(
+    filters_ref, bounds_ref, margin_ref, loading_ref, lift_ref, adjoint_ref, coef_ref, spectral_ref, limits_ref
+):
+    bases, taps = filters_ref.shape
+    height = taps
+    size = bases * height
+    margin = margin_ref[lax.axis_index("facet")]
+    source = lax.broadcasted_iota(jnp.int32, (2 * height, size), 0)
+    target = lax.broadcasted_iota(jnp.int32, (2 * height, size), 1)
+    tap_of = lax.rem(target, height) - source + height
+    tap_of = jnp.where((source >= height) | (height - source <= margin), tap_of, -1)
+    basis_of = lax.div(target, height)
+    matrix = jnp.zeros((2 * height, size), F32)
     for tap in range(taps):
-        hit = (index == tap) & allowed
-        result = jnp.where(hit[None], taps_of[:, tap][:, None, None], result)
-    return result.reshape(bases * height, 2 * height)
-
-
-def reflect_kernel(x_ref, d_ref, *r_refs):
+        values = jnp.zeros((2 * height, size), F32)
+        for basis in range(bases):
+            if tap < 2 * (basis + 1):
+                values = jnp.where(basis_of == basis, filters_ref[basis, tap], values)
+        matrix = jnp.where(tap_of == tap, values, matrix)
+    adjoint_ref[...] = two_lhs(matrix)
+    lift_ref[...] = three_lhs(DUAL * matrix.T)
+    loading = loading_ref[...]
+    coef_ref[...] = two_lhs(loading)
+    spectral_ref[...] = three_lhs(loading.T)
+    row = lax.broadcasted_iota(jnp.int32, limits_ref.shape, 0)
+    limits = jnp.zeros(limits_ref.shape, F32)
+    for index in range(bounds_ref.shape[0]):
+        limits = jnp.where(row == index, bounds_ref[index], limits)
+    limits_ref[...] = limits
+
+
+def reflect_kernel(x_ref, d_ref, *refs):
+    r_refs, (x_buffer, d_buffer, sems) = refs[:-3], refs[-3:]
     block = r_refs[0].shape[0]
+    copies = []
+    for index in range(len(r_refs)):
+        rows = pl.ds(index * block, block)
+        for turn, (source, target) in enumerate(((x_ref, x_buffer), (d_ref, d_buffer))):
+            copy = pltpu.make_async_copy(source.at[rows], target.at[rows], sems.at[2 * index + turn])
+            copy.start()
+            copies.append(copy)
     for index, r_ref in enumerate(r_refs):
+        copies[2 * index].wait()
+        copies[2 * index + 1].wait()
         rows = pl.ds(index * block, block)
-        x = x_ref[rows, :]
-        updated = jnp.maximum(x - PRIMAL * (x - d_ref[rows, :]), 0.0)
+        x = x_buffer[rows, :]
+        updated = jnp.maximum(x - PRIMAL * (x - d_buffer[rows, :]), 0.0)
         r_ref[...] = 2.0 * updated - x
 
 
@@ -127,7 +147,7 @@
 def spectral_kernel(height, lhs_ref, own_ref, other_ref, bounds_ref, out_ref):
     lanes = out_ref.shape[1]
     channels = out_ref.shape[0] // height
-    limit = bounds_ref[...]
+    limit = jnp.concatenate([bounds_ref[...]] * 2, axis=1)
     lhs = lhs_ref[...]
     for row in range(0, height, 2):
         span = slice(row * lanes, (row + 2) * lanes)
@@ -158,10 +178,11 @@
     lanes = own_ref.shape[1]
     channels = own_ref.shape[0] // height
     lhs = lhs_ref[...]
+    many = min(GROUP, channels)
 
     def step(group, total):
-        for pair in range(0, GROUP, 2):
-            channel = group * GROUP + pair
+        for pair in range(0, many, 2):
+            channel = group * many + pair
             value = jnp.concatenate(
                 [extended(halo_ref, own_ref, height, channel), extended(halo_ref, own_ref, height, channel + 1)], axis=1
             )
@@ -175,7 +196,7 @@
                 total = total + lifted * lifted
         return total
 
-    squares_ref[...] = lax.fori_loop(0, channels // GROUP, step, before_ref[...])
+    squares_ref[...] = lax.fori_loop(0, channels // many, step, before_ref[...])
 
 
 def adjoint_kernel(height, start, dual_ref, lhs_ref, weights_ref, mine_ref, other_ref, x_ref, d_ref, s_ref, border_ref, partial_ref):
@@ -183,10 +204,11 @@
     channels = border_ref.shape[0] // height
     scale = scale_of(weights_ref, mine_ref, other_ref)
     lhs = lhs_ref[...]
+    many = min(GROUP, channels)
 
     def step(group, carry):
-        for pair in range(0, GROUP, 2):
-            channel = group * GROUP + pair
+        for pair in range(0, many, 2):
+            channel = group * many + pair
             duals = [
                 dual_ref[pl.ds(pl.multiple_of((channel + half) * size, size), size), :] * scale for half in range(2)
             ]
@@ -203,16 +225,19 @@
                 partial_ref[rows, :] = updated - PRIMAL * gradient
         return carry
 
-    lax.fori_loop(0, channels // GROUP, step, 0)
-
-
-def update_kernel(start, partial_ref, border_ref, x_ref, d_ref, u_ref, r_ref):
-    cube = pl.ds(start, u_ref.shape[0])
-    x = x_ref[cube, :]
-    before = jnp.maximum(x - PRIMAL * (x - d_ref[cube, :]), 0.0)
-    updated = jnp.maximum(partial_ref[...] - PRIMAL * border_ref[...], 0.0)
-    u_ref[...] = updated
-    r_ref[...] = 2.0 * updated - before
+    lax.fori_loop(0, channels // many, step, 0)
+
+
+def update_kernel(chunks, *refs):
+    partial_refs, border_refs = refs[:chunks], refs[chunks : 2 * chunks]
+    x_ref, d_ref, u_ref = refs[2 * chunks : 2 * chunks + 3]
+    for index, r_ref in enumerate(refs[2 * chunks + 3 :]):
+        rows = pl.ds(index * r_ref.shape[0], r_ref.shape[0])
+        x = x_ref[rows, :]
+        before = jnp.maximum(x - PRIMAL * (x - d_ref[rows, :]), 0.0)
+        updated = jnp.maximum(partial_refs[index][...] - PRIMAL * border_refs[index][...], 0.0)
+        u_ref[rows, :] = updated
+        r_ref[...] = 2.0 * updated - before
 
 
 def wavelet_kernel(chunks, height, *refs):
@@ -255,14 +280,14 @@
     return pl.BlockSpec(memory_space=pltpu.VMEM)
 
 
-def call(kernel, outs, ins, operands, flops, nbytes, scratch=(), out_specs=None):
+def call(kernel, outs, ins, operands, flops, nbytes, scratch=(), out_specs=None, limit=VMEM_LIMIT):
     return pl.pallas_call(
         kernel,
         out_shape=outs,
         in_specs=ins,
         out_specs=out_specs if out_specs is not None else jax.tree.map(lambda _: whole(), outs),
         scratch_shapes=scratch,
-        compiler_params=pltpu.CompilerParams(vmem_limit_bytes=VMEM_LIMIT),
+        compiler_params=pltpu.CompilerParams(vmem_limit_bytes=limit),
         cost_estimate=pl.CostEstimate(flops=flops, bytes_accessed=nbytes, transcendentals=0),
     )(*operands)
 
@@ -284,21 +309,29 @@
     x = x_start.reshape(rows, lanes)
     d = dirty.reshape(rows, lanes)
     w = weights.reshape(size, lanes)
-    margin = lax.dynamic_index_in_dim(margin_rows, lax.axis_index("facet"), 0, keepdims=False)
-    matrix = edge_toeplitz(filters, height, margin)
-    lift_lhs = three_lhs(DUAL * matrix)
-    adjoint_lhs = two_lhs(matrix.T)
-    loading = basis[0]
-    coef_lhs = two_lhs(loading.T)
-    spectral_lhs = three_lhs(loading)
-    limits = bounds[:, None]
+    loading = basis[0].T
     cubes = rows * lanes * 4
     duals = per * size * lanes * 4
 
+    distant = pl.BlockSpec(memory_space=pltpu.HBM)
     reflected = call(
-        reflect_kernel, [flat(block)] * chunks, [whole()] * 2, (x, d), 4 * rows * lanes, 3 * cubes
+        reflect_kernel, [flat(block)] * chunks, [distant] * 2, (x, d), 4 * rows * lanes, 3 * cubes,
+        scratch=[pltpu.VMEM((rows, lanes), F32)] * 2 + [pltpu.SemaphoreType.DMA((2 * chunks,))], limit=None,
     )
     halos = [shift(r, "facet", 1) for r in reflected]
+
+    scalars = pl.BlockSpec(memory_space=pltpu.SMEM)
+    lift_lhs, adjoint_lhs, coef_lhs, spectral_lhs, limits = call(
+        setup_kernel,
+        [
+            jax.ShapeDtypeStruct((size, 6 * height), BF16),
+            jax.ShapeDtypeStruct((4 * height, 2 * size), BF16),
+            jax.ShapeDtypeStruct((2 * rank, 2 * channels), BF16),
+            jax.ShapeDtypeStruct((channels, 3 * rank), BF16),
+            flat(rank),
+        ],
+        [scalars] * 3 + [whole()], (filters, bounds, margin_rows, loading), 100000, 100000,
+    )
 
     def coefficients(parts, spectral):
         operands = (coef_lhs,) + ((spectral,) if spectral is not None else ()) + tuple(parts)
@@ -326,21 +359,20 @@
         lifted.append(out)
     own, other = chan_terms(squares)
 
-    image, reflected, halos = [], [], []
+    borders, partials = [], []
     for index in range(chunks):
-        borders, partial = call(
-            functools.partial(adjoint_kernel, height, index * block), [flat(block)] * 2,
-            [whole()] * 8,
+        border, partial = call(
+            functools.partial(adjoint_kernel, height, index * block), [flat(block)] * 2, [whole()] * 8,
             (lifted[index], adjoint_lhs, w, own, other, x, d, spectral), 6 * 32 * per * size * lanes, duals,
         )
-        received = shift(borders, "facet", -1)
-        updated, r = call(
-            functools.partial(update_kernel, index * block), [flat(block)] * 2, [whole()] * 4,
-            (partial, received, x, d), 5 * block * lanes, 6 * block * lanes * 4,
-        )
-        image.append(updated)
-        reflected.append(r)
-        halos.append(shift(r, "facet", 1))
+        borders.append(shift(border, "facet", -1))
+        partials.append(partial)
+    updates = call(
+        functools.partial(update_kernel, chunks), [flat(rows)] + [flat(block)] * chunks, [whole()] * (2 * chunks + 2),
+        (*partials, *borders, x, d), 5 * rows * lanes, 6 * cubes,
+    )
+    image, reflected = updates[0], updates[1:]
+    halos = [shift(r, "facet", 1) for r in reflected]
 
     terms = chan_terms(coefficients(reflected, spectral))
 
@@ -362,10 +394,10 @@
         jax.ShapeDtypeStruct((bases, channels, height, lanes), F32),
         [whole()] * (chunks + 3), (*final, w, own, other), rows * lanes * bases, 2 * cubes * bases,
         scratch=[pltpu.VMEM((3, bases, slab, height, lanes), F32), pltpu.SemaphoreType.DMA((3,))],
-        out_specs=pl.BlockSpec(memory_space=pl.ANY),
+        out_specs=distant,
     )
     return (
-        jnp.concatenate(image, axis=0).reshape(channels, height, lanes),
+        image.reshape(channels, height, lanes),
         wavelet,
         spectral.reshape(channels, height, lanes),
     )

time: 96.2 us -> 70 us (0.73)
  the two profiles are of different devices: /device:TPU:10 before, /device:TPU:16 now
where the time goes in v2:
time: 70 us; the launch traced here: 69.5 us
  waiting for transfers between devices  24.4 us (35%)
  starting transfers between devices  20.8 us (30%)
  Pallas kernels  17.6 us (25%)
  local copies, waits for them, and re-layouts  5.85 us (8%)
  between operations  0.8 us (1%)
    ppermute x6, waiting for transfers between devices, shift(): lax.ppermute(value, axis, [(source, source + steps) for source in range(i...  20.8 us
    pallas_call x14, Pallas kernels, call(): pl.pallas_call(kernel, out_shape=outs, in_specs=ins, out_specs=out_specs...  17.6 us
    ppermute x6, starting transfers between devices, shift(): lax.ppermute(value, axis, [(source, source + steps) for source in range(i...  14.5 us
    ppermute x4, starting transfers between devices, chan_pairs(): lax.ppermute(value, 'chan', [(source, source ^ stride) for source in rang...  6.31 us
    unnamed x20, local copies, waits for them, and re-layouts  5.84 us
    ppermute x4, waiting for transfers between devices, chan_pairs(): lax.ppermute(value, 'chan', [(source, source ^ stride) for source in rang...  3.58 us
  transfers between devices with their start and end apart: 10, of which 7 were waited for; matrix products, arithmetic and copies ran while one was open for 0% of the time, Pallas kernels for 13%

profile of v2, /device:TPU:16, one launch (start us, length us, event | category | flops | bytes accessed | tf_op | source)
XLA Modules:
  0.0 69.5 jit_solution(8415687718709001673)
XLA Ops:
  0.6 2.7 %shard_map.94 = (f32[1024,128]{1,0:T(8,128)}, f32[1024,128]{1,0:T(8,128)}) custom-call(f32[2048,128]{1,0:T(8,128)} %bitcast.8, f32[2048,128]{1,0:T(8,128)} %bitcast.12), custom_call_target="tpu_custom_call" | custom-call | flops 1048576 | bytes 3145728 | tf_op jit(solution)/shard_map/pallas_call | solution.py:284
  3.3 1.9 %collective-permute-start = (f32[1024,128]{1,0:T(8,128)}, f32[1024,128]{1,0:T(8,128)S(1)}, u32[]{:S(2)}, u32[]{:S(2)}) collective-permute-start(f32[1024,128]{1,0:T(8,128)} %get-tuple-element.25.refs_1_.refs_0_), channel_id=1, source_target_pairs={{0,2},{2,4},{4,6},{6,8},{8,10},{10,12},{12,14},{14,16},{16,18},{18... | collective-permute-start | bytes 1572872 | tf_op jit(solution)/shard_map/ppermute | solution.py:22
  5.2 3.5 %collective-permute-start.1 = (f32[1024,128]{1,0:T(8,128)}, f32[1024,128]{1,0:T(8,128)S(1)}, u32[]{:S(2)}, u32[]{:S(2)}) collective-permute-start(f32[1024,128]{1,0:T(8,128)} %get-tuple-element.29.refs_1_), channel_id=1, source_target_pairs={{0,2},{2,4},{4,6},{6,8},{8,10},{10,12},{12,14},{14,16},{16,18},{18... | collective-permute-start | bytes 1572872 | tf_op jit(solution)/shard_map/ppermute | solution.py:22
  14.9 1.6 %collective-permute-start.3 = (f32[32,2048]{1,0:T(8,128)S(1)}, f32[32,2048]{1,0:T(8,128)S(1)}, u32[]{:S(2)}, u32[]{:S(2)}) collective-permute-start(f32[32,2048]{1,0:T(8,128)S(1)} %shard_map.98.own_ref), channel_id=1, source_target_pairs={{0,1},{1,0},{2,3},{3,2},{4,5},{5,4},{6,7},{7,6},{8,9},{9,8},{10,11... | collective-permute-start | bytes 786440 | tf_op jit(solution)/shard_map/ppermute | solution.py:27
  17.4 3.2 %collective-permute-done.1.refs_0_ = f32[1024,128]{1,0:T(8,128)S(1)} collective-permute-done((f32[1024,128]{1,0:T(8,128)}, f32[1024,128]{1,0:T(8,128)S(1)}, u32[]{:S(2)}, u32[]{:S(2)}) %collective-permute-start.1) | collective-permute-done | bytes 524320 | tf_op jit(solution)/shard_map/ppermute | solution.py:22
  20.5 1.0 %copy-done.3 = f32[1024,128]{1,0:T(8,128)S(1)} copy-done((f32[1024,128]{1,0:T(8,128)S(1)}, f32[1024,128]{1,0:T(8,128)}, u32[]{:S(2)}) %copy-start.3) | copy-done | bytes 524312
  22.4 1.6 %collective-permute-start.2 = (f32[128,128]{1,0:T(8,128)S(1)}, f32[128,128]{1,0:T(8,128)S(1)}, u32[]{:S(2)}, u32[]{:S(2)}) collective-permute-start(f32[128,128]{1,0:T(8,128)S(1)} %get-tuple-element.31.mine_ref.refs_6_), channel_id=1, source_target_pairs={{0,1},{1,0},{2,3},{3,2},{4,5},{5,4},{6,7},{7,6},{8,9},{9,8},{10,11... | collective-permute-start | bytes 196616 | tf_op jit(solution)/shard_map/ppermute | solution.py:27
  24.5 2.3 %collective-permute-done.2.other_ref.refs_7_ = f32[128,128]{1,0:T(8,128)S(1)} collective-permute-done((f32[128,128]{1,0:T(8,128)S(1)}, f32[128,128]{1,0:T(8,128)S(1)}, u32[]{:S(2)}, u32[]{:S(2)}) %collective-permute-start.2) | collective-permute-done | bytes 65568 | tf_op jit(solution)/shard_map/ppermute | solution.py:27
  26.8 1.2 %shard_map.101 = (f32[1024,128]{1,0:T(8,128)S(1)}, f32[1024,128]{1,0:T(8,128)S(1)}) custom-call(f32[8192,128]{1,0:T(8,128)S(1)} %get-tuple-element.36.dual_ref.refs_4_, bf16[64,256]{1,0:T(8,128)(2,1)S(1)} %get-tuple-element.28.lhs_ref, f32[128,128]{1,0:T(8,128)S(1)} %bitcast.16, f32[128,128]{1,0:T(8,128)S(1)} %get-tuple-element.31.mine_ref.refs_6_, ...), custom_call_target="tpu_custom_call" | custom-call | flops 201326592 | bytes 4194304 | tf_op jit(solution)/shard_map/pallas_call | solution.py:284
  28.0 1.9 %collective-permute-start.5 = (f32[1024,128]{1,0:T(8,128)S(1)}, f32[1024,128]{1,0:T(8,128)S(1)}, u32[]{:S(2)}, u32[]{:S(2)}) collective-permute-start(f32[1024,128]{1,0:T(8,128)S(1)} %get-tuple-element.39), channel_id=1, source_target_pairs={{2,0},{4,2},{6,4},{8,6},{10,8},{12,10},{14,12},{16,14},{18,16},{20... | collective-permute-start | bytes 1572872 | tf_op jit(solution)/shard_map/ppermute | solution.py:22
  29.9 1.2 %shard_map.100 = (f32[1024,128]{1,0:T(8,128)S(1)}, f32[1024,128]{1,0:T(8,128)S(1)}) custom-call(f32[8192,128]{1,0:T(8,128)S(1)} %get-tuple-element.27.dual_ref.refs_4_, bf16[64,256]{1,0:T(8,128)(2,1)S(1)} %get-tuple-element.28.lhs_ref, f32[128,128]{1,0:T(8,128)S(1)} %bitcast.17, f32[128,128]{1,0:T(8,128)S(1)} %get-tuple-element.31.mine_ref.refs_6_, ...), custom_call_target="tpu_custom_call" | custom-call | flops 201326592 | bytes 4194304 | tf_op jit(solution)/shard_map/pallas_call | solution.py:284
  31.0 2.5 %collective-permute-start.4 = (f32[1024,128]{1,0:T(8,128)S(1)}, f32[1024,128]{1,0:T(8,128)S(1)}, u32[]{:S(2)}, u32[]{:S(2)}) collective-permute-start(f32[1024,128]{1,0:T(8,128)S(1)} %get-tuple-element.38), channel_id=1, source_target_pairs={{2,0},{4,2},{6,4},{8,6},{10,8},{12,10},{14,12},{16,14},{18,16},{20... | collective-permute-start | bytes 1572872 | tf_op jit(solution)/shard_map/ppermute | solution.py:22
  33.5 3.0 %collective-permute-done.5.refs_3_ = f32[1024,128]{1,0:T(8,128)S(1)} collective-permute-done((f32[1024,128]{1,0:T(8,128)S(1)}, f32[1024,128]{1,0:T(8,128)S(1)}, u32[]{:S(2)}, u32[]{:S(2)}) %collective-permute-start.5) | collective-permute-done | bytes 524320 | tf_op jit(solution)/shard_map/ppermute | solution.py:22
  36.6 5.6 %collective-permute-done.4.refs_2_ = f32[1024,128]{1,0:T(8,128)S(1)} collective-permute-done((f32[1024,128]{1,0:T(8,128)S(1)}, f32[1024,128]{1,0:T(8,128)S(1)}, u32[]{:S(2)}, u32[]{:S(2)}) %collective-permute-start.4) | collective-permute-done | bytes 524320 | tf_op jit(solution)/shard_map/ppermute | solution.py:22
  42.2 1.2 %shard_map.102 = (f32[2048,128]{1,0:T(8,128)}, f32[1024,128]{1,0:T(8,128)S(1)}, f32[1024,128]{1,0:T(8,128)S(1)}) custom-call(f32[1024,128]{1,0:T(8,128)S(1)} %get-tuple-element.35.refs_0_, f32[1024,128]{1,0:T(8,128)S(1)} %get-tuple-element.37.refs_1_, f32[1024,128]{1,0:T(8,128)S(1)} %collective-permute-done.4.refs_2_, ...), custom_call_target="tpu_custom_call" | custom-call | flops 1310720 | bytes 6291456 | tf_op jit(solution)/shard_map/pallas_call | solution.py:284
  43.4 2.8 %collective-permute-start.6 = (f32[1024,128]{1,0:T(8,128)S(1)}, f32[1024,128]{1,0:T(8,128)S(1)}, u32[]{:S(2)}, u32[]{:S(2)}) collective-permute-start(f32[1024,128]{1,0:T(8,128)S(1)} %get-tuple-element.41.refs_1_), channel_id=1, source_target_pairs={{0,2},{2,4},{4,6},{6,8},{8,10},{10,12},{12,14},{14,16},{16,18},{18... | collective-permute-start | bytes 1572872 | tf_op jit(solution)/shard_map/ppermute | solution.py:22
  46.2 1.9 %collective-permute-start.7 = (f32[1024,128]{1,0:T(8,128)S(1)}, f32[1024,128]{1,0:T(8,128)S(1)}, u32[]{:S(2)}, u32[]{:S(2)}) collective-permute-start(f32[1024,128]{1,0:T(8,128)S(1)} %get-tuple-element.43.refs_1_.refs_2_), channel_id=1, source_target_pairs={{0,2},{2,4},{4,6},{6,8},{8,10},{10,12},{12,14},{14,16},{16,18},{18... | collective-permute-start | bytes 1572872 | tf_op jit(solution)/shard_map/ppermute | solution.py:22
  49.0 1.6 %collective-permute-start.9 = (f32[32,2048]{1,0:T(8,128)S(1)}, f32[32,2048]{1,0:T(8,128)S(1)}, u32[]{:S(2)}, u32[]{:S(2)}) collective-permute-start(f32[32,2048]{1,0:T(8,128)S(1)} %shard_map.106.own_ref), channel_id=1, source_target_pairs={{0,1},{1,0},{2,3},{3,2},{4,5},{5,4},{6,7},{7,6},{8,9},{9,8},{10,11... | collective-permute-start | bytes 786440 | tf_op jit(solution)/shard_map/ppermute | solution.py:27
  50.6 4.4 %collective-permute-done.6.refs_0_ = f32[1024,128]{1,0:T(8,128)S(1)} collective-permute-done((f32[1024,128]{1,0:T(8,128)S(1)}, f32[1024,128]{1,0:T(8,128)S(1)}, u32[]{:S(2)}, u32[]{:S(2)}) %collective-permute-start.6) | collective-permute-done | bytes 524320 | tf_op jit(solution)/shard_map/ppermute | solution.py:22
  55.9 4.6 %collective-permute-done.7.refs_0_ = f32[1024,128]{1,0:T(8,128)S(1)} collective-permute-done((f32[1024,128]{1,0:T(8,128)S(1)}, f32[1024,128]{1,0:T(8,128)S(1)}, u32[]{:S(2)}, u32[]{:S(2)}) %collective-permute-start.7) | collective-permute-done | bytes 524320 | tf_op jit(solution)/shard_map/ppermute | solution.py:22
  61.6 1.6 %collective-permute-start.8 = (f32[128,128]{1,0:T(8,128)S(1)}, f32[128,128]{1,0:T(8,128)S(1)}, u32[]{:S(2)}, u32[]{:S(2)}) collective-permute-start(f32[128,128]{1,0:T(8,128)S(1)} %get-tuple-element.46.refs_3_), channel_id=1, source_target_pairs={{0,1},{1,0},{2,3},{3,2},{4,5},{5,4},{6,7},{7,6},{8,9},{9,8},{10,11... | collective-permute-start | bytes 196616 | tf_op jit(solution)/shard_map/ppermute | solution.py:27
  63.1 1.4 %shard_map.107 = f32[2048,128]{1,0:T(8,128)} custom-call(bf16[128,96]{1,0:T(8,128)(2,1)S(1)} %get-tuple-element.32.lhs_ref, f32[32,2048]{1,0:T(8,128)S(1)} %shard_map.106.own_ref, f32[32,2048]{1,0:T(8,128)S(1)} %collective-permute-done.9.other_ref, f32[32,128]{1,0:T(8,128)S(1)} %get-tuple-element.34.bounds_ref), custom_call_target="tpu_custom_call" | custom-call | flops 50331648 | bytes 2097152 | tf_op jit(solution)/shard_map/pallas_call | solution.py:284
  64.6 1.3 %collective-permute-done.8.refs_4_ = f32[128,128]{1,0:T(8,128)S(1)} collective-permute-done((f32[128,128]{1,0:T(8,128)S(1)}, f32[128,128]{1,0:T(8,128)S(1)}, u32[]{:S(2)}, u32[]{:S(2)}) %collective-permute-start.8) | collective-permute-done | bytes 65568 | tf_op jit(solution)/shard_map/ppermute | solution.py:27
  65.9 3.6 %shard_map.105 = f32[8,128,16,128]{3,2,1,0:T(8,128)} custom-call(f32[8192,128]{1,0:T(8,128)S(1)} %get-tuple-element.42.refs_0_, f32[8192,128]{1,0:T(8,128)S(1)} %get-tuple-element.45.refs_1_, f32[128,128]{1,0:T(8,128)S(1)} %bitcast.20, f32[128,128]{1,0:T(8,128)S(1)} %get-tuple-element.46.refs_3_, f32[128,128]{1,0:T(8,128)S(1)} %collective-permute-done.8.refs_4_), custom_call_target="tpu_custom_call" | custom-call | flops 2097152 | bytes 16777216 | tf_op jit(solution)/shard_map/pallas_call | solution.py:284
  (31 shorter events, 11.2 us)
Async XLA Ops:
  0.6 26.2 %copy-start.1 = (f32[128,16,128]{2,1,0:T(8,128)S(1)}, f32[128,16,128]{2,1,0:T(8,128)}, u32[]{:S(2)}) copy-start(f32[128,16,128]{2,1,0:T(8,128)} %param.8) | copy-start | bytes 3145732
  0.6 26.1 %copy-start = (f32[128,16,128]{2,1,0:T(8,128)S(1)}, f32[128,16,128]{2,1,0:T(8,128)}, u32[]{:S(2)}) copy-start(f32[128,16,128]{2,1,0:T(8,128)} %param.7) | copy-start | bytes 3145732
  3.3 13.2 %collective-permute-start = (f32[1024,128]{1,0:T(8,128)}, f32[1024,128]{1,0:T(8,128)S(1)}, u32[]{:S(2)}, u32[]{:S(2)}) collective-permute-start(f32[1024,128]{1,0:T(8,128)} %get-tuple-element.25.refs_1_.refs_0_), channel_id=1, source_target_pairs={{0,2},{2,4},{4,6},{6,8},{8,10},{10,12},{12,14},{14,16},{16,18},{18... | collective-permute-start | bytes 1572872 | tf_op jit(solution)/shard_map/ppermute | solution.py:22
  5.2 15.3 %collective-permute-start.1 = (f32[1024,128]{1,0:T(8,128)}, f32[1024,128]{1,0:T(8,128)S(1)}, u32[]{:S(2)}, u32[]{:S(2)}) collective-permute-start(f32[1024,128]{1,0:T(8,128)} %get-tuple-element.29.refs_1_), channel_id=1, source_target_pairs={{0,2},{2,4},{4,6},{6,8},{8,10},{10,12},{12,14},{14,16},{16,18},{18... | collective-permute-start | bytes 1572872 | tf_op jit(solution)/shard_map/ppermute | solution.py:22
  8.8 0.7 %copy-start.6 = (f32[1,128,32]{1,2,0:T(8,128)S(1)}, f32[1,128,32]{1,2,0:T(8,128)}, u32[]{:S(2)}) copy-start(f32[1,128,32]{1,2,0:T(8,128)} %param.11) | copy-start | bytes 49156
  9.5 0.7 copy-start.7
  10.2 0.7 copy-start.8
  10.8 0.7 copy-start.9
  12.3 1.0 %copy-start.2 = (f32[1024,128]{1,0:T(8,128)S(1)}, f32[1024,128]{1,0:T(8,128)}, u32[]{:S(2)}) copy-start(f32[1024,128]{1,0:T(8,128)} %get-tuple-element.29.refs_1_) | copy-start | bytes 1572868
  13.4 1.0 %copy-start.4 = (f32[1024,128]{1,0:T(8,128)S(1)}, f32[1024,128]{1,0:T(8,128)}, u32[]{:S(2)}) copy-start(f32[1024,128]{1,0:T(8,128)} %get-tuple-element.25.refs_1_.refs_0_) | copy-start | bytes 1572868
  14.4 12.4 %copy-start.5 = (f32[8,16,128]{2,1,0:T(8,128)S(1)}, f32[8,16,128]{2,1,0:T(8,128)}, u32[]{:S(2)}) copy-start(f32[8,16,128]{2,1,0:T(8,128)} %param.9) | copy-start | bytes 196612
  14.9 9.1 %collective-permute-start.3 = (f32[32,2048]{1,0:T(8,128)S(1)}, f32[32,2048]{1,0:T(8,128)S(1)}, u32[]{:S(2)}, u32[]{:S(2)}) collective-permute-start(f32[32,2048]{1,0:T(8,128)S(1)} %shard_map.98.own_ref), channel_id=1, source_target_pairs={{0,1},{1,0},{2,3},{3,2},{4,5},{5,4},{6,7},{7,6},{8,9},{9,8},{10,11... | collective-permute-start | bytes 786440 | tf_op jit(solution)/shard_map/ppermute | solution.py:27
  20.5 1.0 %copy-start.3 = (f32[1024,128]{1,0:T(8,128)S(1)}, f32[1024,128]{1,0:T(8,128)}, u32[]{:S(2)}) copy-start(f32[1024,128]{1,0:T(8,128)} %get-tuple-element.29.refs_1_) | copy-start | bytes 1572868
  22.4 4.3 %collective-permute-start.2 = (f32[128,128]{1,0:T(8,128)S(1)}, f32[128,128]{1,0:T(8,128)S(1)}, u32[]{:S(2)}, u32[]{:S(2)}) collective-permute-start(f32[128,128]{1,0:T(8,128)S(1)} %get-tuple-element.31.mine_ref.refs_6_), channel_id=1, source_target_pairs={{0,1},{1,0},{2,3},{3,2},{4,5},{5,4},{6,7},{7,6},{8,9},{9,8},{10,11... | collective-permute-start | bytes 196616 | tf_op jit(solution)/shard_map/ppermute | solution.py:27
  28.0 8.6 %collective-permute-start.5 = (f32[1024,128]{1,0:T(8,128)S(1)}, f32[1024,128]{1,0:T(8,128)S(1)}, u32[]{:S(2)}, u32[]{:S(2)}) collective-permute-start(f32[1024,128]{1,0:T(8,128)S(1)} %get-tuple-element.39), channel_id=1, source_target_pairs={{2,0},{4,2},{6,4},{8,6},{10,8},{12,10},{14,12},{16,14},{18,16},{20... | collective-permute-start | bytes 1572872 | tf_op jit(solution)/shard_map/ppermute | solution.py:22
  31.0 11.1 %collective-permute-start.4 = (f32[1024,128]{1,0:T(8,128)S(1)}, f32[1024,128]{1,0:T(8,128)S(1)}, u32[]{:S(2)}, u32[]{:S(2)}) collective-permute-start(f32[1024,128]{1,0:T(8,128)S(1)} %get-tuple-element.38), channel_id=1, source_target_pairs={{2,0},{4,2},{6,4},{8,6},{10,8},{12,10},{14,12},{16,14},{18,16},{20... | collective-permute-start | bytes 1572872 | tf_op jit(solution)/shard_map/ppermute | solution.py:22
  43.4 11.6 %collective-permute-start.6 = (f32[1024,128]{1,0:T(8,128)S(1)}, f32[1024,128]{1,0:T(8,128)S(1)}, u32[]{:S(2)}, u32[]{:S(2)}) collective-permute-start(f32[1024,128]{1,0:T(8,128)S(1)} %get-tuple-element.41.refs_1_), channel_id=1, source_target_pairs={{0,2},{2,4},{4,6},{6,8},{8,10},{10,12},{12,14},{14,16},{16,18},{18... | collective-permute-start | bytes 1572872 | tf_op jit(solution)/shard_map/ppermute | solution.py:22
  46.2 14.4 %collective-permute-start.7 = (f32[1024,128]{1,0:T(8,128)S(1)}, f32[1024,128]{1,0:T(8,128)S(1)}, u32[]{:S(2)}, u32[]{:S(2)}) collective-permute-start(f32[1024,128]{1,0:T(8,128)S(1)} %get-tuple-element.43.refs_1_.refs_2_), channel_id=1, source_target_pairs={{0,2},{2,4},{4,6},{6,8},{8,10},{10,12},{12,14},{14,16},{16,18},{18... | collective-permute-start | bytes 1572872 | tf_op jit(solution)/shard_map/ppermute | solution.py:22
  49.0 14.1 %collective-permute-start.9 = (f32[32,2048]{1,0:T(8,128)S(1)}, f32[32,2048]{1,0:T(8,128)S(1)}, u32[]{:S(2)}, u32[]{:S(2)}) collective-permute-start(f32[32,2048]{1,0:T(8,128)S(1)} %shard_map.106.own_ref), channel_id=1, source_target_pairs={{0,1},{1,0},{2,3},{3,2},{4,5},{5,4},{6,7},{7,6},{8,9},{9,8},{10,11... | collective-permute-start | bytes 786440 | tf_op jit(solution)/shard_map/ppermute | solution.py:27
  61.6 4.3 %collective-permute-start.8 = (f32[128,128]{1,0:T(8,128)S(1)}, f32[128,128]{1,0:T(8,128)S(1)}, u32[]{:S(2)}, u32[]{:S(2)}) collective-permute-start(f32[128,128]{1,0:T(8,128)S(1)} %get-tuple-element.46.refs_3_), channel_id=1, source_target_pairs={{0,1},{1,0},{2,3},{3,2},{4,5},{5,4},{6,7},{7,6},{8,9},{9,8},{10,11... | collective-permute-start | bytes 196616 | tf_op jit(solution)/shard_map/ppermute | solution.py:27

commit v3 on v2

--- a/solution.py
+++ b/solution.py
@@ -74,16 +74,19 @@
 
 
 def setup_kernel(
-    filters_ref, bounds_ref, margin_ref, loading_ref, lift_ref, adjoint_ref, coef_ref, spectral_ref, limits_ref
+    filters_ref, bounds_ref, margin_ref, loading_ref,
+    lift_ref, next_ref, interior_ref, border_ref, coef_ref, spectral_ref, limits_ref,
 ):
     bases, taps = filters_ref.shape
     height = taps
     size = bases * height
-    margin = margin_ref[lax.axis_index("facet")]
+    facet = lax.axis_index("facet")
+    last = margin_ref.shape[0] - 1
+    own_margin = margin_ref[facet]
+    next_margin = jnp.where(facet < last, margin_ref[jnp.minimum(facet + 1, last)], 0)
     source = lax.broadcasted_iota(jnp.int32, (2 * height, size), 0)
     target = lax.broadcasted_iota(jnp.int32, (2 * height, size), 1)
     tap_of = lax.rem(target, height) - source + height
-    tap_of = jnp.where((source >= height) | (height - source <= margin), tap_of, -1)
     basis_of = lax.div(target, height)
     matrix = jnp.zeros((2 * height, size), F32)
     for tap in range(taps):
@@ -92,8 +95,15 @@
             if tap < 2 * (basis + 1):
                 values = jnp.where(basis_of == basis, filters_ref[basis, tap], values)
         matrix = jnp.where(tap_of == tap, values, matrix)
-    adjoint_ref[...] = two_lhs(matrix)
-    lift_ref[...] = three_lhs(DUAL * matrix.T)
+
+    def masked(margin):
+        return jnp.where((source >= height) | (height - source <= margin), matrix, 0.0)
+
+    below = masked(next_margin)
+    lift_ref[...] = three_lhs(DUAL * masked(own_margin).T)
+    next_ref[...] = three_lhs(DUAL * below.T)
+    interior_ref[...] = two_lhs(matrix[height:])
+    border_ref[...] = two_lhs(below[:height])
     loading = loading_ref[...]
     coef_ref[...] = two_lhs(loading)
     spectral_ref[...] = three_lhs(loading.T)
@@ -104,25 +114,6 @@
     limits_ref[...] = limits
 
 
-def reflect_kernel(x_ref, d_ref, *refs):
-    r_refs, (x_buffer, d_buffer, sems) = refs[:-3], refs[-3:]
-    block = r_refs[0].shape[0]
-    copies = []
-    for index in range(len(r_refs)):
-        rows = pl.ds(index * block, block)
-        for turn, (source, target) in enumerate(((x_ref, x_buffer), (d_ref, d_buffer))):
-            copy = pltpu.make_async_copy(source.at[rows], target.at[rows], sems.at[2 * index + turn])
-            copy.start()
-            copies.append(copy)
-    for index, r_ref in enumerate(r_refs):
-        copies[2 * index].wait()
-        copies[2 * index + 1].wait()
-        rows = pl.ds(index * block, block)
-        x = x_buffer[rows, :]
-        updated = jnp.maximum(x - PRIMAL * (x - d_buffer[rows, :]), 0.0)
-        r_ref[...] = 2.0 * updated - x
-
-
 def coef_kernel(height, spectral, lhs_ref, *refs):
     out_ref = refs[-1]
     s_ref = refs[0] if spectral else None
@@ -144,7 +135,12 @@
         out_ref[:, row * lanes : (row + 2) * lanes] = both[:rank] + both[rank:]
 
 
-def spectral_kernel(height, lhs_ref, own_ref, other_ref, bounds_ref, out_ref):
+def spectral_kernel(height, lhs_ref, own_ref, other_ref, bounds_ref, *refs):
+    image_refs, out_ref = refs[:-1], refs[-1]
+    if image_refs:
+        image_ref, image_refs = refs[-2], refs[:-2]
+        for index, part_ref in enumerate(image_refs):
+            image_ref[pl.ds(index * part_ref.shape[0], part_ref.shape[0]), :] = part_ref[...]
     lanes = out_ref.shape[1]
     channels = out_ref.shape[0] // height
     limit = jnp.concatenate([bounds_ref[...]] * 2, axis=1)
@@ -158,9 +154,9 @@
         out_ref[pl.ds(row + 1, channels, stride=height), :] = both[:, lanes:]
 
 
-def scale_of(weights_ref, own_ref, other_ref):
+def scale_kernel(weights_ref, own_ref, other_ref, scale_ref):
     weights = weights_ref[...]
-    return weights / jnp.maximum(jnp.sqrt(own_ref[...] + other_ref[...]), weights)
+    scale_ref[...] = weights / jnp.maximum(jnp.sqrt(own_ref[...] + other_ref[...]), weights)
 
 
 def extended(halo_ref, own_ref, height, channel):
@@ -168,16 +164,18 @@
     return jnp.concatenate([halo_ref[rows, :], own_ref[rows, :]], axis=0)
 
 
-def lift_kernel(height, first, *refs):
-    if first:
+def lift_kernel(height, kind, *refs):
+    if kind == "next":
+        halo_ref, own_ref, lhs_ref, out_ref = refs
+    elif kind == "first":
         halo_ref, own_ref, lhs_ref, before_ref, out_ref, squares_ref = refs
     else:
-        (halo_ref, own_ref, lhs_ref, before_ref, dual_ref, weights_ref, mine_ref, other_ref, out_ref, squares_ref) = refs
-        scale = scale_of(weights_ref, mine_ref, other_ref)
-    size = squares_ref.shape[0]
+        halo_ref, own_ref, lhs_ref, before_ref, dual_ref, scale_ref, out_ref, squares_ref = refs
+        scale = scale_ref[...]
+    lhs = lhs_ref[...]
+    size = lhs.shape[0]
     lanes = own_ref.shape[1]
     channels = own_ref.shape[0] // height
-    lhs = lhs_ref[...]
     many = min(GROUP, channels)
 
     def step(group, total):
@@ -190,19 +188,27 @@
             for half in range(2):
                 rows = pl.ds(pl.multiple_of((channel + half) * size, size), size)
                 lifted = both[:, half * lanes : (half + 1) * lanes]
-                if not first:
+                if kind == "second":
                     lifted = lifted + dual_ref[rows, :] * scale
                 out_ref[rows, :] = lifted
-                total = total + lifted * lifted
+                if kind != "next":
+                    total = total + lifted * lifted
         return total
 
-    squares_ref[...] = lax.fori_loop(0, channels // many, step, before_ref[...])
-
-
-def adjoint_kernel(height, start, dual_ref, lhs_ref, weights_ref, mine_ref, other_ref, x_ref, d_ref, s_ref, border_ref, partial_ref):
-    size, lanes = weights_ref.shape
-    channels = border_ref.shape[0] // height
-    scale = scale_of(weights_ref, mine_ref, other_ref)
+    if kind == "next":
+        lax.fori_loop(0, channels // many, step, 0)
+    else:
+        squares_ref[...] = lax.fori_loop(0, channels // many, step, before_ref[...])
+
+
+def adjoint_kernel(height, start, border, dual_ref, lhs_ref, scale_ref, *refs):
+    if border:
+        partial_ref, x_ref, d_ref, updated_ref, reflected_ref = refs
+    else:
+        s_ref, x_ref, d_ref, partial_ref = refs
+    size, lanes = scale_ref.shape
+    channels = partial_ref.shape[0] // height
+    scale = scale_ref[...]
     lhs = lhs_ref[...]
     many = min(GROUP, channels)
 
@@ -213,31 +219,22 @@
                 dual_ref[pl.ds(pl.multiple_of((channel + half) * size, size), size), :] * scale for half in range(2)
             ]
             both = dot(lhs, two_rhs(jnp.concatenate(duals, axis=1)))
-            spread = both[: 2 * height] + both[2 * height :]
+            spread = both[:height] + both[height:]
             for half in range(2):
                 rows = pl.ds(pl.multiple_of((channel + half) * height, height), height)
+                cube = pl.ds(pl.multiple_of(start + (channel + half) * height, height), height)
                 mine = spread[:, half * lanes : (half + 1) * lanes]
-                border_ref[rows, :] = mine[:height]
-                cube = pl.ds(pl.multiple_of(start + (channel + half) * height, height), height)
                 x, d = x_ref[cube, :], d_ref[cube, :]
-                updated = jnp.maximum(x - PRIMAL * (x - d), 0.0)
-                gradient = (updated - d) + s_ref[cube, :] + mine[height:]
-                partial_ref[rows, :] = updated - PRIMAL * gradient
+                before = jnp.maximum(x - PRIMAL * (x - d), 0.0)
+                if border:
+                    updated = jnp.maximum(partial_ref[rows, :] - PRIMAL * mine, 0.0)
+                    updated_ref[rows, :] = updated
+                    reflected_ref[rows, :] = 2.0 * updated - before
+                else:
+                    partial_ref[rows, :] = before - PRIMAL * ((before - d) + s_ref[cube, :] + mine)
         return carry
 
     lax.fori_loop(0, channels // many, step, 0)
-
-
-def update_kernel(chunks, *refs):
-    partial_refs, border_refs = refs[:chunks], refs[chunks : 2 * chunks]
-    x_ref, d_ref, u_ref = refs[2 * chunks : 2 * chunks + 3]
-    for index, r_ref in enumerate(refs[2 * chunks + 3 :]):
-        rows = pl.ds(index * r_ref.shape[0], r_ref.shape[0])
-        x = x_ref[rows, :]
-        before = jnp.maximum(x - PRIMAL * (x - d_ref[rows, :]), 0.0)
-        updated = jnp.maximum(partial_refs[index][...] - PRIMAL * border_refs[index][...], 0.0)
-        u_ref[rows, :] = updated
-        r_ref[...] = 2.0 * updated - before
 
 
 def wavelet_kernel(chunks, height, *refs):
@@ -245,7 +242,8 @@
     weights_ref, mine_ref, other_ref, out_ref, buffer, sems = refs[chunks:]
     size = weights_ref.shape[0]
     bases = size // height
-    scale = scale_of(weights_ref, mine_ref, other_ref)
+    weights = weights_ref[...]
+    scale = weights / jnp.maximum(jnp.sqrt(mine_ref[...] + other_ref[...]), weights)
     block = buffer.shape[2]
     slots = buffer.shape[0]
     pending = [None] * slots
@@ -314,18 +312,23 @@
     duals = per * size * lanes * 4
 
     distant = pl.BlockSpec(memory_space=pltpu.HBM)
-    reflected = call(
-        reflect_kernel, [flat(block)] * chunks, [distant] * 2, (x, d), 4 * rows * lanes, 3 * cubes,
-        scratch=[pltpu.VMEM((rows, lanes), F32)] * 2 + [pltpu.SemaphoreType.DMA((2 * chunks,))], limit=None,
-    )
+    scalars = pl.BlockSpec(memory_space=pltpu.SMEM)
+    work = 6 * 2 * height * per * size * lanes
+
+    reflected = []
+    for index in range(chunks):
+        some = slice(index * block, (index + 1) * block)
+        updated = jnp.maximum(x[some] - PRIMAL * (x[some] - d[some]), 0.0)
+        reflected.append(2.0 * updated - x[some])
     halos = [shift(r, "facet", 1) for r in reflected]
 
-    scalars = pl.BlockSpec(memory_space=pltpu.SMEM)
-    lift_lhs, adjoint_lhs, coef_lhs, spectral_lhs, limits = call(
+    lift_lhs, next_lhs, interior_lhs, border_lhs, coef_lhs, spectral_lhs, limits = call(
         setup_kernel,
         [
             jax.ShapeDtypeStruct((size, 6 * height), BF16),
-            jax.ShapeDtypeStruct((4 * height, 2 * size), BF16),
+            jax.ShapeDtypeStruct((size, 6 * height), BF16),
+            jax.ShapeDtypeStruct((2 * height, 2 * size), BF16),
+            jax.ShapeDtypeStruct((2 * height, 2 * size), BF16),
             jax.ShapeDtypeStruct((2 * rank, 2 * channels), BF16),
             jax.ShapeDtypeStruct((channels, 3 * rank), BF16),
             flat(rank),
@@ -341,52 +344,59 @@
             [whole()] * len(operands), operands, 6 * rank * rows * lanes, 2 * cubes,
         )
 
-    def synthesis(own, other):
+    def synthesis(own, other, image=()):
+        outs = [flat(rows)] * (2 if image else 1)
         return call(
-            functools.partial(spectral_kernel, height), flat(rows), [whole()] * 4,
-            (spectral_lhs, own, other, limits), 6 * rank * rows * lanes, 2 * cubes,
-        )
-
-    spectral = synthesis(*chan_terms(coefficients(reflected, None)))
+            functools.partial(spectral_kernel, height), outs, [whole()] * (4 + len(image)),
+            (spectral_lhs, own, other, limits, *image), 6 * rank * rows * lanes, 2 * cubes,
+        )
+
+    coefs = coefficients(reflected, None)
+    tied = lax.optimization_barrier((coefs, *reflected))
+    terms = chan_terms(tied[0])
+    below = [shift(r, "facet", -1) for r in tied[1:]]
+    (spectral,) = synthesis(*terms)
 
     squares = jnp.zeros((size, lanes), F32)
     lifted = []
     for index in range(chunks):
         out, squares = call(
-            functools.partial(lift_kernel, height, True), [flat(per * size), flat(size)], [whole()] * 4,
-            (halos[index], reflected[index], lift_lhs, squares), 6 * 32 * per * size * lanes, duals,
+            functools.partial(lift_kernel, height, "first"), [flat(per * size), flat(size)], [whole()] * 4,
+            (halos[index], reflected[index], lift_lhs, squares), work, duals,
         )
         lifted.append(out)
-    own, other = chan_terms(squares)
-
-    borders, partials = [], []
+    scale = call(scale_kernel, flat(size), [whole()] * 3, (w, *chan_terms(squares)), 10 * size * lanes, 16 * size * lanes)
+    scale_below = shift(scale, "facet", -1)
+
+    image, halos, again = [], [], []
     for index in range(chunks):
-        border, partial = call(
-            functools.partial(adjoint_kernel, height, index * block), [flat(block)] * 2, [whole()] * 8,
-            (lifted[index], adjoint_lhs, w, own, other, x, d, spectral), 6 * 32 * per * size * lanes, duals,
-        )
-        borders.append(shift(border, "facet", -1))
-        partials.append(partial)
-    updates = call(
-        functools.partial(update_kernel, chunks), [flat(rows)] + [flat(block)] * chunks, [whole()] * (2 * chunks + 2),
-        (*partials, *borders, x, d), 5 * rows * lanes, 6 * cubes,
-    )
-    image, reflected = updates[0], updates[1:]
-    halos = [shift(r, "facet", 1) for r in reflected]
-
-    terms = chan_terms(coefficients(reflected, spectral))
+        dual_below = call(
+            functools.partial(lift_kernel, height, "next"), flat(per * size), [whole()] * 3,
+            (reflected[index], below[index], next_lhs), work, duals,
+        )
+        partial = call(
+            functools.partial(adjoint_kernel, height, index * block, False), flat(block), [whole()] * 6,
+            (lifted[index], interior_lhs, scale, spectral, x, d), work, duals,
+        )
+        updated, r = call(
+            functools.partial(adjoint_kernel, height, index * block, True), [flat(block)] * 2, [whole()] * 6,
+            (dual_below, border_lhs, scale_below, partial, x, d), work, duals,
+        )
+        image.append(updated)
+        again.append(r)
+        halos.append(shift(r, "facet", 1))
+    terms = chan_terms(coefficients(again, spectral))
 
     squares = jnp.zeros((size, lanes), F32)
     final = []
     for index in range(chunks):
         out, squares = call(
-            functools.partial(lift_kernel, height, False), [flat(per * size), flat(size)], [whole()] * 8,
-            (halos[index], reflected[index], lift_lhs, squares, lifted[index], w, own, other),
-            6 * 32 * per * size * lanes, 2 * duals,
+            functools.partial(lift_kernel, height, "second"), [flat(per * size), flat(size)], [whole()] * 6,
+            (halos[index], again[index], lift_lhs, squares, lifted[index], scale), work, 2 * duals,
         )
         final.append(out)
     own, other = chan_terms(squares)
-    spectral = synthesis(*terms)
+    image, spectral = synthesis(*terms, image)
 
     slab = min(per, 16)
     wavelet = call(

time: 70 us -> 67.3 us (0.961)
  starting transfers between devices: 20.8 us -> 29.7 us
  waiting for transfers between devices: 24.4 us -> 16.5 us
  local copies, waits for them, and re-layouts: 5.85 us -> 1.78 us
    ppermute x6 -> x7, starting transfers between devices: 14.5 us -> 23.3 us  [shift(): lax.ppermute(value, axis, [(source, source + steps) for source in range(i...]
    ppermute x6 -> x7, waiting for transfers between devices: 20.8 us -> 13.2 us  [shift(): lax.ppermute(value, axis, [(source, source + steps) for source in range(i...]
    unnamed x20 -> x14, local copies, waits for them, and re-layouts: 5.84 us -> 0.04 us
    slice x0 -> x1, local copies, waits for them, and re-layouts: none -> 1.74 us  [body(): updated = jnp.maximum(x[some] - PRIMAL * (x[some] - d[some]), 0.0)]
    pallas_call x14 -> x17, Pallas kernels: 17.6 us -> 17.7 us  [call(): pl.pallas_call(kernel, out_shape=outs, in_specs=ins, out_specs=out_specs...]
  transfers between devices with their start and end apart: 10 -> 11, of which waited for: 7 -> 7; matrix products, arithmetic and copies ran while one was open for 0% -> 0% of each run, Pallas kernels for 13% -> 20%
where the time goes in v3:
time: 67.3 us; the launch traced here: 66.8 us
  starting transfers between devices  29.7 us (44%)
  Pallas kernels  17.7 us (26%)
  waiting for transfers between devices  16.5 us (25%)
  local copies, waits for them, and re-layouts  1.78 us (3%)
  between operations  0.9 us (1%)
    ppermute x7, starting transfers between devices, shift(): lax.ppermute(value, axis, [(source, source + steps) for source in range(i...  23.3 us
    pallas_call x17, Pallas kernels, call(): pl.pallas_call(kernel, out_shape=outs, in_specs=ins, out_specs=out_specs...  17.7 us
    ppermute x7, waiting for transfers between devices, shift(): lax.ppermute(value, axis, [(source, source + steps) for source in range(i...  13.2 us
    ppermute x4, starting transfers between devices, chan_pairs(): lax.ppermute(value, 'chan', [(source, source ^ stride) for source in rang...  6.34 us
    ppermute x4, waiting for transfers between devices, chan_pairs(): lax.ppermute(value, 'chan', [(source, source ^ stride) for source in rang...  3.24 us
    slice x1, local copies, waits for them, and re-layouts, body(): updated = jnp.maximum(x[some] - PRIMAL * (x[some] - d[some]), 0.0)  1.74 us
  transfers between devices with their start and end apart: 11, of which 7 were waited for; matrix products, arithmetic and copies ran while one was open for 0% of the time, Pallas kernels for 20%

profile of v3, /device:TPU:16, one launch (start us, length us, event | category | flops | bytes accessed | tf_op | source)
XLA Modules:
  0.0 66.8 jit_solution(16392474129536616557)
XLA Ops:
  0.7 1.7 %fusion.10 = (f32[64,16,128]{2,1,0:T(8,128)S(1)}, f32[64,16,128]{2,1,0:T(8,128)S(1)}, f32[64,16,128]{2,1,0:T(8,128)S(1)}, f32[64,16,128]{2,1,0:T(8,128)S(1)}) fusion(f32[128,16,128]{2,1,0:T(8,128)} %param.7, f32[128,16,128]{2,1,0:T(8,128)} %param.8), kind=kLoop, calls=%fused_computation.12 | loop fusion | bytes 4194304 | tf_op jit(solution)/shard_map/slice | solution.py:321
  2.6 1.9 %collective-permute-start.3 = (f32[1024,128]{1,0:T(8,128)S(1)}, f32[1024,128]{1,0:T(8,128)S(1)}, u32[]{:S(2)}, u32[]{:S(2)}) collective-permute-start(f32[1024,128]{1,0:T(8,128)S(1)} %fusion.9.refs_0_.refs_1_), channel_id=1, source_target_pairs={{0,2},{2,4},{4,6},{6,8},{8,10},{10,12},{12,14},{14,16},{16,18},{18... | collective-permute-start | bytes 1572872 | tf_op jit(solution)/shard_map/ppermute | solution.py:22
  4.6 3.5 %collective-permute-start.2 = (f32[1024,128]{1,0:T(8,128)S(1)}, f32[1024,128]{1,0:T(8,128)S(1)}, u32[]{:S(2)}, u32[]{:S(2)}) collective-permute-start(f32[1024,128]{1,0:T(8,128)S(1)} %fusion.4.refs_1_.refs_0_), channel_id=1, source_target_pairs={{0,2},{2,4},{4,6},{6,8},{8,10},{10,12},{12,14},{14,16},{16,18},{18... | collective-permute-start | bytes 1572872 | tf_op jit(solution)/shard_map/ppermute | solution.py:22
  9.6 3.0 %collective-permute-start.1 = (f32[1024,128]{1,0:T(8,128)S(1)}, f32[1024,128]{1,0:T(8,128)S(1)}, u32[]{:S(2)}, u32[]{:S(2)}) collective-permute-start(f32[1024,128]{1,0:T(8,128)S(1)} %fusion.9.refs_0_.refs_1_), channel_id=1, source_target_pairs={{2,0},{4,2},{6,4},{8,6},{10,8},{12,10},{14,12},{16,14},{18,16},{20... | collective-permute-start | bytes 1572872 | tf_op jit(solution)/shard_map/ppermute | solution.py:22
  12.6 2.4 %collective-permute-start.6 = (f32[1024,128]{1,0:T(8,128)S(1)}, f32[1024,128]{1,0:T(8,128)S(1)}, u32[]{:S(2)}, u32[]{:S(2)}) collective-permute-start(f32[1024,128]{1,0:T(8,128)S(1)} %fusion.4.refs_1_.refs_0_), channel_id=1, source_target_pairs={{2,0},{4,2},{6,4},{8,6},{10,8},{12,10},{14,12},{16,14},{18,16},{20... | collective-permute-start | bytes 1572872 | tf_op jit(solution)/shard_map/ppermute | solution.py:22
  15.0 1.6 %collective-permute-start = (f32[32,2048]{1,0:T(8,128)S(1)}, f32[32,2048]{1,0:T(8,128)S(1)}, u32[]{:S(2)}, u32[]{:S(2)}) collective-permute-start(f32[32,2048]{1,0:T(8,128)S(1)} %shard_map.95.own_ref), channel_id=1, source_target_pairs={{0,1},{1,0},{2,3},{3,2},{4,5},{5,4},{6,7},{7,6},{8,9},{9,8},{10,11... | collective-permute-start | bytes 786440 | tf_op jit(solution)/shard_map/ppermute | solution.py:27
  17.4 2.3 %collective-permute-done.2.refs_0_ = f32[1024,128]{1,0:T(8,128)S(1)} collective-permute-done((f32[1024,128]{1,0:T(8,128)S(1)}, f32[1024,128]{1,0:T(8,128)S(1)}, u32[]{:S(2)}, u32[]{:S(2)}) %collective-permute-start.2) | collective-permute-done | bytes 524320 | tf_op jit(solution)/shard_map/ppermute | solution.py:22
  20.5 1.6 %collective-permute-start.4 = (f32[128,128]{1,0:T(8,128)S(1)}, f32[128,128]{1,0:T(8,128)S(1)}, u32[]{:S(2)}, u32[]{:S(2)}) collective-permute-start(f32[128,128]{1,0:T(8,128)S(1)} %get-tuple-element.36.own_ref), channel_id=1, source_target_pairs={{0,1},{1,0},{2,3},{3,2},{4,5},{5,4},{6,7},{7,6},{8,9},{9,8},{10,11... | collective-permute-start | bytes 196616 | tf_op jit(solution)/shard_map/ppermute | solution.py:27
  22.1 1.1 %collective-permute-done.other_ref = f32[32,2048]{1,0:T(8,128)S(1)} collective-permute-done((f32[32,2048]{1,0:T(8,128)S(1)}, f32[32,2048]{1,0:T(8,128)S(1)}, u32[]{:S(2)}, u32[]{:S(2)}) %collective-permute-start) | collective-permute-done | bytes 262176 | tf_op jit(solution)/shard_map/ppermute | solution.py:27
  23.7 1.1 %collective-permute-done.4.other_ref = f32[128,128]{1,0:T(8,128)S(1)} collective-permute-done((f32[128,128]{1,0:T(8,128)S(1)}, f32[128,128]{1,0:T(8,128)S(1)}, u32[]{:S(2)}, u32[]{:S(2)}) %collective-permute-start.4) | collective-permute-done | bytes 65568 | tf_op jit(solution)/shard_map/ppermute | solution.py:27
  24.9 1.9 %collective-permute-start.5 = (f32[128,128]{1,0:T(8,128)S(1)}, f32[128,128]{1,0:T(8,128)S(1)}, u32[]{:S(2)}, u32[]{:S(2)}) collective-permute-start(f32[128,128]{1,0:T(8,128)S(1)} %shard_map.100.scale_ref.refs_5_), channel_id=1, source_target_pairs={{2,0},{4,2},{6,4},{8,6},{10,8},{12,10},{14,12},{16,14},{18,16},{20... | collective-permute-start | bytes 196616 | tf_op jit(solution)/shard_map/ppermute | solution.py:22
  28.6 1.1 %shard_map.101.refs_0_ = f32[1024,128]{1,0:T(8,128)S(1)} custom-call(f32[8192,128]{1,0:T(8,128)S(1)} %get-tuple-element.37.dual_ref.refs_4_, bf16[32,256]{1,0:T(8,128)(2,1)S(1)} %get-tuple-element.38.lhs_ref, f32[128,128]{1,0:T(8,128)S(1)} %shard_map.100.scale_ref.refs_5_, f32[2048,128]{1,0:T(8,128)S(1)} %shard_map.96.refs_0_, f32[2048,128]{1,0:T(8,128)S(1)} %bitcast.36, ...), custom_call_target="tpu_custom_call" | custom-call | flops 201326592 | bytes 4194304 | tf_op jit(solution)/shard_map/pallas_call | solution.py:282
  29.7 1.1 %shard_map.104.refs_0_ = f32[1024,128]{1,0:T(8,128)S(1)} custom-call(f32[8192,128]{1,0:T(8,128)S(1)} %get-tuple-element.41.dual_ref.refs_4_, bf16[32,256]{1,0:T(8,128)(2,1)S(1)} %get-tuple-element.38.lhs_ref, f32[128,128]{1,0:T(8,128)S(1)} %shard_map.100.scale_ref.refs_5_, f32[2048,128]{1,0:T(8,128)S(1)} %shard_map.96.refs_0_, f32[2048,128]{1,0:T(8,128)S(1)} %bitcast.37, ...), custom_call_target="tpu_custom_call" | custom-call | flops 201326592 | bytes 4194304 | tf_op jit(solution)/shard_map/pallas_call | solution.py:282
  30.7 5.0 %collective-permute-done.5.scale_ref = f32[128,128]{1,0:T(8,128)S(1)} collective-permute-done((f32[128,128]{1,0:T(8,128)S(1)}, f32[128,128]{1,0:T(8,128)S(1)}, u32[]{:S(2)}, u32[]{:S(2)}) %collective-permute-start.5) | collective-permute-done | bytes 65568 | tf_op jit(solution)/shard_map/ppermute | solution.py:22
  35.8 1.1 %shard_map.102 = (f32[1024,128]{1,0:T(8,128)S(1)}, f32[1024,128]{1,0:T(8,128)S(1)}) custom-call(f32[8192,128]{1,0:T(8,128)S(1)} %shard_map.97.dual_ref, bf16[32,256]{1,0:T(8,128)(2,1)S(1)} %get-tuple-element.33.lhs_ref, f32[128,128]{1,0:T(8,128)S(1)} %collective-permute-done.5.scale_ref, f32[1024,128]{1,0:T(8,128)S(1)} %shard_map.101.refs_0_, ...), custom_call_target="tpu_custom_call" | custom-call | flops 201326592 | bytes 4194304 | tf_op jit(solution)/shard_map/pallas_call | solution.py:282
  36.8 6.7 %collective-permute-start.8 = (f32[1024,128]{1,0:T(8,128)S(1)}, f32[1024,128]{1,0:T(8,128)S(1)}, u32[]{:S(2)}, u32[]{:S(2)}) collective-permute-start(f32[1024,128]{1,0:T(8,128)S(1)} %get-tuple-element.39.refs_1_), channel_id=1, source_target_pairs={{0,2},{2,4},{4,6},{6,8},{8,10},{10,12},{12,14},{14,16},{16,18},{18... | collective-permute-start | bytes 1572872 | tf_op jit(solution)/shard_map/ppermute | solution.py:22
  43.6 1.1 %shard_map.105 = (f32[1024,128]{1,0:T(8,128)S(1)}, f32[1024,128]{1,0:T(8,128)S(1)}) custom-call(f32[8192,128]{1,0:T(8,128)S(1)} %shard_map.103.dual_ref, bf16[32,256]{1,0:T(8,128)(2,1)S(1)} %get-tuple-element.33.lhs_ref, f32[128,128]{1,0:T(8,128)S(1)} %collective-permute-done.5.scale_ref, f32[1024,128]{1,0:T(8,128)S(1)} %shard_map.104.refs_0_, ...), custom_call_target="tpu_custom_call" | custom-call | flops 201326592 | bytes 4194304 | tf_op jit(solution)/shard_map/pallas_call | solution.py:282
  44.6 3.9 %collective-permute-start.9 = (f32[1024,128]{1,0:T(8,128)S(1)}, f32[1024,128]{1,0:T(8,128)S(1)}, u32[]{:S(2)}, u32[]{:S(2)}) collective-permute-start(f32[1024,128]{1,0:T(8,128)S(1)} %get-tuple-element.42.refs_2_.refs_1_), channel_id=1, source_target_pairs={{0,2},{2,4},{4,6},{6,8},{8,10},{10,12},{12,14},{14,16},{16,18},{18... | collective-permute-start | bytes 1572872 | tf_op jit(solution)/shard_map/ppermute | solution.py:22
  49.4 1.6 %collective-permute-start.7 = (f32[32,2048]{1,0:T(8,128)S(1)}, f32[32,2048]{1,0:T(8,128)S(1)}, u32[]{:S(2)}, u32[]{:S(2)}) collective-permute-start(f32[32,2048]{1,0:T(8,128)S(1)} %shard_map.106.own_ref), channel_id=1, source_target_pairs={{0,1},{1,0},{2,3},{3,2},{4,5},{5,4},{6,7},{7,6},{8,9},{9,8},{10,11... | collective-permute-start | bytes 786440 | tf_op jit(solution)/shard_map/ppermute | solution.py:27
  51.0 1.3 %collective-permute-done.8.refs_0_ = f32[1024,128]{1,0:T(8,128)S(1)} collective-permute-done((f32[1024,128]{1,0:T(8,128)S(1)}, f32[1024,128]{1,0:T(8,128)S(1)}, u32[]{:S(2)}, u32[]{:S(2)}) %collective-permute-start.8) | collective-permute-done | bytes 524320 | tf_op jit(solution)/shard_map/ppermute | solution.py:22
  53.2 4.7 %collective-permute-done.9.refs_0_ = f32[1024,128]{1,0:T(8,128)S(1)} collective-permute-done((f32[1024,128]{1,0:T(8,128)S(1)}, f32[1024,128]{1,0:T(8,128)S(1)}, u32[]{:S(2)}, u32[]{:S(2)}) %collective-permute-start.9) | collective-permute-done | bytes 524320 | tf_op jit(solution)/shard_map/ppermute | solution.py:22
  58.9 1.6 %collective-permute-start.10 = (f32[128,128]{1,0:T(8,128)S(1)}, f32[128,128]{1,0:T(8,128)S(1)}, u32[]{:S(2)}, u32[]{:S(2)}) collective-permute-start(f32[128,128]{1,0:T(8,128)S(1)} %get-tuple-element.49.refs_3_), channel_id=1, source_target_pairs={{0,1},{1,0},{2,3},{3,2},{4,5},{5,4},{6,7},{7,6},{8,9},{9,8},{10,11... | collective-permute-start | bytes 196616 | tf_op jit(solution)/shard_map/ppermute | solution.py:27
  60.4 1.8 %shard_map.107 = (f32[2048,128]{1,0:T(8,128)}, f32[2048,128]{1,0:T(8,128)}) custom-call(bf16[128,96]{1,0:T(8,128)(2,1)S(1)} %get-tuple-element.27.lhs_ref, f32[32,2048]{1,0:T(8,128)S(1)} %shard_map.106.own_ref, f32[32,2048]{1,0:T(8,128)S(1)} %collective-permute-done.7.other_ref, f32[32,128]{1,0:T(8,128)S(1)} %get-tuple-element.30.bounds_ref, ...), custom_call_target="tpu_custom_call" | custom-call | flops 50331648 | bytes 2097152 | tf_op jit(solution)/shard_map/pallas_call | solution.py:282
  63.2 3.6 %shard_map.110 = f32[8,128,16,128]{3,2,1,0:T(8,128)} custom-call(f32[8192,128]{1,0:T(8,128)S(1)} %get-tuple-element.46.refs_0_, f32[8192,128]{1,0:T(8,128)S(1)} %get-tuple-element.48.refs_1_, f32[128,128]{1,0:T(8,128)S(1)} %bitcast.45, f32[128,128]{1,0:T(8,128)S(1)} %get-tuple-element.49.refs_3_, f32[128,128]{1,0:T(8,128)S(1)} %collective-permute-done.10.refs_4_), custom_call_target="tpu_custom_call" | custom-call | flops 2097152 | bytes 16777216 | tf_op jit(solution)/shard_map/pallas_call | solution.py:282
  (33 shorter events, 9.3 us)
Async XLA Ops:
  0.6 7.5 %copy-start.4 = (f32[8,16]{1,0:T(8,128)S(1)}, f32[8,16]{1,0:T(8,128)}, u32[]{:S(2)}) copy-start(f32[8,16]{1,0:T(8,128)} %filters_ref.1) | copy-start | bytes 1540
  0.6 7.5 %copy-start.5 = (f32[32]{0:T(128)S(1)}, f32[32]{0:T(128)}, u32[]{:S(2)}) copy-start(f32[32]{0:T(128)} %bounds_ref.1) | copy-start | bytes 388
  0.7 7.5 %copy-start.6 = (s32[16]{0:T(128)S(1)}, s32[16]{0:T(128)}, u32[]{:S(2)}) copy-start(s32[16]{0:T(128)} %margin_ref.1) | copy-start | bytes 196
  0.7 7.5 %copy-start.3 = (f32[1,128,32]{1,2,0:T(8,128)S(1)}, f32[1,128,32]{1,2,0:T(8,128)}, u32[]{:S(2)}) copy-start(f32[1,128,32]{1,2,0:T(8,128)} %param.11) | copy-start | bytes 49156
  2.4 22.5 %copy-start.2 = (f32[8,16,128]{2,1,0:T(8,128)S(1)}, f32[8,16,128]{2,1,0:T(8,128)}, u32[]{:S(2)}) copy-start(f32[8,16,128]{2,1,0:T(8,128)} %param.9) | copy-start | bytes 196612
  2.6 14.0 %collective-permute-start.3 = (f32[1024,128]{1,0:T(8,128)S(1)}, f32[1024,128]{1,0:T(8,128)S(1)}, u32[]{:S(2)}, u32[]{:S(2)}) collective-permute-start(f32[1024,128]{1,0:T(8,128)S(1)} %fusion.9.refs_0_.refs_1_), channel_id=1, source_target_pairs={{0,2},{2,4},{4,6},{6,8},{8,10},{10,12},{12,14},{14,16},{16,18},{18... | collective-permute-start | bytes 1572872 | tf_op jit(solution)/shard_map/ppermute | solution.py:22
  4.6 15.1 %collective-permute-start.2 = (f32[1024,128]{1,0:T(8,128)S(1)}, f32[1024,128]{1,0:T(8,128)S(1)}, u32[]{:S(2)}, u32[]{:S(2)}) collective-permute-start(f32[1024,128]{1,0:T(8,128)S(1)} %fusion.4.refs_1_.refs_0_), channel_id=1, source_target_pairs={{0,2},{2,4},{4,6},{6,8},{8,10},{10,12},{12,14},{14,16},{16,18},{18... | collective-permute-start | bytes 1572872 | tf_op jit(solution)/shard_map/ppermute | solution.py:22
  9.6 17.3 %collective-permute-start.1 = (f32[1024,128]{1,0:T(8,128)S(1)}, f32[1024,128]{1,0:T(8,128)S(1)}, u32[]{:S(2)}, u32[]{:S(2)}) collective-permute-start(f32[1024,128]{1,0:T(8,128)S(1)} %fusion.9.refs_0_.refs_1_), channel_id=1, source_target_pairs={{2,0},{4,2},{6,4},{8,6},{10,8},{12,10},{14,12},{16,14},{18,16},{20... | collective-permute-start | bytes 1572872 | tf_op jit(solution)/shard_map/ppermute | solution.py:22
  12.6 15.2 %collective-permute-start.6 = (f32[1024,128]{1,0:T(8,128)S(1)}, f32[1024,128]{1,0:T(8,128)S(1)}, u32[]{:S(2)}, u32[]{:S(2)}) collective-permute-start(f32[1024,128]{1,0:T(8,128)S(1)} %fusion.4.refs_1_.refs_0_), channel_id=1, source_target_pairs={{2,0},{4,2},{6,4},{8,6},{10,8},{12,10},{14,12},{16,14},{18,16},{20... | collective-permute-start | bytes 1572872 | tf_op jit(solution)/shard_map/ppermute | solution.py:22
  15.0 8.3 %collective-permute-start = (f32[32,2048]{1,0:T(8,128)S(1)}, f32[32,2048]{1,0:T(8,128)S(1)}, u32[]{:S(2)}, u32[]{:S(2)}) collective-permute-start(f32[32,2048]{1,0:T(8,128)S(1)} %shard_map.95.own_ref), channel_id=1, source_target_pairs={{0,1},{1,0},{2,3},{3,2},{4,5},{5,4},{6,7},{7,6},{8,9},{9,8},{10,11... | collective-permute-start | bytes 786440 | tf_op jit(solution)/shard_map/ppermute | solution.py:27
  20.5 4.3 %collective-permute-start.4 = (f32[128,128]{1,0:T(8,128)S(1)}, f32[128,128]{1,0:T(8,128)S(1)}, u32[]{:S(2)}, u32[]{:S(2)}) collective-permute-start(f32[128,128]{1,0:T(8,128)S(1)} %get-tuple-element.36.own_ref), channel_id=1, source_target_pairs={{0,1},{1,0},{2,3},{3,2},{4,5},{5,4},{6,7},{7,6},{8,9},{9,8},{10,11... | collective-permute-start | bytes 196616 | tf_op jit(solution)/shard_map/ppermute | solution.py:27
  24.9 10.9 %collective-permute-start.5 = (f32[128,128]{1,0:T(8,128)S(1)}, f32[128,128]{1,0:T(8,128)S(1)}, u32[]{:S(2)}, u32[]{:S(2)}) collective-permute-start(f32[128,128]{1,0:T(8,128)S(1)} %shard_map.100.scale_ref.refs_5_), channel_id=1, source_target_pairs={{2,0},{4,2},{6,4},{8,6},{10,8},{12,10},{14,12},{16,14},{18,16},{20... | collective-permute-start | bytes 196616 | tf_op jit(solution)/shard_map/ppermute | solution.py:22
  26.9 1.7 %copy-start = (f32[128,16,128]{2,1,0:T(8,128)S(1)}, f32[128,16,128]{2,1,0:T(8,128)}, u32[]{:S(2)}) copy-start(f32[128,16,128]{2,1,0:T(8,128)} %param.7) | copy-start | bytes 3145732
  26.9 1.7 %copy-start.1 = (f32[128,16,128]{2,1,0:T(8,128)S(1)}, f32[128,16,128]{2,1,0:T(8,128)}, u32[]{:S(2)}) copy-start(f32[128,16,128]{2,1,0:T(8,128)} %param.8) | copy-start | bytes 3145732
  36.8 15.5 %collective-permute-start.8 = (f32[1024,128]{1,0:T(8,128)S(1)}, f32[1024,128]{1,0:T(8,128)S(1)}, u32[]{:S(2)}, u32[]{:S(2)}) collective-permute-start(f32[1024,128]{1,0:T(8,128)S(1)} %get-tuple-element.39.refs_1_), channel_id=1, source_target_pairs={{0,2},{2,4},{4,6},{6,8},{8,10},{10,12},{12,14},{14,16},{16,18},{18... | collective-permute-start | bytes 1572872 | tf_op jit(solution)/shard_map/ppermute | solution.py:22
  44.6 13.3 %collective-permute-start.9 = (f32[1024,128]{1,0:T(8,128)S(1)}, f32[1024,128]{1,0:T(8,128)S(1)}, u32[]{:S(2)}, u32[]{:S(2)}) collective-permute-start(f32[1024,128]{1,0:T(8,128)S(1)} %get-tuple-element.42.refs_2_.refs_1_), channel_id=1, source_target_pairs={{0,2},{2,4},{4,6},{6,8},{8,10},{10,12},{12,14},{14,16},{16,18},{18... | collective-permute-start | bytes 1572872 | tf_op jit(solution)/shard_map/ppermute | solution.py:22
  49.4 11.0 %collective-permute-start.7 = (f32[32,2048]{1,0:T(8,128)S(1)}, f32[32,2048]{1,0:T(8,128)S(1)}, u32[]{:S(2)}, u32[]{:S(2)}) collective-permute-start(f32[32,2048]{1,0:T(8,128)S(1)} %shard_map.106.own_ref), channel_id=1, source_target_pairs={{0,1},{1,0},{2,3},{3,2},{4,5},{5,4},{6,7},{7,6},{8,9},{9,8},{10,11... | collective-permute-start | bytes 786440 | tf_op jit(solution)/shard_map/ppermute | solution.py:27
  58.9 4.3 %collective-permute-start.10 = (f32[128,128]{1,0:T(8,128)S(1)}, f32[128,128]{1,0:T(8,128)S(1)}, u32[]{:S(2)}, u32[]{:S(2)}) collective-permute-start(f32[128,128]{1,0:T(8,128)S(1)} %get-tuple-element.49.refs_3_), channel_id=1, source_target_pairs={{0,1},{1,0},{2,3},{3,2},{4,5},{5,4},{6,7},{7,6},{8,9},{9,8},{10,11... | collective-permute-start | bytes 196616 | tf_op jit(solution)/shard_map/ppermute | solution.py:27

commit v4 on v3

--- a/solution.py
+++ b/solution.py
@@ -14,6 +14,7 @@
 CHUNKS = 2
 GROUP = 32
 VMEM_LIMIT = 24 << 20
+REFLECT_LIMIT = 56000000
 
 
 def shift(value, axis, steps):
@@ -114,10 +115,25 @@
     limits_ref[...] = limits
 
 
+def reflect_kernel(start, x_ref, d_ref, r_ref, x_buffer, d_buffer, sems):
+    rows = pl.ds(start, r_ref.shape[0])
+    copies = [
+        pltpu.make_async_copy(source.at[rows], target, sems.at[turn])
+        for turn, (source, target) in enumerate(((x_ref, x_buffer), (d_ref, d_buffer)))
+    ]
+    for copy in copies:
+        copy.start()
+    for copy in copies:
+        copy.wait()
+    x = x_buffer[...]
+    updated = jnp.maximum(x - PRIMAL * (x - d_buffer[...]), 0.0)
+    r_ref[...] = 2.0 * updated - x
+
+
 def coef_kernel(height, spectral, lhs_ref, *refs):
-    out_ref = refs[-1]
-    s_ref = refs[0] if spectral else None
-    r_refs = refs[1 if spectral else 0 : -1]
+    *r_refs, out_ref = refs
+    if spectral:
+        s_ref, *r_refs = r_refs
     rank = out_ref.shape[0]
 
     def pixels(row):
@@ -165,9 +181,7 @@
 
 
 def lift_kernel(height, kind, *refs):
-    if kind == "next":
-        halo_ref, own_ref, lhs_ref, out_ref = refs
-    elif kind == "first":
+    if kind == "first":
         halo_ref, own_ref, lhs_ref, before_ref, out_ref, squares_ref = refs
     else:
         halo_ref, own_ref, lhs_ref, before_ref, dual_ref, scale_ref, out_ref, squares_ref = refs
@@ -191,21 +205,13 @@
                 if kind == "second":
                     lifted = lifted + dual_ref[rows, :] * scale
                 out_ref[rows, :] = lifted
-                if kind != "next":
-                    total = total + lifted * lifted
+                total = total + lifted * lifted
         return total
 
-    if kind == "next":
-        lax.fori_loop(0, channels // many, step, 0)
-    else:
-        squares_ref[...] = lax.fori_loop(0, channels // many, step, before_ref[...])
-
-
-def adjoint_kernel(height, start, border, dual_ref, lhs_ref, scale_ref, *refs):
-    if border:
-        partial_ref, x_ref, d_ref, updated_ref, reflected_ref = refs
-    else:
-        s_ref, x_ref, d_ref, partial_ref = refs
+    squares_ref[...] = lax.fori_loop(0, channels // many, step, before_ref[...])
+
+
+def adjoint_kernel(height, start, dual_ref, lhs_ref, scale_ref, s_ref, x_ref, d_ref, partial_ref):
     size, lanes = scale_ref.shape
     channels = partial_ref.shape[0] // height
     scale = scale_ref[...]
@@ -223,15 +229,48 @@
             for half in range(2):
                 rows = pl.ds(pl.multiple_of((channel + half) * height, height), height)
                 cube = pl.ds(pl.multiple_of(start + (channel + half) * height, height), height)
-                mine = spread[:, half * lanes : (half + 1) * lanes]
                 x, d = x_ref[cube, :], d_ref[cube, :]
                 before = jnp.maximum(x - PRIMAL * (x - d), 0.0)
-                if border:
-                    updated = jnp.maximum(partial_ref[rows, :] - PRIMAL * mine, 0.0)
-                    updated_ref[rows, :] = updated
-                    reflected_ref[rows, :] = 2.0 * updated - before
-                else:
-                    partial_ref[rows, :] = before - PRIMAL * ((before - d) + s_ref[cube, :] + mine)
+                mine = spread[:, half * lanes : (half + 1) * lanes]
+                partial_ref[rows, :] = before - PRIMAL * ((before - d) + s_ref[cube, :] + mine)
+        return carry
+
+    lax.fori_loop(0, channels // many, step, 0)
+
+
+def border_kernel(
+    height, start, own_ref, below_ref, next_ref, border_ref, scale_ref, partial_ref, x_ref, d_ref, updated_ref, reflected_ref
+):
+    size, lanes = scale_ref.shape
+    channels = partial_ref.shape[0] // height
+    scale = jnp.concatenate([scale_ref[...]] * 2, axis=1)
+    lift_lhs = next_ref[...]
+    border_lhs = border_ref[...]
+    many = min(GROUP, channels)
+
+    def step(group, carry):
+        for pair in range(0, many, 2):
+            channel = group * many + pair
+            spans = [
+                (
+                    pl.ds(pl.multiple_of((channel + half) * height, height), height),
+                    pl.ds(pl.multiple_of(start + (channel + half) * height, height), height),
+                )
+                for half in range(2)
+            ]
+            value = jnp.concatenate(
+                [jnp.concatenate([own_ref[rows, :], below_ref[rows, :]], axis=0) for rows, cube in spans], axis=1
+            )
+            duals = dot(lift_lhs, three_rhs(value)) * scale
+            both = dot(border_lhs, two_rhs(duals))
+            spread = both[:height] + both[height:]
+            for half, (rows, cube) in enumerate(spans):
+                x, d = x_ref[cube, :], d_ref[cube, :]
+                before = jnp.maximum(x - PRIMAL * (x - d), 0.0)
+                mine = spread[:, half * lanes : (half + 1) * lanes]
+                updated = jnp.maximum(partial_ref[rows, :] - PRIMAL * mine, 0.0)
+                updated_ref[rows, :] = updated
+                reflected_ref[rows, :] = 2.0 * updated - before
         return carry
 
     lax.fori_loop(0, channels // many, step, 0)
@@ -317,9 +356,11 @@
 
     reflected = []
     for index in range(chunks):
-        some = slice(index * block, (index + 1) * block)
-        updated = jnp.maximum(x[some] - PRIMAL * (x[some] - d[some]), 0.0)
-        reflected.append(2.0 * updated - x[some])
+        reflected.append(call(
+            functools.partial(reflect_kernel, index * block), flat(block), [distant] * 2, (x, d),
+            4 * block * lanes, 12 * block * lanes,
+            scratch=[pltpu.VMEM((block, lanes), F32)] * 2 + [pltpu.SemaphoreType.DMA((2,))], limit=REFLECT_LIMIT,
+        ))
     halos = [shift(r, "facet", 1) for r in reflected]
 
     lift_lhs, next_lhs, interior_lhs, border_lhs, coef_lhs, spectral_lhs, limits = call(
@@ -338,9 +379,9 @@
 
     def coefficients(parts, spectral):
         operands = (coef_lhs,) + ((spectral,) if spectral is not None else ()) + tuple(parts)
+        outs = jax.ShapeDtypeStruct((rank, height * lanes), F32)
         return call(
-            functools.partial(coef_kernel, height, spectral is not None),
-            jax.ShapeDtypeStruct((rank, height * lanes), F32),
+            functools.partial(coef_kernel, height, spectral is not None), outs,
             [whole()] * len(operands), operands, 6 * rank * rows * lanes, 2 * cubes,
         )
 
@@ -352,35 +393,43 @@
         )
 
     coefs = coefficients(reflected, None)
-    tied = lax.optimization_barrier((coefs, *reflected))
-    terms = chan_terms(tied[0])
-    below = [shift(r, "facet", -1) for r in tied[1:]]
-    (spectral,) = synthesis(*terms)
-
+    terms = chan_terms(coefs)
     squares = jnp.zeros((size, lanes), F32)
-    lifted = []
+    lifted, below = [], []
     for index in range(chunks):
         out, squares = call(
             functools.partial(lift_kernel, height, "first"), [flat(per * size), flat(size)], [whole()] * 4,
             (halos[index], reflected[index], lift_lhs, squares), work, duals,
         )
         lifted.append(out)
-    scale = call(scale_kernel, flat(size), [whole()] * 3, (w, *chan_terms(squares)), 10 * size * lanes, 16 * size * lanes)
+        if index < chunks - 1:
+            tied, _, _ = lax.optimization_barrier((reflected[index], squares, coefs))
+            below.append(shift(tied, "facet", -1))
+            squares, halos[index + 1] = lax.optimization_barrier((squares, halos[index + 1]))
+        elif index:
+            tied, _, *terms = lax.optimization_barrier((reflected[index], halos[index], *terms))
+            below.append(shift(tied, "facet", -1))
+        else:
+            below.append(shift(reflected[index], "facet", -1))
+    own, other = chan_terms(squares)
+    *terms, _ = lax.optimization_barrier((*terms, squares))
+    (spectral,) = synthesis(*terms)
+    other, spectral = lax.optimization_barrier((other, spectral))
+    scale = call(scale_kernel, flat(size), [whole()] * 3, (w, own, other), 10 * size * lanes, 16 * size * lanes)
     scale_below = shift(scale, "facet", -1)
 
+    partials = [
+        call(
+            functools.partial(adjoint_kernel, height, index * block), flat(block), [whole()] * 6,
+            (lifted[index], interior_lhs, scale, spectral, x, d), work, duals,
+        )
+        for index in range(chunks)
+    ]
     image, halos, again = [], [], []
     for index in range(chunks):
-        dual_below = call(
-            functools.partial(lift_kernel, height, "next"), flat(per * size), [whole()] * 3,
-            (reflected[index], below[index], next_lhs), work, duals,
-        )
-        partial = call(
-            functools.partial(adjoint_kernel, height, index * block, False), flat(block), [whole()] * 6,
-            (lifted[index], interior_lhs, scale, spectral, x, d), work, duals,
-        )
         updated, r = call(
-            functools.partial(adjoint_kernel, height, index * block, True), [flat(block)] * 2, [whole()] * 6,
-            (dual_below, border_lhs, scale_below, partial, x, d), work, duals,
+            functools.partial(border_kernel, height, index * block), [flat(block)] * 2, [whole()] * 8,
+            (reflected[index], below[index], next_lhs, border_lhs, scale_below, partials[index], x, d), 2 * work, duals,
         )
         image.append(updated)
         again.append(r)

time: 67.3 us -> 58.8 us (0.87)
  starting transfers between devices: 29.7 us -> 22.9 us
  Pallas kernels: 17.7 us -> 19.9 us
  local copies, waits for them, and re-layouts: 1.78 us -> 0.04 us
  waiting for transfers between devices: 16.5 us -> 14.8 us
    ppermute x7, starting transfers between devices: 23.3 us -> 16.6 us  [shift(): lax.ppermute(value, axis, [(source, source + steps) for source in range(i...]
    pallas_call x17, Pallas kernels: 17.7 us -> 19.9 us  [call(): pl.pallas_call(kernel, out_shape=outs, in_specs=ins, out_specs=out_specs...]
    ppermute x7, waiting for transfers between devices: 13.2 us -> 11.3 us  [shift(): lax.ppermute(value, axis, [(source, source + steps) for source in range(i...]
    slice x1 -> x0, local copies, waits for them, and re-layouts: 1.74 us -> none  [body(): updated = jnp.maximum(x[some] - PRIMAL * (x[some] - d[some]), 0.0)]
  transfers between devices with their start and end apart: 11 -> 11, of which waited for: 7 -> 6; matrix products, arithmetic and copies ran while one was open for 0% -> 0% of each run, Pallas kernels for 20% -> 26%
where the time goes in v4:
time: 58.8 us; the launch traced here: 58.5 us
  starting transfers between devices  22.9 us (39%)
  Pallas kernels  19.9 us (34%)
  waiting for transfers between devices  14.8 us (25%)
  between operations  0.89 us (2%)
    pallas_call x17, Pallas kernels, call(): pl.pallas_call(kernel, out_shape=outs, in_specs=ins, out_specs=out_specs...  19.9 us
    ppermute x7, starting transfers between devices, shift(): lax.ppermute(value, axis, [(source, source + steps) for source in range(i...  16.6 us
    ppermute x7, waiting for transfers between devices, shift(): lax.ppermute(value, axis, [(source, source + steps) for source in range(i...  11.3 us
    ppermute x4, starting transfers between devices, chan_pairs(): lax.ppermute(value, 'chan', [(source, source ^ stride) for source in rang...  6.3 us
    ppermute x4, waiting for transfers between devices, chan_pairs(): lax.ppermute(value, 'chan', [(source, source ^ stride) for source in rang...  3.48 us
  transfers between devices with their start and end apart: 11, of which 6 were waited for; matrix products, arithmetic and copies ran while one was open for 0% of the time, Pallas kernels for 26%

profile of v4, /device:TPU:16, one launch (start us, length us, event | category | flops | bytes accessed | tf_op | source)
XLA Modules:
  0.0 58.5 jit_solution(4546791687487174039)
XLA Ops:
  0.7 1.3 %shard_map.95.refs_1_.refs_0_.own_ref = f32[1024,128]{1,0:T(8,128)S(1)} custom-call(f32[2048,128]{1,0:T(8,128)} %bitcast.8, f32[2048,128]{1,0:T(8,128)} %bitcast.14), custom_call_target="tpu_custom_call" | custom-call | flops 524288 | bytes 1572864 | tf_op jit(solution)/shard_map/pallas_call | solution.py:321
  2.1 2.1 %collective-permute-start = (f32[1024,128]{1,0:T(8,128)S(1)}, f32[1024,128]{1,0:T(8,128)S(1)}, u32[]{:S(2)}, u32[]{:S(2)}) collective-permute-start(f32[1024,128]{1,0:T(8,128)S(1)} %shard_map.95.refs_1_.refs_0_.own_ref), channel_id=1, source_target_pairs={{0,2},{2,4},{4,6},{6,8},{8,10},{10,12},{12,14},{14,16},{16,18},{18... | collective-permute-start | bytes 1572872 | tf_op jit(solution)/shard_map/ppermute | solution.py:23
  4.1 1.3 %shard_map.97.refs_1_.own_ref = f32[1024,128]{1,0:T(8,128)S(1)} custom-call(f32[2048,128]{1,0:T(8,128)} %bitcast.9, f32[2048,128]{1,0:T(8,128)} %bitcast.15), custom_call_target="tpu_custom_call" | custom-call | flops 524288 | bytes 1572864 | tf_op jit(solution)/shard_map/pallas_call | solution.py:321
  5.5 3.5 %collective-permute-start.1 = (f32[1024,128]{1,0:T(8,128)S(1)}, f32[1024,128]{1,0:T(8,128)S(1)}, u32[]{:S(2)}, u32[]{:S(2)}) collective-permute-start(f32[1024,128]{1,0:T(8,128)S(1)} %shard_map.97.refs_1_.own_ref), channel_id=1, source_target_pairs={{0,2},{2,4},{4,6},{6,8},{8,10},{10,12},{12,14},{14,16},{16,18},{18... | collective-permute-start | bytes 1572872 | tf_op jit(solution)/shard_map/ppermute | solution.py:23
  10.4 1.6 %collective-permute-start.3 = (f32[32,2048]{1,0:T(8,128)S(1)}, f32[32,2048]{1,0:T(8,128)S(1)}, u32[]{:S(2)}, u32[]{:S(2)}) collective-permute-start(f32[32,2048]{1,0:T(8,128)S(1)} %shard_map.99.own_ref), channel_id=1, source_target_pairs={{0,1},{1,0},{2,3},{3,2},{4,5},{5,4},{6,7},{7,6},{8,9},{9,8},{10,11... | collective-permute-start | bytes 786440 | tf_op jit(solution)/shard_map/ppermute | solution.py:28
  12.0 1.6 %collective-permute-done.refs_0_ = f32[1024,128]{1,0:T(8,128)S(1)} collective-permute-done((f32[1024,128]{1,0:T(8,128)S(1)}, f32[1024,128]{1,0:T(8,128)S(1)}, u32[]{:S(2)}, u32[]{:S(2)}) %collective-permute-start) | collective-permute-done | bytes 524320 | tf_op jit(solution)/shard_map/ppermute | solution.py:23
  14.5 1.9 %collective-permute-start.4 = (f32[1024,128]{1,0:T(8,128)S(1)}, f32[1024,128]{1,0:T(8,128)S(1)}, u32[]{:S(2)}, u32[]{:S(2)}) collective-permute-start(f32[1024,128]{1,0:T(8,128)S(1)} %shard_map.95.refs_1_.refs_0_.own_ref), channel_id=1, source_target_pairs={{2,0},{4,2},{6,4},{8,6},{10,8},{12,10},{14,12},{16,14},{18,16},{20... | collective-permute-start | bytes 1572872 | tf_op jit(solution)/shard_map/ppermute | solution.py:23
  16.4 2.9 %collective-permute-done.1.refs_0_ = f32[1024,128]{1,0:T(8,128)S(1)} collective-permute-done((f32[1024,128]{1,0:T(8,128)S(1)}, f32[1024,128]{1,0:T(8,128)S(1)}, u32[]{:S(2)}, u32[]{:S(2)}) %collective-permute-start.1) | collective-permute-done | bytes 524320 | tf_op jit(solution)/shard_map/ppermute | solution.py:23
  19.3 1.9 %collective-permute-start.6 = (f32[1024,128]{1,0:T(8,128)S(1)}, f32[1024,128]{1,0:T(8,128)S(1)}, u32[]{:S(2)}, u32[]{:S(2)}) collective-permute-start(f32[1024,128]{1,0:T(8,128)S(1)} %shard_map.97.refs_1_.own_ref), channel_id=1, source_target_pairs={{2,0},{4,2},{6,4},{8,6},{10,8},{12,10},{14,12},{16,14},{18,16},{20... | collective-permute-start | bytes 1572872 | tf_op jit(solution)/shard_map/ppermute | solution.py:23
  22.1 1.6 %collective-permute-start.2 = (f32[128,128]{1,0:T(8,128)S(1)}, f32[128,128]{1,0:T(8,128)S(1)}, u32[]{:S(2)}, u32[]{:S(2)}) collective-permute-start(f32[128,128]{1,0:T(8,128)S(1)} %get-tuple-element.40.own_ref), channel_id=1, source_target_pairs={{0,1},{1,0},{2,3},{3,2},{4,5},{5,4},{6,7},{7,6},{8,9},{9,8},{10,11... | collective-permute-start | bytes 196616 | tf_op jit(solution)/shard_map/ppermute | solution.py:28
  24.1 2.5 %collective-permute-done.2.other_ref = f32[128,128]{1,0:T(8,128)S(1)} collective-permute-done((f32[128,128]{1,0:T(8,128)S(1)}, f32[128,128]{1,0:T(8,128)S(1)}, u32[]{:S(2)}, u32[]{:S(2)}) %collective-permute-start.2) | collective-permute-done | bytes 65568 | tf_op jit(solution)/shard_map/ppermute | solution.py:28
  26.7 2.1 %collective-permute-start.5 = (f32[128,128]{1,0:T(8,128)S(1)}, f32[128,128]{1,0:T(8,128)S(1)}, u32[]{:S(2)}, u32[]{:S(2)}) collective-permute-start(f32[128,128]{1,0:T(8,128)S(1)} %shard_map.101.scale_ref.refs_5_), channel_id=1, source_target_pairs={{2,0},{4,2},{6,4},{8,6},{10,8},{12,10},{14,12},{16,14},{18,16},{20... | collective-permute-start | bytes 196616 | tf_op jit(solution)/shard_map/ppermute | solution.py:23
  28.8 1.1 %shard_map.104.partial_ref = f32[1024,128]{1,0:T(8,128)S(1)} custom-call(f32[8192,128]{1,0:T(8,128)S(1)} %get-tuple-element.55.dual_ref.refs_4_, bf16[32,256]{1,0:T(8,128)(2,1)S(1)} %get-tuple-element.52.lhs_ref, f32[128,128]{1,0:T(8,128)S(1)} %shard_map.101.scale_ref.refs_5_, f32[2048,128]{1,0:T(8,128)S(1)} %shard_map.100.s_ref.refs_0_, ...), custom_call_target="tpu_custom_call" | custom-call | flops 201326592 | bytes 4194304 | tf_op jit(solution)/shard_map/pallas_call | solution.py:321
  29.8 1.1 %shard_map.102.partial_ref = f32[1024,128]{1,0:T(8,128)S(1)} custom-call(f32[8192,128]{1,0:T(8,128)S(1)} %get-tuple-element.51.dual_ref.refs_4_, bf16[32,256]{1,0:T(8,128)(2,1)S(1)} %get-tuple-element.52.lhs_ref, f32[128,128]{1,0:T(8,128)S(1)} %shard_map.101.scale_ref.refs_5_, f32[2048,128]{1,0:T(8,128)S(1)} %shard_map.100.s_ref.refs_0_, ...), custom_call_target="tpu_custom_call" | custom-call | flops 201326592 | bytes 4194304 | tf_op jit(solution)/shard_map/pallas_call | solution.py:321
  30.9 1.7 %shard_map.103 = (f32[1024,128]{1,0:T(8,128)S(1)}, f32[1024,128]{1,0:T(8,128)S(1)}) custom-call(f32[1024,128]{1,0:T(8,128)S(1)} %shard_map.95.refs_1_.refs_0_.own_ref, f32[1024,128]{1,0:T(8,128)S(1)} %collective-permute-done.4.below_ref, bf16[128,96]{1,0:T(8,128)(2,1)S(1)} %get-tuple-element.48.next_ref, bf16[32,256]{1,0:T(8,128)(2,1)S(1)} %get-tuple-element.49.border_ref, ...), custom_call_target="tpu_custom_call" | custom-call | flops 402653184 | bytes 4194304 | tf_op jit(solution)/shard_map/pallas_call | solution.py:321
  32.6 3.0 %collective-permute-start.8 = (f32[1024,128]{1,0:T(8,128)S(1)}, f32[1024,128]{1,0:T(8,128)S(1)}, u32[]{:S(2)}, u32[]{:S(2)}) collective-permute-start(f32[1024,128]{1,0:T(8,128)S(1)} %get-tuple-element.53.refs_1_), channel_id=1, source_target_pairs={{0,2},{2,4},{4,6},{6,8},{8,10},{10,12},{12,14},{14,16},{16,18},{18... | collective-permute-start | bytes 1572872 | tf_op jit(solution)/shard_map/ppermute | solution.py:23
  35.6 1.7 %shard_map.105 = (f32[1024,128]{1,0:T(8,128)S(1)}, f32[1024,128]{1,0:T(8,128)S(1)}) custom-call(f32[1024,128]{1,0:T(8,128)S(1)} %shard_map.97.refs_1_.own_ref, f32[1024,128]{1,0:T(8,128)S(1)} %collective-permute-done.6.below_ref, bf16[128,96]{1,0:T(8,128)(2,1)S(1)} %get-tuple-element.48.next_ref, bf16[32,256]{1,0:T(8,128)(2,1)S(1)} %get-tuple-element.49.border_ref, ...), custom_call_target="tpu_custom_call" | custom-call | flops 402653184 | bytes 4194304 | tf_op jit(solution)/shard_map/pallas_call | solution.py:321
  37.3 2.2 %collective-permute-start.9 = (f32[1024,128]{1,0:T(8,128)S(1)}, f32[1024,128]{1,0:T(8,128)S(1)}, u32[]{:S(2)}, u32[]{:S(2)}) collective-permute-start(f32[1024,128]{1,0:T(8,128)S(1)} %get-tuple-element.56.refs_2_.refs_1_), channel_id=1, source_target_pairs={{0,2},{2,4},{4,6},{6,8},{8,10},{10,12},{12,14},{14,16},{16,18},{18... | collective-permute-start | bytes 1572872 | tf_op jit(solution)/shard_map/ppermute | solution.py:23
  40.3 1.6 %collective-permute-start.7 = (f32[32,2048]{1,0:T(8,128)S(1)}, f32[32,2048]{1,0:T(8,128)S(1)}, u32[]{:S(2)}, u32[]{:S(2)}) collective-permute-start(f32[32,2048]{1,0:T(8,128)S(1)} %shard_map.106.own_ref), channel_id=1, source_target_pairs={{0,1},{1,0},{2,3},{3,2},{4,5},{5,4},{6,7},{7,6},{8,9},{9,8},{10,11... | collective-permute-start | bytes 786440 | tf_op jit(solution)/shard_map/ppermute | solution.py:28
  41.9 2.1 %collective-permute-done.8.refs_0_ = f32[1024,128]{1,0:T(8,128)S(1)} collective-permute-done((f32[1024,128]{1,0:T(8,128)S(1)}, f32[1024,128]{1,0:T(8,128)S(1)}, u32[]{:S(2)}, u32[]{:S(2)}) %collective-permute-start.8) | collective-permute-done | bytes 524320 | tf_op jit(solution)/shard_map/ppermute | solution.py:23
  44.9 4.7 %collective-permute-done.9.refs_0_ = f32[1024,128]{1,0:T(8,128)S(1)} collective-permute-done((f32[1024,128]{1,0:T(8,128)S(1)}, f32[1024,128]{1,0:T(8,128)S(1)}, u32[]{:S(2)}, u32[]{:S(2)}) %collective-permute-start.9) | collective-permute-done | bytes 524320 | tf_op jit(solution)/shard_map/ppermute | solution.py:23
  50.6 1.6 %collective-permute-start.10 = (f32[128,128]{1,0:T(8,128)S(1)}, f32[128,128]{1,0:T(8,128)S(1)}, u32[]{:S(2)}, u32[]{:S(2)}) collective-permute-start(f32[128,128]{1,0:T(8,128)S(1)} %get-tuple-element.63.refs_3_), channel_id=1, source_target_pairs={{0,1},{1,0},{2,3},{3,2},{4,5},{5,4},{6,7},{7,6},{8,9},{9,8},{10,11... | collective-permute-start | bytes 196616 | tf_op jit(solution)/shard_map/ppermute | solution.py:28
  52.2 1.8 %shard_map.107 = (f32[2048,128]{1,0:T(8,128)}, f32[2048,128]{1,0:T(8,128)}) custom-call(bf16[128,96]{1,0:T(8,128)(2,1)S(1)} %get-tuple-element.34.lhs_ref, f32[32,2048]{1,0:T(8,128)S(1)} %shard_map.106.own_ref, f32[32,2048]{1,0:T(8,128)S(1)} %collective-permute-done.7.other_ref, f32[32,128]{1,0:T(8,128)S(1)} %get-tuple-element.45.bounds_ref, ...), custom_call_target="tpu_custom_call" | custom-call | flops 50331648 | bytes 2097152 | tf_op jit(solution)/shard_map/pallas_call | solution.py:321
  54.9 3.6 %shard_map.110 = f32[8,128,16,128]{3,2,1,0:T(8,128)} custom-call(f32[8192,128]{1,0:T(8,128)S(1)} %get-tuple-element.60.refs_0_, f32[8192,128]{1,0:T(8,128)S(1)} %get-tuple-element.62.refs_1_, f32[128,128]{1,0:T(8,128)S(1)} %bitcast.21, f32[128,128]{1,0:T(8,128)S(1)} %get-tuple-element.63.refs_3_, f32[128,128]{1,0:T(8,128)S(1)} %collective-permute-done.10.refs_4_), custom_call_target="tpu_custom_call" | custom-call | flops 2097152 | bytes 16777216 | tf_op jit(solution)/shard_map/pallas_call | solution.py:321
  (30 shorter events, 7.4 us)
Async XLA Ops:
  0.6 8.3 %copy-start.6 = (s32[16]{0:T(128)S(1)}, s32[16]{0:T(128)}, u32[]{:S(2)}) copy-start(s32[16]{0:T(128)} %margin_ref.1) | copy-start | bytes 196
  0.6 8.3 %copy-start.5 = (f32[32]{0:T(128)S(1)}, f32[32]{0:T(128)}, u32[]{:S(2)}) copy-start(f32[32]{0:T(128)} %bounds_ref.1) | copy-start | bytes 388
  0.7 8.3 %copy-start.3 = (f32[1,128,32]{1,2,0:T(8,128)S(1)}, f32[1,128,32]{1,2,0:T(8,128)}, u32[]{:S(2)}) copy-start(f32[1,128,32]{1,2,0:T(8,128)} %param.11) | copy-start | bytes 49156
  0.7 8.3 %copy-start.4 = (f32[8,16]{1,0:T(8,128)S(1)}, f32[8,16]{1,0:T(8,128)}, u32[]{:S(2)}) copy-start(f32[8,16]{1,0:T(8,128)} %filters_ref.1) | copy-start | bytes 1540
  2.0 24.6 %copy-start.2 = (f32[8,16,128]{2,1,0:T(8,128)S(1)}, f32[8,16,128]{2,1,0:T(8,128)}, u32[]{:S(2)}) copy-start(f32[8,16,128]{2,1,0:T(8,128)} %param.9) | copy-start | bytes 196612
  2.0 26.7 %copy-start = (f32[128,16,128]{2,1,0:T(8,128)S(1)}, f32[128,16,128]{2,1,0:T(8,128)}, u32[]{:S(2)}) copy-start(f32[128,16,128]{2,1,0:T(8,128)} %param.7) | copy-start | bytes 3145732
  2.0 26.7 %copy-start.1 = (f32[128,16,128]{2,1,0:T(8,128)S(1)}, f32[128,16,128]{2,1,0:T(8,128)}, u32[]{:S(2)}) copy-start(f32[128,16,128]{2,1,0:T(8,128)} %param.8) | copy-start | bytes 3145732
  2.1 11.5 %collective-permute-start = (f32[1024,128]{1,0:T(8,128)S(1)}, f32[1024,128]{1,0:T(8,128)S(1)}, u32[]{:S(2)}, u32[]{:S(2)}) collective-permute-start(f32[1024,128]{1,0:T(8,128)S(1)} %shard_map.95.refs_1_.refs_0_.own_ref), channel_id=1, source_target_pairs={{0,2},{2,4},{4,6},{6,8},{8,10},{10,12},{12,14},{14,16},{16,18},{18... | collective-permute-start | bytes 1572872 | tf_op jit(solution)/shard_map/ppermute | solution.py:23
  5.5 13.8 %collective-permute-start.1 = (f32[1024,128]{1,0:T(8,128)S(1)}, f32[1024,128]{1,0:T(8,128)S(1)}, u32[]{:S(2)}, u32[]{:S(2)}) collective-permute-start(f32[1024,128]{1,0:T(8,128)S(1)} %shard_map.97.refs_1_.own_ref), channel_id=1, source_target_pairs={{0,2},{2,4},{4,6},{6,8},{8,10},{10,12},{12,14},{14,16},{16,18},{18... | collective-permute-start | bytes 1572872 | tf_op jit(solution)/shard_map/ppermute | solution.py:23
  10.4 8.9 %collective-permute-start.3 = (f32[32,2048]{1,0:T(8,128)S(1)}, f32[32,2048]{1,0:T(8,128)S(1)}, u32[]{:S(2)}, u32[]{:S(2)}) collective-permute-start(f32[32,2048]{1,0:T(8,128)S(1)} %shard_map.99.own_ref), channel_id=1, source_target_pairs={{0,1},{1,0},{2,3},{3,2},{4,5},{5,4},{6,7},{7,6},{8,9},{9,8},{10,11... | collective-permute-start | bytes 786440 | tf_op jit(solution)/shard_map/ppermute | solution.py:28
  14.5 16.5 %collective-permute-start.4 = (f32[1024,128]{1,0:T(8,128)S(1)}, f32[1024,128]{1,0:T(8,128)S(1)}, u32[]{:S(2)}, u32[]{:S(2)}) collective-permute-start(f32[1024,128]{1,0:T(8,128)S(1)} %shard_map.95.refs_1_.refs_0_.own_ref), channel_id=1, source_target_pairs={{2,0},{4,2},{6,4},{8,6},{10,8},{12,10},{14,12},{16,14},{18,16},{20... | collective-permute-start | bytes 1572872 | tf_op jit(solution)/shard_map/ppermute | solution.py:23
  19.3 16.3 %collective-permute-start.6 = (f32[1024,128]{1,0:T(8,128)S(1)}, f32[1024,128]{1,0:T(8,128)S(1)}, u32[]{:S(2)}, u32[]{:S(2)}) collective-permute-start(f32[1024,128]{1,0:T(8,128)S(1)} %shard_map.97.refs_1_.own_ref), channel_id=1, source_target_pairs={{2,0},{4,2},{6,4},{8,6},{10,8},{12,10},{14,12},{16,14},{18,16},{20... | collective-permute-start | bytes 1572872 | tf_op jit(solution)/shard_map/ppermute | solution.py:23
  22.1 4.6 %collective-permute-start.2 = (f32[128,128]{1,0:T(8,128)S(1)}, f32[128,128]{1,0:T(8,128)S(1)}, u32[]{:S(2)}, u32[]{:S(2)}) collective-permute-start(f32[128,128]{1,0:T(8,128)S(1)} %get-tuple-element.40.own_ref), channel_id=1, source_target_pairs={{0,1},{1,0},{2,3},{3,2},{4,5},{5,4},{6,7},{7,6},{8,9},{9,8},{10,11... | collective-permute-start | bytes 196616 | tf_op jit(solution)/shard_map/ppermute | solution.py:28
  26.7 4.2 %collective-permute-start.5 = (f32[128,128]{1,0:T(8,128)S(1)}, f32[128,128]{1,0:T(8,128)S(1)}, u32[]{:S(2)}, u32[]{:S(2)}) collective-permute-start(f32[128,128]{1,0:T(8,128)S(1)} %shard_map.101.scale_ref.refs_5_), channel_id=1, source_target_pairs={{2,0},{4,2},{6,4},{8,6},{10,8},{12,10},{14,12},{16,14},{18,16},{20... | collective-permute-start | bytes 196616 | tf_op jit(solution)/shard_map/ppermute | solution.py:23
  32.6 11.4 %collective-permute-start.8 = (f32[1024,128]{1,0:T(8,128)S(1)}, f32[1024,128]{1,0:T(8,128)S(1)}, u32[]{:S(2)}, u32[]{:S(2)}) collective-permute-start(f32[1024,128]{1,0:T(8,128)S(1)} %get-tuple-element.53.refs_1_), channel_id=1, source_target_pairs={{0,2},{2,4},{4,6},{6,8},{8,10},{10,12},{12,14},{14,16},{16,18},{18... | collective-permute-start | bytes 1572872 | tf_op jit(solution)/shard_map/ppermute | solution.py:23
  37.3 12.4 %collective-permute-start.9 = (f32[1024,128]{1,0:T(8,128)S(1)}, f32[1024,128]{1,0:T(8,128)S(1)}, u32[]{:S(2)}, u32[]{:S(2)}) collective-permute-start(f32[1024,128]{1,0:T(8,128)S(1)} %get-tuple-element.56.refs_2_.refs_1_), channel_id=1, source_target_pairs={{0,2},{2,4},{4,6},{6,8},{8,10},{10,12},{12,14},{14,16},{16,18},{18... | collective-permute-start | bytes 1572872 | tf_op jit(solution)/shard_map/ppermute | solution.py:23
  40.3 11.8 %collective-permute-start.7 = (f32[32,2048]{1,0:T(8,128)S(1)}, f32[32,2048]{1,0:T(8,128)S(1)}, u32[]{:S(2)}, u32[]{:S(2)}) collective-permute-start(f32[32,2048]{1,0:T(8,128)S(1)} %shard_map.106.own_ref), channel_id=1, source_target_pairs={{0,1},{1,0},{2,3},{3,2},{4,5},{5,4},{6,7},{7,6},{8,9},{9,8},{10,11... | collective-permute-start | bytes 786440 | tf_op jit(solution)/shard_map/ppermute | solution.py:28
  50.6 4.3 %collective-permute-start.10 = (f32[128,128]{1,0:T(8,128)S(1)}, f32[128,128]{1,0:T(8,128)S(1)}, u32[]{:S(2)}, u32[]{:S(2)}) collective-permute-start(f32[128,128]{1,0:T(8,128)S(1)} %get-tuple-element.63.refs_3_), channel_id=1, source_target_pairs={{0,1},{1,0},{2,3},{3,2},{4,5},{5,4},{6,7},{7,6},{8,9},{9,8},{10,11... | collective-permute-start | bytes 196616 | tf_op jit(solution)/shard_map/ppermute | solution.py:28

commit v5 on v4

--- a/solution.py
+++ b/solution.py
@@ -13,6 +13,7 @@
 BF16 = jnp.bfloat16
 CHUNKS = 2
 GROUP = 32
+PAD = 8
 VMEM_LIMIT = 24 << 20
 REFLECT_LIMIT = 56000000
 
@@ -85,25 +86,40 @@
     last = margin_ref.shape[0] - 1
     own_margin = margin_ref[facet]
     next_margin = jnp.where(facet < last, margin_ref[jnp.minimum(facet + 1, last)], 0)
-    source = lax.broadcasted_iota(jnp.int32, (2 * height, size), 0)
-    target = lax.broadcasted_iota(jnp.int32, (2 * height, size), 1)
-    tap_of = lax.rem(target, height) - source + height
-    basis_of = lax.div(target, height)
-    matrix = jnp.zeros((2 * height, size), F32)
-    for tap in range(taps):
-        values = jnp.zeros((2 * height, size), F32)
-        for basis in range(bases):
-            if tap < 2 * (basis + 1):
+
+    def toeplitz(columns, column, tap_of):
+        basis_of, _ = column(lax.broadcasted_iota(jnp.int32, (1, columns), 1))
+        matrix = jnp.zeros((2 * height, columns), F32)
+        for tap in range(taps):
+            values = jnp.zeros((1, columns), F32)
+            for basis in range(tap // 2, bases):
                 values = jnp.where(basis_of == basis, filters_ref[basis, tap], values)
-        matrix = jnp.where(tap_of == tap, values, matrix)
-
-    def masked(margin):
-        return jnp.where((source >= height) | (height - source <= margin), matrix, 0.0)
-
-    below = masked(next_margin)
-    lift_ref[...] = three_lhs(DUAL * masked(own_margin).T)
+            matrix = jnp.where(tap_of == tap, values, matrix)
+        return matrix
+
+    def grids(columns, column):
+        source = lax.broadcasted_iota(jnp.int32, (2 * height, columns), 0)
+        return source, column(lax.broadcasted_iota(jnp.int32, (2 * height, columns), 1))[1]
+
+    def dense(index):
+        return lax.div(index, height), lax.rem(index, height)
+
+    def reaching(index):
+        basis = jnp.zeros_like(index)
+        for number in range(1, bases):
+            basis = basis + (index >= number * number).astype(jnp.int32)
+        return basis, index - basis * basis
+
+    source, target = grids(size, dense)
+    borrowed = jnp.where((source < height - 1) & (height - 1 - source <= own_margin), target - source + height - 1, -1)
+    own = toeplitz(size, dense, jnp.where(source >= height, target - source + height, borrowed))
+    source, target = grids(bases * bases, reaching)
+    tap_of = target - source + height
+    below = toeplitz(bases * bases, reaching, jnp.where((source >= height) | (height - source <= next_margin), tap_of, -1))
+
+    lift_ref[...] = three_lhs(DUAL * own.T)
     next_ref[...] = three_lhs(DUAL * below.T)
-    interior_ref[...] = two_lhs(matrix[height:])
+    interior_ref[...] = two_lhs(own[height:])
     border_ref[...] = two_lhs(below[:height])
     loading = loading_ref[...]
     coef_ref[...] = two_lhs(loading)
@@ -115,7 +131,17 @@
     limits_ref[...] = limits
 
 
-def reflect_kernel(start, x_ref, d_ref, r_ref, x_buffer, d_buffer, sems):
+def pack(source_ref, target_ref, height, first, start=0):
+    reach = height - 1
+    for channel in range(source_ref.shape[0] // height):
+        target_ref[pl.ds(start + channel * reach, reach), :] = source_ref[pl.ds(channel * height + first, reach), :]
+
+
+def clear_tail(packed_ref):
+    packed_ref[pl.ds(packed_ref.shape[0] - PAD, PAD), :] = jnp.zeros((PAD, packed_ref.shape[1]), F32)
+
+
+def reflect_kernel(height, start, x_ref, d_ref, r_ref, packed_ref, x_buffer, d_buffer, sems):
     rows = pl.ds(start, r_ref.shape[0])
     copies = [
         pltpu.make_async_copy(source.at[rows], target, sems.at[turn])
@@ -128,12 +154,20 @@
     x = x_buffer[...]
     updated = jnp.maximum(x - PRIMAL * (x - d_buffer[...]), 0.0)
     r_ref[...] = 2.0 * updated - x
+    pack(r_ref, packed_ref, height, 1)
+    clear_tail(packed_ref)
 
 
 def coef_kernel(height, spectral, lhs_ref, *refs):
-    *r_refs, out_ref = refs
     if spectral:
-        s_ref, *r_refs = r_refs
+        s_ref, *r_refs, out_ref = refs
+    else:
+        *r_refs, out_ref, packed_ref = refs
+        start = 0
+        for r_ref in r_refs:
+            pack(r_ref, packed_ref, height, 0, start)
+            start += r_ref.shape[0] // height * (height - 1)
+        clear_tail(packed_ref)
     rank = out_ref.shape[0]
 
     def pixels(row):
@@ -170,14 +204,12 @@
         out_ref[pl.ds(row + 1, channels, stride=height), :] = both[:, lanes:]
 
 
-def scale_kernel(weights_ref, own_ref, other_ref, scale_ref):
+def scale_kernel(height, weights_ref, own_ref, other_ref, scale_ref, above_ref):
     weights = weights_ref[...]
     scale_ref[...] = weights / jnp.maximum(jnp.sqrt(own_ref[...] + other_ref[...]), weights)
-
-
-def extended(halo_ref, own_ref, height, channel):
-    rows = pl.ds(pl.multiple_of(channel * height, height), height)
-    return jnp.concatenate([halo_ref[rows, :], own_ref[rows, :]], axis=0)
+    for basis in range(weights.shape[0] // height):
+        count = 2 * basis + 1
+        above_ref[pl.ds(basis * basis, count), :] = scale_ref[pl.ds(basis * height, count), :]
 
 
 def lift_kernel(height, kind, *refs):
@@ -189,26 +221,30 @@
     lhs = lhs_ref[...]
     size = lhs.shape[0]
     lanes = own_ref.shape[1]
-    channels = own_ref.shape[0] // height
-    many = min(GROUP, channels)
-
-    def step(group, total):
-        for pair in range(0, many, 2):
-            channel = group * many + pair
-            value = jnp.concatenate(
-                [extended(halo_ref, own_ref, height, channel), extended(halo_ref, own_ref, height, channel + 1)], axis=1
-            )
-            both = dot(lhs, three_rhs(value))
-            for half in range(2):
-                rows = pl.ds(pl.multiple_of((channel + half) * size, size), size)
-                lifted = both[:, half * lanes : (half + 1) * lanes]
-                if kind == "second":
-                    lifted = lifted + dual_ref[rows, :] * scale
-                out_ref[rows, :] = lifted
-                total = total + lifted * lifted
-        return total
-
-    squares_ref[...] = lax.fori_loop(0, channels // many, step, before_ref[...])
+    total = before_ref[...]
+    for pair in range(0, own_ref.shape[0] // height, 2):
+        value = jnp.concatenate(
+            [
+                jnp.concatenate(
+                    [
+                        halo_ref[pl.ds(channel * (height - 1), height), :],
+                        own_ref[pl.ds(channel * height, height), :],
+                    ],
+                    axis=0,
+                )
+                for channel in (pair, pair + 1)
+            ],
+            axis=1,
+        )
+        both = dot(lhs, three_rhs(value))
+        for half in range(2):
+            rows = pl.ds((pair + half) * size, size)
+            lifted = both[:, half * lanes : (half + 1) * lanes]
+            if kind == "second":
+                lifted = lifted + dual_ref[rows, :] * scale
+            out_ref[rows, :] = lifted
+            total = total + lifted * lifted
+    squares_ref[...] = total
 
 
 def adjoint_kernel(height, start, dual_ref, lhs_ref, scale_ref, s_ref, x_ref, d_ref, partial_ref):
@@ -239,41 +275,42 @@
 
 
 def border_kernel(
-    height, start, own_ref, below_ref, next_ref, border_ref, scale_ref, partial_ref, x_ref, d_ref, updated_ref, reflected_ref
+    height, start, own_ref, below_ref, next_ref, border_ref, scale_ref, partial_ref, x_ref, d_ref,
+    updated_ref, reflected_ref, packed_ref,
 ):
-    size, lanes = scale_ref.shape
-    channels = partial_ref.shape[0] // height
+    lanes = scale_ref.shape[1]
     scale = jnp.concatenate([scale_ref[...]] * 2, axis=1)
     lift_lhs = next_ref[...]
     border_lhs = border_ref[...]
-    many = min(GROUP, channels)
-
-    def step(group, carry):
-        for pair in range(0, many, 2):
-            channel = group * many + pair
-            spans = [
-                (
-                    pl.ds(pl.multiple_of((channel + half) * height, height), height),
-                    pl.ds(pl.multiple_of(start + (channel + half) * height, height), height),
+    for pair in range(0, partial_ref.shape[0] // height, 2):
+        channels = (pair, pair + 1)
+        value = jnp.concatenate(
+            [
+                jnp.concatenate(
+                    [
+                        own_ref[pl.ds(channel * height, height), :],
+                        below_ref[pl.ds((start + channel) * (height - 1), height), :],
+                    ],
+                    axis=0,
                 )
-                for half in range(2)
-            ]
-            value = jnp.concatenate(
-                [jnp.concatenate([own_ref[rows, :], below_ref[rows, :]], axis=0) for rows, cube in spans], axis=1
-            )
-            duals = dot(lift_lhs, three_rhs(value)) * scale
-            both = dot(border_lhs, two_rhs(duals))
-            spread = both[:height] + both[height:]
-            for half, (rows, cube) in enumerate(spans):
-                x, d = x_ref[cube, :], d_ref[cube, :]
-                before = jnp.maximum(x - PRIMAL * (x - d), 0.0)
-                mine = spread[:, half * lanes : (half + 1) * lanes]
-                updated = jnp.maximum(partial_ref[rows, :] - PRIMAL * mine, 0.0)
-                updated_ref[rows, :] = updated
-                reflected_ref[rows, :] = 2.0 * updated - before
-        return carry
-
-    lax.fori_loop(0, channels // many, step, 0)
+                for channel in channels
+            ],
+            axis=1,
+        )
+        duals = dot(lift_lhs, three_rhs(value)) * scale
+        both = dot(border_lhs, two_rhs(duals))
+        spread = both[:height] + both[height:]
+        for half, channel in enumerate(channels):
+            rows = pl.ds(channel * height, height)
+            cube = pl.ds((start + channel) * height, height)
+            x, d = x_ref[cube, :], d_ref[cube, :]
+            before = jnp.maximum(x - PRIMAL * (x - d), 0.0)
+            mine = spread[:, half * lanes : (half + 1) * lanes]
+            updated = jnp.maximum(partial_ref[rows, :] - PRIMAL * mine, 0.0)
+            updated_ref[rows, :] = updated
+            reflected_ref[rows, :] = 2.0 * updated - before
+    pack(reflected_ref, packed_ref, height, 1)
+    clear_tail(packed_ref)
 
 
 def wavelet_kernel(chunks, height, *refs):
@@ -335,6 +372,7 @@
     rank = bounds.shape[0]
     assert taps == height
     size = bases * height
+    reaching = bases * bases
     chunks = CHUNKS if channels >= 8 * CHUNKS else 1
     per = channels // chunks
     block = per * height
@@ -354,22 +392,24 @@
     scalars = pl.BlockSpec(memory_space=pltpu.SMEM)
     work = 6 * 2 * height * per * size * lanes
 
-    reflected = []
+    packed = per * (height - 1) + PAD
+    reflected, halos = [], []
     for index in range(chunks):
-        reflected.append(call(
-            functools.partial(reflect_kernel, index * block), flat(block), [distant] * 2, (x, d),
+        r, ahead = call(
+            functools.partial(reflect_kernel, height, index * block), [flat(block), flat(packed)], [distant] * 2, (x, d),
             4 * block * lanes, 12 * block * lanes,
             scratch=[pltpu.VMEM((block, lanes), F32)] * 2 + [pltpu.SemaphoreType.DMA((2,))], limit=REFLECT_LIMIT,
-        ))
-    halos = [shift(r, "facet", 1) for r in reflected]
+        )
+        reflected.append(r)
+        halos.append(shift(ahead, "facet", 1))
 
     lift_lhs, next_lhs, interior_lhs, border_lhs, coef_lhs, spectral_lhs, limits = call(
         setup_kernel,
         [
             jax.ShapeDtypeStruct((size, 6 * height), BF16),
-            jax.ShapeDtypeStruct((size, 6 * height), BF16),
+            jax.ShapeDtypeStruct((reaching, 6 * height), BF16),
             jax.ShapeDtypeStruct((2 * height, 2 * size), BF16),
-            jax.ShapeDtypeStruct((2 * height, 2 * size), BF16),
+            jax.ShapeDtypeStruct((2 * height, 2 * reaching), BF16),
             jax.ShapeDtypeStruct((2 * rank, 2 * channels), BF16),
             jax.ShapeDtypeStruct((channels, 3 * rank), BF16),
             flat(rank),
@@ -379,7 +419,7 @@
 
     def coefficients(parts, spectral):
         operands = (coef_lhs,) + ((spectral,) if spectral is not None else ()) + tuple(parts)
-        outs = jax.ShapeDtypeStruct((rank, height * lanes), F32)
+        outs = [jax.ShapeDtypeStruct((rank, height * lanes), F32)] + [flat(channels * (height - 1) + PAD)] * (spectral is None)
         return call(
             functools.partial(coef_kernel, height, spectral is not None), outs,
             [whole()] * len(operands), operands, 6 * rank * rows * lanes, 2 * cubes,
@@ -392,49 +432,46 @@
             (spectral_lhs, own, other, limits, *image), 6 * rank * rows * lanes, 2 * cubes,
         )
 
-    coefs = coefficients(reflected, None)
+    coefs, everything = coefficients(reflected, None)
     terms = chan_terms(coefs)
     squares = jnp.zeros((size, lanes), F32)
-    lifted, below = [], []
+    lifted = []
     for index in range(chunks):
         out, squares = call(
             functools.partial(lift_kernel, height, "first"), [flat(per * size), flat(size)], [whole()] * 4,
             (halos[index], reflected[index], lift_lhs, squares), work, duals,
         )
         lifted.append(out)
-        if index < chunks - 1:
-            tied, _, _ = lax.optimization_barrier((reflected[index], squares, coefs))
-            below.append(shift(tied, "facet", -1))
-            squares, halos[index + 1] = lax.optimization_barrier((squares, halos[index + 1]))
-        elif index:
-            tied, _, *terms = lax.optimization_barrier((reflected[index], halos[index], *terms))
-            below.append(shift(tied, "facet", -1))
-        else:
-            below.append(shift(reflected[index], "facet", -1))
+        if index == 0:
+            tied, _ = lax.optimization_barrier((everything, squares))
+            below = shift(tied, "facet", -1)
+            squares, *terms = lax.optimization_barrier((squares, *terms))
     own, other = chan_terms(squares)
-    *terms, _ = lax.optimization_barrier((*terms, squares))
     (spectral,) = synthesis(*terms)
     other, spectral = lax.optimization_barrier((other, spectral))
-    scale = call(scale_kernel, flat(size), [whole()] * 3, (w, own, other), 10 * size * lanes, 16 * size * lanes)
-    scale_below = shift(scale, "facet", -1)
+    scale, scale_above = call(
+        functools.partial(scale_kernel, height), [flat(size), flat(reaching)], [whole()] * 3, (w, own, other),
+        10 * size * lanes, 16 * size * lanes,
+    )
+    scale_below = shift(scale_above, "facet", -1)
 
     partials = [
         call(
             functools.partial(adjoint_kernel, height, index * block), flat(block), [whole()] * 6,
-            (lifted[index], interior_lhs, scale, spectral, x, d), work, duals,
+            (lifted[index], interior_lhs, scale, spectral, x, d), 22 * work, 22 * duals,
         )
         for index in range(chunks)
     ]
     image, halos, again = [], [], []
     for index in range(chunks):
-        updated, r = call(
-            functools.partial(border_kernel, height, index * block), [flat(block)] * 2, [whole()] * 8,
-            (reflected[index], below[index], next_lhs, border_lhs, scale_below, partials[index], x, d), 2 * work, duals,
+        updated, r, ahead = call(
+            functools.partial(border_kernel, height, index * per), [flat(block)] * 2 + [flat(packed)], [whole()] * 8,
+            (reflected[index], below, next_lhs, border_lhs, scale_below, partials[index], x, d), 22 * work, 22 * duals,
         )
         image.append(updated)
         again.append(r)
-        halos.append(shift(r, "facet", 1))
-    terms = chan_terms(coefficients(again, spectral))
+        halos.append(shift(ahead, "facet", 1))
+    terms = chan_terms(*coefficients(again, spectral))
 
     squares = jnp.zeros((size, lanes), F32)
     final = []

time: 58.8 us -> 59.7 us (1.015)
  local copies, waits for them, and re-layouts: 0.04 us -> 3.17 us
  waiting for transfers between devices: 14.8 us -> 13.1 us
  starting transfers between devices: 22.9 us -> 22 us
    ppermute x7 -> x6, waiting for transfers between devices: 11.3 us -> 6.57 us  [shift(): lax.ppermute(value, axis, [(source, source + steps) for source in range(i...]
    unnamed x14 -> x24, local copies, waits for them, and re-layouts: 0.04 us -> 3.16 us
    ppermute x4, waiting for transfers between devices: 3.48 us -> 6.54 us  [chan_pairs(): lax.ppermute(value, 'chan', [(source, source ^ stride) for source in rang...]
    ppermute x7 -> x6, starting transfers between devices: 16.6 us -> 15.6 us  [shift(): lax.ppermute(value, axis, [(source, source + steps) for source in range(i...]
  transfers between devices with their start and end apart: 11 -> 10, of which waited for: 6 -> 5; matrix products, arithmetic and copies ran while one was open for 0% -> 0% of each run, Pallas kernels for 26% -> 23%
where the time goes in v5:
time: 59.7 us; the launch traced here: 59.3 us
  starting transfers between devices  22 us (37%)
  Pallas kernels  20.2 us (34%)
  waiting for transfers between devices  13.1 us (22%)
  local copies, waits for them, and re-layouts  3.17 us (5%)
  between operations  0.9 us (2%)
    pallas_call x17, Pallas kernels, call(): pl.pallas_call(kernel, out_shape=outs, in_specs=ins, out_specs=out_specs...  20.2 us
    ppermute x6, starting transfers between devices, shift(): lax.ppermute(value, axis, [(source, source + steps) for source in range(i...  15.6 us
    ppermute x6, waiting for transfers between devices, shift(): lax.ppermute(value, axis, [(source, source + steps) for source in range(i...  6.57 us
    ppermute x4, waiting for transfers between devices, chan_pairs(): lax.ppermute(value, 'chan', [(source, source ^ stride) for source in rang...  6.54 us
    ppermute x4, starting transfers between devices, chan_pairs(): lax.ppermute(value, 'chan', [(source, source ^ stride) for source in rang...  6.33 us
    unnamed x24, local copies, waits for them, and re-layouts  3.16 us
  transfers between devices with their start and end apart: 10, of which 5 were waited for; matrix products, arithmetic and copies ran while one was open for 0% of the time, Pallas kernels for 23%

profile of v5, /device:TPU:16, one launch (start us, length us, event | category | flops | bytes accessed | tf_op | source)
XLA Modules:
  0.0 59.3 jit_solution(10352460765822177275)
XLA Ops:
  0.7 2.3 %shard_map.96 = (f32[1024,128]{1,0:T(8,128)}, f32[968,128]{1,0:T(8,128)S(1)}) custom-call(f32[2048,128]{1,0:T(8,128)} %bitcast.8, f32[2048,128]{1,0:T(8,128)} %bitcast.14), custom_call_target="tpu_custom_call" | custom-call | flops 524288 | bytes 1572864 | tf_op jit(solution)/shard_map/pallas_call | solution.py:358
  3.0 2.1 %collective-permute-start.1 = (f32[968,128]{1,0:T(8,128)S(1)}, f32[968,128]{1,0:T(8,128)S(1)}, u32[]{:S(2)}, u32[]{:S(2)}) collective-permute-start(f32[968,128]{1,0:T(8,128)S(1)} %get-tuple-element.45), channel_id=1, source_target_pairs={{0,2},{2,4},{4,6},{6,8},{8,10},{10,12},{12,14},{14,16},{16,18},{18... | collective-permute-start | bytes 1486856 | tf_op jit(solution)/shard_map/ppermute | solution.py:24
  5.1 2.2 %shard_map.95 = (f32[1024,128]{1,0:T(8,128)}, f32[968,128]{1,0:T(8,128)S(1)}) custom-call(f32[2048,128]{1,0:T(8,128)} %bitcast.9, f32[2048,128]{1,0:T(8,128)} %bitcast.15), custom_call_target="tpu_custom_call" | custom-call | flops 524288 | bytes 1572864 | tf_op jit(solution)/shard_map/pallas_call | solution.py:358
  7.3 3.5 %collective-permute-start = (f32[968,128]{1,0:T(8,128)S(1)}, f32[968,128]{1,0:T(8,128)S(1)}, u32[]{:S(2)}, u32[]{:S(2)}) collective-permute-start(f32[968,128]{1,0:T(8,128)S(1)} %get-tuple-element.42), channel_id=1, source_target_pairs={{0,2},{2,4},{4,6},{6,8},{8,10},{10,12},{12,14},{14,16},{16,18},{18... | collective-permute-start | bytes 1486856 | tf_op jit(solution)/shard_map/ppermute | solution.py:24
  11.8 1.0 %copy-done.2 = f32[1024,128]{1,0:T(8,128)S(1)} copy-done((f32[1024,128]{1,0:T(8,128)S(1)}, f32[1024,128]{1,0:T(8,128)}, u32[]{:S(2)}) %copy-start.2) | copy-done | bytes 524312
  12.8 1.0 %copy-done.5 = f32[1024,128]{1,0:T(8,128)S(1)} copy-done((f32[1024,128]{1,0:T(8,128)S(1)}, f32[1024,128]{1,0:T(8,128)}, u32[]{:S(2)}) %copy-start.5) | copy-done | bytes 524312
  14.5 1.6 %collective-permute-start.2 = (f32[32,2048]{1,0:T(8,128)S(1)}, f32[32,2048]{1,0:T(8,128)S(1)}, u32[]{:S(2)}, u32[]{:S(2)}) collective-permute-start(f32[32,2048]{1,0:T(8,128)S(1)} %get-tuple-element.51.own_ref), channel_id=1, source_target_pairs={{0,1},{1,0},{2,3},{3,2},{4,5},{5,4},{6,7},{7,6},{8,9},{9,8},{10,11... | collective-permute-start | bytes 786440 | tf_op jit(solution)/shard_map/ppermute | solution.py:29
  16.8 2.7 %collective-permute-start.4 = (f32[1928,128]{1,0:T(8,128)S(1)}, f32[1928,128]{1,0:T(8,128)S(1)}, u32[]{:S(2)}, u32[]{:S(2)}) collective-permute-start(f32[1928,128]{1,0:T(8,128)S(1)} %get-tuple-element.56), channel_id=1, source_target_pairs={{2,0},{4,2},{6,4},{8,6},{10,8},{12,10},{14,12},{16,14},{18,16},{20... | collective-permute-start | bytes 2961416 | tf_op jit(solution)/shard_map/ppermute | solution.py:24
  19.5 3.3 %collective-permute-done.2.other_ref = f32[32,2048]{1,0:T(8,128)S(1)} collective-permute-done((f32[32,2048]{1,0:T(8,128)S(1)}, f32[32,2048]{1,0:T(8,128)S(1)}, u32[]{:S(2)}, u32[]{:S(2)}) %collective-permute-start.2) | collective-permute-done | bytes 262176 | tf_op jit(solution)/shard_map/ppermute | solution.py:29
  22.8 1.0 %copy-done.3 = f32[1024,128]{1,0:T(8,128)S(1)} copy-done((f32[1024,128]{1,0:T(8,128)S(1)}, f32[1024,128]{1,0:T(8,128)}, u32[]{:S(2)}) %copy-start.3) | copy-done | bytes 524312
  24.5 1.6 %collective-permute-start.3 = (f32[128,128]{1,0:T(8,128)S(1)}, f32[128,128]{1,0:T(8,128)S(1)}, u32[]{:S(2)}, u32[]{:S(2)}) collective-permute-start(f32[128,128]{1,0:T(8,128)S(1)} %get-tuple-element.50.own_ref), channel_id=1, source_target_pairs={{0,1},{1,0},{2,3},{3,2},{4,5},{5,4},{6,7},{7,6},{8,9},{9,8},{10,11... | collective-permute-start | bytes 196616 | tf_op jit(solution)/shard_map/ppermute | solution.py:29
  26.6 2.3 %collective-permute-done.3.other_ref = f32[128,128]{1,0:T(8,128)S(1)} collective-permute-done((f32[128,128]{1,0:T(8,128)S(1)}, f32[128,128]{1,0:T(8,128)S(1)}, u32[]{:S(2)}, u32[]{:S(2)}) %collective-permute-start.3) | collective-permute-done | bytes 65568 | tf_op jit(solution)/shard_map/ppermute | solution.py:29
  28.9 1.9 %collective-permute-start.5 = (f32[64,128]{1,0:T(8,128)S(1)}, f32[64,128]{1,0:T(8,128)S(1)}, u32[]{:S(2)}, u32[]{:S(2)}) collective-permute-start(f32[64,128]{1,0:T(8,128)S(1)} %get-tuple-element.60), channel_id=1, source_target_pairs={{2,0},{4,2},{6,4},{8,6},{10,8},{12,10},{14,12},{16,14},{18,16},{20... | collective-permute-start | bytes 98312 | tf_op jit(solution)/shard_map/ppermute | solution.py:24
  30.8 1.1 %shard_map.104.partial_ref = f32[1024,128]{1,0:T(8,128)S(1)} custom-call(f32[8192,128]{1,0:T(8,128)S(1)} %get-tuple-element.65.dual_ref.refs_4_, bf16[32,256]{1,0:T(8,128)(2,1)S(1)} %get-tuple-element.62.lhs_ref, f32[128,128]{1,0:T(8,128)S(1)} %get-tuple-element.63.scale_ref.refs_5_, f32[2048,128]{1,0:T(8,128)S(1)} %shard_map.100.s_ref.refs_0_, ...), custom_call_target="tpu_custom_call" | custom-call | flops 4429185024 | bytes 92274688 | tf_op jit(solution)/shard_map/pallas_call | solution.py:358
  32.0 1.1 %shard_map.102.partial_ref = f32[1024,128]{1,0:T(8,128)S(1)} custom-call(f32[8192,128]{1,0:T(8,128)S(1)} %get-tuple-element.61.dual_ref.refs_4_, bf16[32,256]{1,0:T(8,128)(2,1)S(1)} %get-tuple-element.62.lhs_ref, f32[128,128]{1,0:T(8,128)S(1)} %get-tuple-element.63.scale_ref.refs_5_, f32[2048,128]{1,0:T(8,128)S(1)} %shard_map.100.s_ref.refs_0_, ...), custom_call_target="tpu_custom_call" | custom-call | flops 4429185024 | bytes 92274688 | tf_op jit(solution)/shard_map/pallas_call | solution.py:358
  34.1 2.8 %collective-permute-start.7 = (f32[968,128]{1,0:T(8,128)S(1)}, f32[968,128]{1,0:T(8,128)S(1)}, u32[]{:S(2)}, u32[]{:S(2)}) collective-permute-start(f32[968,128]{1,0:T(8,128)S(1)} %get-tuple-element.70), channel_id=1, source_target_pairs={{0,2},{2,4},{4,6},{6,8},{8,10},{10,12},{12,14},{14,16},{16,18},{18... | collective-permute-start | bytes 1486856 | tf_op jit(solution)/shard_map/ppermute | solution.py:24
  37.8 2.6 %collective-permute-start.8 = (f32[968,128]{1,0:T(8,128)S(1)}, f32[968,128]{1,0:T(8,128)S(1)}, u32[]{:S(2)}, u32[]{:S(2)}) collective-permute-start(f32[968,128]{1,0:T(8,128)S(1)} %get-tuple-element.72), channel_id=1, source_target_pairs={{0,2},{2,4},{4,6},{6,8},{8,10},{10,12},{12,14},{14,16},{16,18},{18... | collective-permute-start | bytes 1486856 | tf_op jit(solution)/shard_map/ppermute | solution.py:24
  41.4 1.6 %collective-permute-start.6 = (f32[32,2048]{1,0:T(8,128)S(1)}, f32[32,2048]{1,0:T(8,128)S(1)}, u32[]{:S(2)}, u32[]{:S(2)}) collective-permute-start(f32[32,2048]{1,0:T(8,128)S(1)} %shard_map.106.own_ref), channel_id=1, source_target_pairs={{0,1},{1,0},{2,3},{3,2},{4,5},{5,4},{6,7},{7,6},{8,9},{9,8},{10,11... | collective-permute-start | bytes 786440 | tf_op jit(solution)/shard_map/ppermute | solution.py:29
  43.0 2.2 %collective-permute-done.7.refs_0_ = f32[968,128]{1,0:T(8,128)S(1)} collective-permute-done((f32[968,128]{1,0:T(8,128)S(1)}, f32[968,128]{1,0:T(8,128)S(1)}, u32[]{:S(2)}, u32[]{:S(2)}) %collective-permute-start.7) | collective-permute-done | bytes 495648 | tf_op jit(solution)/shard_map/ppermute | solution.py:24
  46.1 4.4 %collective-permute-done.8.refs_0_ = f32[968,128]{1,0:T(8,128)S(1)} collective-permute-done((f32[968,128]{1,0:T(8,128)S(1)}, f32[968,128]{1,0:T(8,128)S(1)}, u32[]{:S(2)}, u32[]{:S(2)}) %collective-permute-start.8) | collective-permute-done | bytes 495648 | tf_op jit(solution)/shard_map/ppermute | solution.py:24
  51.4 1.6 %collective-permute-start.9 = (f32[128,128]{1,0:T(8,128)S(1)}, f32[128,128]{1,0:T(8,128)S(1)}, u32[]{:S(2)}, u32[]{:S(2)}) collective-permute-start(f32[128,128]{1,0:T(8,128)S(1)} %get-tuple-element.75.refs_3_), channel_id=1, source_target_pairs={{0,1},{1,0},{2,3},{3,2},{4,5},{5,4},{6,7},{7,6},{8,9},{9,8},{10,11... | collective-permute-start | bytes 196616 | tf_op jit(solution)/shard_map/ppermute | solution.py:29
  53.0 1.8 %shard_map.107 = (f32[2048,128]{1,0:T(8,128)}, f32[2048,128]{1,0:T(8,128)}) custom-call(bf16[128,96]{1,0:T(8,128)(2,1)S(1)} %get-tuple-element.40.lhs_ref, f32[32,2048]{1,0:T(8,128)S(1)} %shard_map.106.own_ref, f32[32,2048]{1,0:T(8,128)S(1)} %collective-permute-done.6.other_ref, f32[32,128]{1,0:T(8,128)S(1)} %get-tuple-element.53.bounds_ref, ...), custom_call_target="tpu_custom_call" | custom-call | flops 50331648 | bytes 2097152 | tf_op jit(solution)/shard_map/pallas_call | solution.py:358
  54.8 1.0 %collective-permute-done.9.refs_4_ = f32[128,128]{1,0:T(8,128)S(1)} collective-permute-done((f32[128,128]{1,0:T(8,128)S(1)}, f32[128,128]{1,0:T(8,128)S(1)}, u32[]{:S(2)}, u32[]{:S(2)}) %collective-permute-start.9) | collective-permute-done | bytes 65568 | tf_op jit(solution)/shard_map/ppermute | solution.py:29
  55.7 3.6 %shard_map.110 = f32[8,128,16,128]{3,2,1,0:T(8,128)} custom-call(f32[8192,128]{1,0:T(8,128)S(1)} %get-tuple-element.71.refs_0_, f32[8192,128]{1,0:T(8,128)S(1)} %get-tuple-element.74.refs_1_, f32[128,128]{1,0:T(8,128)S(1)} %bitcast.21, f32[128,128]{1,0:T(8,128)S(1)} %get-tuple-element.75.refs_3_, f32[128,128]{1,0:T(8,128)S(1)} %collective-permute-done.9.refs_4_), custom_call_target="tpu_custom_call" | custom-call | flops 2097152 | bytes 16777216 | tf_op jit(solution)/shard_map/pallas_call | solution.py:358
  (38 shorter events, 8.1 us)
Async XLA Ops:
  0.6 10.2 %copy-start.11 = (s32[16]{0:T(128)S(1)}, s32[16]{0:T(128)}, u32[]{:S(2)}) copy-start(s32[16]{0:T(128)} %margin_ref.1) | copy-start | bytes 196
  0.6 10.2 %copy-start.10 = (f32[32]{0:T(128)S(1)}, f32[32]{0:T(128)}, u32[]{:S(2)}) copy-start(f32[32]{0:T(128)} %bounds_ref.1) | copy-start | bytes 388
  0.7 10.2 %copy-start.8 = (f32[1,128,32]{1,2,0:T(8,128)S(1)}, f32[1,128,32]{1,2,0:T(8,128)}, u32[]{:S(2)}) copy-start(f32[1,128,32]{1,2,0:T(8,128)} %param.11) | copy-start | bytes 49156
  0.7 10.2 %copy-start.9 = (f32[8,16]{1,0:T(8,128)S(1)}, f32[8,16]{1,0:T(8,128)}, u32[]{:S(2)}) copy-start(f32[8,16]{1,0:T(8,128)} %filters_ref.1) | copy-start | bytes 1540
  0.7 28.2 %copy-start.7 = (f32[8,16,128]{2,1,0:T(8,128)S(1)}, f32[8,16,128]{2,1,0:T(8,128)}, u32[]{:S(2)}) copy-start(f32[8,16,128]{2,1,0:T(8,128)} %param.9) | copy-start | bytes 196612
  3.0 27.9 %copy-start = (f32[128,16,128]{2,1,0:T(8,128)S(1)}, f32[128,16,128]{2,1,0:T(8,128)}, u32[]{:S(2)}) copy-start(f32[128,16,128]{2,1,0:T(8,128)} %param.7) | copy-start | bytes 3145732
  3.0 27.9 %copy-start.1 = (f32[128,16,128]{2,1,0:T(8,128)S(1)}, f32[128,16,128]{2,1,0:T(8,128)}, u32[]{:S(2)}) copy-start(f32[128,16,128]{2,1,0:T(8,128)} %param.8) | copy-start | bytes 3145732
  3.0 13.1 %collective-permute-start.1 = (f32[968,128]{1,0:T(8,128)S(1)}, f32[968,128]{1,0:T(8,128)S(1)}, u32[]{:S(2)}, u32[]{:S(2)}) collective-permute-start(f32[968,128]{1,0:T(8,128)S(1)} %get-tuple-element.45), channel_id=1, source_target_pairs={{0,2},{2,4},{4,6},{6,8},{8,10},{10,12},{12,14},{14,16},{16,18},{18... | collective-permute-start | bytes 1486856 | tf_op jit(solution)/shard_map/ppermute | solution.py:24
  7.3 15.5 %collective-permute-start = (f32[968,128]{1,0:T(8,128)S(1)}, f32[968,128]{1,0:T(8,128)S(1)}, u32[]{:S(2)}, u32[]{:S(2)}) collective-permute-start(f32[968,128]{1,0:T(8,128)S(1)} %get-tuple-element.42), channel_id=1, source_target_pairs={{0,2},{2,4},{4,6},{6,8},{8,10},{10,12},{12,14},{14,16},{16,18},{18... | collective-permute-start | bytes 1486856 | tf_op jit(solution)/shard_map/ppermute | solution.py:24
  11.8 1.0 %copy-start.2 = (f32[1024,128]{1,0:T(8,128)S(1)}, f32[1024,128]{1,0:T(8,128)}, u32[]{:S(2)}) copy-start(f32[1024,128]{1,0:T(8,128)} %get-tuple-element.43.refs_1_.own_ref) | copy-start | bytes 1572868
  12.8 1.0 %copy-start.5 = (f32[1024,128]{1,0:T(8,128)S(1)}, f32[1024,128]{1,0:T(8,128)}, u32[]{:S(2)}) copy-start(f32[1024,128]{1,0:T(8,128)} %get-tuple-element.46.refs_1_.refs_0_.own_ref) | copy-start | bytes 1572868
  14.5 8.3 %collective-permute-start.2 = (f32[32,2048]{1,0:T(8,128)S(1)}, f32[32,2048]{1,0:T(8,128)S(1)}, u32[]{:S(2)}, u32[]{:S(2)}) collective-permute-start(f32[32,2048]{1,0:T(8,128)S(1)} %get-tuple-element.51.own_ref), channel_id=1, source_target_pairs={{0,1},{1,0},{2,3},{3,2},{4,5},{5,4},{6,7},{7,6},{8,9},{9,8},{10,11... | collective-permute-start | bytes 786440 | tf_op jit(solution)/shard_map/ppermute | solution.py:29
  16.8 16.3 %collective-permute-start.4 = (f32[1928,128]{1,0:T(8,128)S(1)}, f32[1928,128]{1,0:T(8,128)S(1)}, u32[]{:S(2)}, u32[]{:S(2)}) collective-permute-start(f32[1928,128]{1,0:T(8,128)S(1)} %get-tuple-element.56), channel_id=1, source_target_pairs={{2,0},{4,2},{6,4},{8,6},{10,8},{12,10},{14,12},{16,14},{18,16},{20... | collective-permute-start | bytes 2961416 | tf_op jit(solution)/shard_map/ppermute | solution.py:24
  22.8 1.0 %copy-start.3 = (f32[1024,128]{1,0:T(8,128)S(1)}, f32[1024,128]{1,0:T(8,128)}, u32[]{:S(2)}) copy-start(f32[1024,128]{1,0:T(8,128)} %get-tuple-element.43.refs_1_.own_ref) | copy-start | bytes 1572868
  24.5 4.3 %collective-permute-start.3 = (f32[128,128]{1,0:T(8,128)S(1)}, f32[128,128]{1,0:T(8,128)S(1)}, u32[]{:S(2)}, u32[]{:S(2)}) collective-permute-start(f32[128,128]{1,0:T(8,128)S(1)} %get-tuple-element.50.own_ref), channel_id=1, source_target_pairs={{0,1},{1,0},{2,3},{3,2},{4,5},{5,4},{6,7},{7,6},{8,9},{9,8},{10,11... | collective-permute-start | bytes 196616 | tf_op jit(solution)/shard_map/ppermute | solution.py:29
  28.9 4.2 %collective-permute-start.5 = (f32[64,128]{1,0:T(8,128)S(1)}, f32[64,128]{1,0:T(8,128)S(1)}, u32[]{:S(2)}, u32[]{:S(2)}) collective-permute-start(f32[64,128]{1,0:T(8,128)S(1)} %get-tuple-element.60), channel_id=1, source_target_pairs={{2,0},{4,2},{6,4},{8,6},{10,8},{12,10},{14,12},{16,14},{18,16},{20... | collective-permute-start | bytes 98312 | tf_op jit(solution)/shard_map/ppermute | solution.py:24
  32.0 1.1 %copy-start.6 = (f32[1024,128]{1,0:T(8,128)S(1)}, f32[1024,128]{1,0:T(8,128)}, u32[]{:S(2)}) copy-start(f32[1024,128]{1,0:T(8,128)} %get-tuple-element.46.refs_1_.refs_0_.own_ref) | copy-start | bytes 1572868
  33.1 3.8 %copy-start.4 = (f32[1024,128]{1,0:T(8,128)S(1)}, f32[1024,128]{1,0:T(8,128)}, u32[]{:S(2)}) copy-start(f32[1024,128]{1,0:T(8,128)} %get-tuple-element.43.refs_1_.own_ref) | copy-start | bytes 1572868
  34.1 11.1 %collective-permute-start.7 = (f32[968,128]{1,0:T(8,128)S(1)}, f32[968,128]{1,0:T(8,128)S(1)}, u32[]{:S(2)}, u32[]{:S(2)}) collective-permute-start(f32[968,128]{1,0:T(8,128)S(1)} %get-tuple-element.70), channel_id=1, source_target_pairs={{0,2},{2,4},{4,6},{6,8},{8,10},{10,12},{12,14},{14,16},{16,18},{18... | collective-permute-start | bytes 1486856 | tf_op jit(solution)/shard_map/ppermute | solution.py:24
  37.8 12.6 %collective-permute-start.8 = (f32[968,128]{1,0:T(8,128)S(1)}, f32[968,128]{1,0:T(8,128)S(1)}, u32[]{:S(2)}, u32[]{:S(2)}) collective-permute-start(f32[968,128]{1,0:T(8,128)S(1)} %get-tuple-element.72), channel_id=1, source_target_pairs={{0,2},{2,4},{4,6},{6,8},{8,10},{10,12},{12,14},{14,16},{16,18},{18... | collective-permute-start | bytes 1486856 | tf_op jit(solution)/shard_map/ppermute | solution.py:24
  41.4 11.6 %collective-permute-start.6 = (f32[32,2048]{1,0:T(8,128)S(1)}, f32[32,2048]{1,0:T(8,128)S(1)}, u32[]{:S(2)}, u32[]{:S(2)}) collective-permute-start(f32[32,2048]{1,0:T(8,128)S(1)} %shard_map.106.own_ref), channel_id=1, source_target_pairs={{0,1},{1,0},{2,3},{3,2},{4,5},{5,4},{6,7},{7,6},{8,9},{9,8},{10,11... | collective-permute-start | bytes 786440 | tf_op jit(solution)/shard_map/ppermute | solution.py:29
  51.4 4.3 %collective-permute-start.9 = (f32[128,128]{1,0:T(8,128)S(1)}, f32[128,128]{1,0:T(8,128)S(1)}, u32[]{:S(2)}, u32[]{:S(2)}) collective-permute-start(f32[128,128]{1,0:T(8,128)S(1)} %get-tuple-element.75.refs_3_), channel_id=1, source_target_pairs={{0,1},{1,0},{2,3},{3,2},{4,5},{5,4},{6,7},{7,6},{8,9},{9,8},{10,11... | collective-permute-start | bytes 196616 | tf_op jit(solution)/shard_map/ppermute | solution.py:29

commit v6 on v5

--- a/solution.py
+++ b/solution.py
@@ -15,7 +15,7 @@
 GROUP = 32
 PAD = 8
 VMEM_LIMIT = 24 << 20
-REFLECT_LIMIT = 56000000
+REFLECT_LIMIT = 55000000
 
 
 def shift(value, axis, steps):

time: 59.7 us -> 54.9 us (0.920)
  local copies, waits for them, and re-layouts: 3.17 us -> 0.04 us
  Pallas kernels: 20.2 us -> 18.6 us
  starting transfers between devices: 22 us -> 21.2 us
  waiting for transfers between devices: 13.1 us -> 13.9 us
    unnamed x24 -> x14, local copies, waits for them, and re-layouts: 3.16 us -> 0.03 us
    pallas_call x17, Pallas kernels: 20.2 us -> 18.6 us  [call(): pl.pallas_call(kernel, out_shape=outs, in_specs=ins, out_specs=out_specs...]
    ppermute x6, waiting for transfers between devices: 6.57 us -> 7.59 us  [shift(): lax.ppermute(value, axis, [(source, source + steps) for source in range(i...]
    ppermute x6, starting transfers between devices: 15.6 us -> 14.9 us  [shift(): lax.ppermute(value, axis, [(source, source + steps) for source in range(i...]
  transfers between devices with their start and end apart: 10 -> 10, of which waited for: 5 -> 6; matrix products, arithmetic and copies ran while one was open for 0% -> 0% of each run, Pallas kernels for 23% -> 23%
where the time goes in v6:
time: 54.9 us; the launch traced here: 54.6 us
  starting transfers between devices  21.2 us (39%)
  Pallas kernels  18.6 us (34%)
  waiting for transfers between devices  13.9 us (25%)
  between operations  0.87 us (2%)
    pallas_call x17, Pallas kernels, call(): pl.pallas_call(kernel, out_shape=outs, in_specs=ins, out_specs=out_specs...  18.6 us
    ppermute x6, starting transfers between devices, shift(): lax.ppermute(value, axis, [(source, source + steps) for source in range(i...  14.9 us
    ppermute x6, waiting for transfers between devices, shift(): lax.ppermute(value, axis, [(source, source + steps) for source in range(i...  7.59 us
    ppermute x4, starting transfers between devices, chan_pairs(): lax.ppermute(value, 'chan', [(source, source ^ stride) for source in rang...  6.36 us
    ppermute x4, waiting for transfers between devices, chan_pairs(): lax.ppermute(value, 'chan', [(source, source ^ stride) for source in rang...  6.29 us
  transfers between devices with their start and end apart: 10, of which 6 were waited for; matrix products, arithmetic and copies ran while one was open for 0% of the time, Pallas kernels for 23%

profile of v6, /device:TPU:16, one launch (start us, length us, event | category | flops | bytes accessed | tf_op | source)
XLA Modules:
  0.0 54.6 jit_solution(3201976339802211656)
XLA Ops:
  0.7 1.5 %shard_map.96 = (f32[1024,128]{1,0:T(8,128)S(1)}, f32[968,128]{1,0:T(8,128)S(1)}) custom-call(f32[2048,128]{1,0:T(8,128)} %bitcast.8, f32[2048,128]{1,0:T(8,128)} %bitcast.14), custom_call_target="tpu_custom_call" | custom-call | flops 524288 | bytes 1572864 | tf_op jit(solution)/shard_map/pallas_call | solution.py:358
  2.2 2.1 %collective-permute-start.1 = (f32[968,128]{1,0:T(8,128)S(1)}, f32[968,128]{1,0:T(8,128)S(1)}, u32[]{:S(2)}, u32[]{:S(2)}) collective-permute-start(f32[968,128]{1,0:T(8,128)S(1)} %get-tuple-element.45), channel_id=1, source_target_pairs={{0,2},{2,4},{4,6},{6,8},{8,10},{10,12},{12,14},{14,16},{16,18},{18... | collective-permute-start | bytes 1486856 | tf_op jit(solution)/shard_map/ppermute | solution.py:24
  4.3 1.5 %shard_map.95 = (f32[1024,128]{1,0:T(8,128)S(1)}, f32[968,128]{1,0:T(8,128)S(1)}) custom-call(f32[2048,128]{1,0:T(8,128)} %bitcast.9, f32[2048,128]{1,0:T(8,128)} %bitcast.15), custom_call_target="tpu_custom_call" | custom-call | flops 524288 | bytes 1572864 | tf_op jit(solution)/shard_map/pallas_call | solution.py:358
  5.7 3.5 %collective-permute-start = (f32[968,128]{1,0:T(8,128)S(1)}, f32[968,128]{1,0:T(8,128)S(1)}, u32[]{:S(2)}, u32[]{:S(2)}) collective-permute-start(f32[968,128]{1,0:T(8,128)S(1)} %get-tuple-element.42), channel_id=1, source_target_pairs={{0,2},{2,4},{4,6},{6,8},{8,10},{10,12},{12,14},{14,16},{16,18},{18... | collective-permute-start | bytes 1486856 | tf_op jit(solution)/shard_map/ppermute | solution.py:24
  10.9 1.6 %collective-permute-start.2 = (f32[32,2048]{1,0:T(8,128)S(1)}, f32[32,2048]{1,0:T(8,128)S(1)}, u32[]{:S(2)}, u32[]{:S(2)}) collective-permute-start(f32[32,2048]{1,0:T(8,128)S(1)} %get-tuple-element.51.own_ref), channel_id=1, source_target_pairs={{0,1},{1,0},{2,3},{3,2},{4,5},{5,4},{6,7},{7,6},{8,9},{9,8},{10,11... | collective-permute-start | bytes 786440 | tf_op jit(solution)/shard_map/ppermute | solution.py:29
  12.4 1.0 %collective-permute-done.1.refs_0_ = f32[968,128]{1,0:T(8,128)S(1)} collective-permute-done((f32[968,128]{1,0:T(8,128)S(1)}, f32[968,128]{1,0:T(8,128)S(1)}, u32[]{:S(2)}, u32[]{:S(2)}) %collective-permute-start.1) | collective-permute-done | bytes 495648 | tf_op jit(solution)/shard_map/ppermute | solution.py:24
  14.2 1.9 %collective-permute-start.4 = (f32[1928,128]{1,0:T(8,128)S(1)}, f32[1928,128]{1,0:T(8,128)S(1)}, u32[]{:S(2)}, u32[]{:S(2)}) collective-permute-start(f32[1928,128]{1,0:T(8,128)S(1)} %get-tuple-element.56), channel_id=1, source_target_pairs={{2,0},{4,2},{6,4},{8,6},{10,8},{12,10},{14,12},{16,14},{18,16},{20... | collective-permute-start | bytes 2961416 | tf_op jit(solution)/shard_map/ppermute | solution.py:24
  16.1 3.1 %collective-permute-done.2.other_ref = f32[32,2048]{1,0:T(8,128)S(1)} collective-permute-done((f32[32,2048]{1,0:T(8,128)S(1)}, f32[32,2048]{1,0:T(8,128)S(1)}, u32[]{:S(2)}, u32[]{:S(2)}) %collective-permute-start.2) | collective-permute-done | bytes 262176 | tf_op jit(solution)/shard_map/ppermute | solution.py:29
  19.9 1.6 %collective-permute-start.3 = (f32[128,128]{1,0:T(8,128)S(1)}, f32[128,128]{1,0:T(8,128)S(1)}, u32[]{:S(2)}, u32[]{:S(2)}) collective-permute-start(f32[128,128]{1,0:T(8,128)S(1)} %get-tuple-element.50.own_ref), channel_id=1, source_target_pairs={{0,1},{1,0},{2,3},{3,2},{4,5},{5,4},{6,7},{7,6},{8,9},{9,8},{10,11... | collective-permute-start | bytes 196616 | tf_op jit(solution)/shard_map/ppermute | solution.py:29
  21.9 2.3 %collective-permute-done.3.other_ref = f32[128,128]{1,0:T(8,128)S(1)} collective-permute-done((f32[128,128]{1,0:T(8,128)S(1)}, f32[128,128]{1,0:T(8,128)S(1)}, u32[]{:S(2)}, u32[]{:S(2)}) %collective-permute-start.3) | collective-permute-done | bytes 65568 | tf_op jit(solution)/shard_map/ppermute | solution.py:29
  24.2 1.9 %collective-permute-start.5 = (f32[64,128]{1,0:T(8,128)S(1)}, f32[64,128]{1,0:T(8,128)S(1)}, u32[]{:S(2)}, u32[]{:S(2)}) collective-permute-start(f32[64,128]{1,0:T(8,128)S(1)} %get-tuple-element.60), channel_id=1, source_target_pairs={{2,0},{4,2},{6,4},{8,6},{10,8},{12,10},{14,12},{16,14},{18,16},{20... | collective-permute-start | bytes 98312 | tf_op jit(solution)/shard_map/ppermute | solution.py:24
  26.2 1.1 %shard_map.104.partial_ref = f32[1024,128]{1,0:T(8,128)S(1)} custom-call(f32[8192,128]{1,0:T(8,128)S(1)} %get-tuple-element.65.dual_ref.refs_4_, bf16[32,256]{1,0:T(8,128)(2,1)S(1)} %get-tuple-element.62.lhs_ref, f32[128,128]{1,0:T(8,128)S(1)} %get-tuple-element.63.scale_ref.refs_5_, f32[2048,128]{1,0:T(8,128)S(1)} %shard_map.100.s_ref.refs_0_, ...), custom_call_target="tpu_custom_call" | custom-call | flops 4429185024 | bytes 92274688 | tf_op jit(solution)/shard_map/pallas_call | solution.py:358
  27.3 1.1 %shard_map.102.partial_ref = f32[1024,128]{1,0:T(8,128)S(1)} custom-call(f32[8192,128]{1,0:T(8,128)S(1)} %get-tuple-element.61.dual_ref.refs_4_, bf16[32,256]{1,0:T(8,128)(2,1)S(1)} %get-tuple-element.62.lhs_ref, f32[128,128]{1,0:T(8,128)S(1)} %get-tuple-element.63.scale_ref.refs_5_, f32[2048,128]{1,0:T(8,128)S(1)} %shard_map.100.s_ref.refs_0_, ...), custom_call_target="tpu_custom_call" | custom-call | flops 4429185024 | bytes 92274688 | tf_op jit(solution)/shard_map/pallas_call | solution.py:358
  29.4 3.0 %collective-permute-start.7 = (f32[968,128]{1,0:T(8,128)S(1)}, f32[968,128]{1,0:T(8,128)S(1)}, u32[]{:S(2)}, u32[]{:S(2)}) collective-permute-start(f32[968,128]{1,0:T(8,128)S(1)} %get-tuple-element.70), channel_id=1, source_target_pairs={{0,2},{2,4},{4,6},{6,8},{8,10},{10,12},{12,14},{14,16},{16,18},{18... | collective-permute-start | bytes 1486856 | tf_op jit(solution)/shard_map/ppermute | solution.py:24
  33.2 2.5 %collective-permute-start.8 = (f32[968,128]{1,0:T(8,128)S(1)}, f32[968,128]{1,0:T(8,128)S(1)}, u32[]{:S(2)}, u32[]{:S(2)}) collective-permute-start(f32[968,128]{1,0:T(8,128)S(1)} %get-tuple-element.72), channel_id=1, source_target_pairs={{0,2},{2,4},{4,6},{6,8},{8,10},{10,12},{12,14},{14,16},{16,18},{18... | collective-permute-start | bytes 1486856 | tf_op jit(solution)/shard_map/ppermute | solution.py:24
  36.7 1.6 %collective-permute-start.6 = (f32[32,2048]{1,0:T(8,128)S(1)}, f32[32,2048]{1,0:T(8,128)S(1)}, u32[]{:S(2)}, u32[]{:S(2)}) collective-permute-start(f32[32,2048]{1,0:T(8,128)S(1)} %shard_map.106.own_ref), channel_id=1, source_target_pairs={{0,1},{1,0},{2,3},{3,2},{4,5},{5,4},{6,7},{7,6},{8,9},{9,8},{10,11... | collective-permute-start | bytes 786440 | tf_op jit(solution)/shard_map/ppermute | solution.py:29
  38.2 2.2 %collective-permute-done.7.refs_0_ = f32[968,128]{1,0:T(8,128)S(1)} collective-permute-done((f32[968,128]{1,0:T(8,128)S(1)}, f32[968,128]{1,0:T(8,128)S(1)}, u32[]{:S(2)}, u32[]{:S(2)}) %collective-permute-start.7) | collective-permute-done | bytes 495648 | tf_op jit(solution)/shard_map/ppermute | solution.py:24
  40.4 0.9 %shard_map.108 = (f32[8192,128]{1,0:T(8,128)S(1)}, f32[128,128]{1,0:T(8,128)S(1)}) custom-call(f32[968,128]{1,0:T(8,128)S(1)} %collective-permute-done.7.refs_0_, f32[1024,128]{1,0:T(8,128)S(1)} %get-tuple-element.64.refs_1_, bf16[128,96]{1,0:T(8,128)(2,1)S(1)} %get-tuple-element.44.refs_2_, f32[128,128]{1,0:T(8,128)S(1)} %broadcast_1_refs_3_.2.refs_3_, ...), custom_call_target="tpu_custom_call" | custom-call | flops 201326592 | bytes 8388608 | tf_op jit(solution)/shard_map/pallas_call | solution.py:358
  41.4 4.4 %collective-permute-done.8.refs_0_ = f32[968,128]{1,0:T(8,128)S(1)} collective-permute-done((f32[968,128]{1,0:T(8,128)S(1)}, f32[968,128]{1,0:T(8,128)S(1)}, u32[]{:S(2)}, u32[]{:S(2)}) %collective-permute-start.8) | collective-permute-done | bytes 495648 | tf_op jit(solution)/shard_map/ppermute | solution.py:24
  45.8 0.9 %shard_map.109 = (f32[8192,128]{1,0:T(8,128)S(1)}, f32[128,128]{1,0:T(8,128)S(1)}) custom-call(f32[968,128]{1,0:T(8,128)S(1)} %collective-permute-done.8.refs_0_, f32[1024,128]{1,0:T(8,128)S(1)} %get-tuple-element.66.refs_2_.refs_1_, bf16[128,96]{1,0:T(8,128)(2,1)S(1)} %get-tuple-element.44.refs_2_, f32[128,128]{1,0:T(8,128)S(1)} %get-tuple-element.73.refs_3_, ...), custom_call_target="tpu_custom_call" | custom-call | flops 201326592 | bytes 8388608 | tf_op jit(solution)/shard_map/pallas_call | solution.py:358
  46.7 1.6 %collective-permute-start.9 = (f32[128,128]{1,0:T(8,128)S(1)}, f32[128,128]{1,0:T(8,128)S(1)}, u32[]{:S(2)}, u32[]{:S(2)}) collective-permute-start(f32[128,128]{1,0:T(8,128)S(1)} %get-tuple-element.75.refs_3_), channel_id=1, source_target_pairs={{0,1},{1,0},{2,3},{3,2},{4,5},{5,4},{6,7},{7,6},{8,9},{9,8},{10,11... | collective-permute-start | bytes 196616 | tf_op jit(solution)/shard_map/ppermute | solution.py:29
  48.3 1.8 %shard_map.107 = (f32[2048,128]{1,0:T(8,128)}, f32[2048,128]{1,0:T(8,128)}) custom-call(bf16[128,96]{1,0:T(8,128)(2,1)S(1)} %get-tuple-element.40.lhs_ref, f32[32,2048]{1,0:T(8,128)S(1)} %shard_map.106.own_ref, f32[32,2048]{1,0:T(8,128)S(1)} %collective-permute-done.6.other_ref, f32[32,128]{1,0:T(8,128)S(1)} %get-tuple-element.53.bounds_ref, ...), custom_call_target="tpu_custom_call" | custom-call | flops 50331648 | bytes 2097152 | tf_op jit(solution)/shard_map/pallas_call | solution.py:358
  50.1 1.0 %collective-permute-done.9.refs_4_ = f32[128,128]{1,0:T(8,128)S(1)} collective-permute-done((f32[128,128]{1,0:T(8,128)S(1)}, f32[128,128]{1,0:T(8,128)S(1)}, u32[]{:S(2)}, u32[]{:S(2)}) %collective-permute-start.9) | collective-permute-done | bytes 65568 | tf_op jit(solution)/shard_map/ppermute | solution.py:29
  51.0 3.6 %shard_map.110 = f32[8,128,16,128]{3,2,1,0:T(8,128)} custom-call(f32[8192,128]{1,0:T(8,128)S(1)} %get-tuple-element.71.refs_0_, f32[8192,128]{1,0:T(8,128)S(1)} %get-tuple-element.74.refs_1_, f32[128,128]{1,0:T(8,128)S(1)} %bitcast.21, f32[128,128]{1,0:T(8,128)S(1)} %get-tuple-element.75.refs_3_, f32[128,128]{1,0:T(8,128)S(1)} %collective-permute-done.9.refs_4_), custom_call_target="tpu_custom_call" | custom-call | flops 2097152 | bytes 16777216 | tf_op jit(solution)/shard_map/pallas_call | solution.py:358
  (28 shorter events, 6.2 us)
Async XLA Ops:
  0.6 8.6 %copy-start.6 = (s32[16]{0:T(128)S(1)}, s32[16]{0:T(128)}, u32[]{:S(2)}) copy-start(s32[16]{0:T(128)} %margin_ref.1) | copy-start | bytes 196
  0.6 8.6 %copy-start.5 = (f32[32]{0:T(128)S(1)}, f32[32]{0:T(128)}, u32[]{:S(2)}) copy-start(f32[32]{0:T(128)} %bounds_ref.1) | copy-start | bytes 388
  0.7 8.6 %copy-start.3 = (f32[1,128,32]{1,2,0:T(8,128)S(1)}, f32[1,128,32]{1,2,0:T(8,128)}, u32[]{:S(2)}) copy-start(f32[1,128,32]{1,2,0:T(8,128)} %param.11) | copy-start | bytes 49156
  0.7 8.6 %copy-start.4 = (f32[8,16]{1,0:T(8,128)S(1)}, f32[8,16]{1,0:T(8,128)}, u32[]{:S(2)}) copy-start(f32[8,16]{1,0:T(8,128)} %filters_ref.1) | copy-start | bytes 1540
  0.7 23.5 %copy-start.2 = (f32[8,16,128]{2,1,0:T(8,128)S(1)}, f32[8,16,128]{2,1,0:T(8,128)}, u32[]{:S(2)}) copy-start(f32[8,16,128]{2,1,0:T(8,128)} %param.9) | copy-start | bytes 196612
  2.2 24.0 %copy-start = (f32[128,16,128]{2,1,0:T(8,128)S(1)}, f32[128,16,128]{2,1,0:T(8,128)}, u32[]{:S(2)}) copy-start(f32[128,16,128]{2,1,0:T(8,128)} %param.7) | copy-start | bytes 3145732
  2.2 24.0 %copy-start.1 = (f32[128,16,128]{2,1,0:T(8,128)S(1)}, f32[128,16,128]{2,1,0:T(8,128)}, u32[]{:S(2)}) copy-start(f32[128,16,128]{2,1,0:T(8,128)} %param.8) | copy-start | bytes 3145732
  2.2 11.2 %collective-permute-start.1 = (f32[968,128]{1,0:T(8,128)S(1)}, f32[968,128]{1,0:T(8,128)S(1)}, u32[]{:S(2)}, u32[]{:S(2)}) collective-permute-start(f32[968,128]{1,0:T(8,128)S(1)} %get-tuple-element.45), channel_id=1, source_target_pairs={{0,2},{2,4},{4,6},{6,8},{8,10},{10,12},{12,14},{14,16},{16,18},{18... | collective-permute-start | bytes 1486856 | tf_op jit(solution)/shard_map/ppermute | solution.py:24
  5.7 13.4 %collective-permute-start = (f32[968,128]{1,0:T(8,128)S(1)}, f32[968,128]{1,0:T(8,128)S(1)}, u32[]{:S(2)}, u32[]{:S(2)}) collective-permute-start(f32[968,128]{1,0:T(8,128)S(1)} %get-tuple-element.42), channel_id=1, source_target_pairs={{0,2},{2,4},{4,6},{6,8},{8,10},{10,12},{12,14},{14,16},{16,18},{18... | collective-permute-start | bytes 1486856 | tf_op jit(solution)/shard_map/ppermute | solution.py:24
  10.9 8.3 %collective-permute-start.2 = (f32[32,2048]{1,0:T(8,128)S(1)}, f32[32,2048]{1,0:T(8,128)S(1)}, u32[]{:S(2)}, u32[]{:S(2)}) collective-permute-start(f32[32,2048]{1,0:T(8,128)S(1)} %get-tuple-element.51.own_ref), channel_id=1, source_target_pairs={{0,1},{1,0},{2,3},{3,2},{4,5},{5,4},{6,7},{7,6},{8,9},{9,8},{10,11... | collective-permute-start | bytes 786440 | tf_op jit(solution)/shard_map/ppermute | solution.py:29
  14.2 14.3 %collective-permute-start.4 = (f32[1928,128]{1,0:T(8,128)S(1)}, f32[1928,128]{1,0:T(8,128)S(1)}, u32[]{:S(2)}, u32[]{:S(2)}) collective-permute-start(f32[1928,128]{1,0:T(8,128)S(1)} %get-tuple-element.56), channel_id=1, source_target_pairs={{2,0},{4,2},{6,4},{8,6},{10,8},{12,10},{14,12},{16,14},{18,16},{20... | collective-permute-start | bytes 2961416 | tf_op jit(solution)/shard_map/ppermute | solution.py:24
  19.9 4.3 %collective-permute-start.3 = (f32[128,128]{1,0:T(8,128)S(1)}, f32[128,128]{1,0:T(8,128)S(1)}, u32[]{:S(2)}, u32[]{:S(2)}) collective-permute-start(f32[128,128]{1,0:T(8,128)S(1)} %get-tuple-element.50.own_ref), channel_id=1, source_target_pairs={{0,1},{1,0},{2,3},{3,2},{4,5},{5,4},{6,7},{7,6},{8,9},{9,8},{10,11... | collective-permute-start | bytes 196616 | tf_op jit(solution)/shard_map/ppermute | solution.py:29
  24.2 4.2 %collective-permute-start.5 = (f32[64,128]{1,0:T(8,128)S(1)}, f32[64,128]{1,0:T(8,128)S(1)}, u32[]{:S(2)}, u32[]{:S(2)}) collective-permute-start(f32[64,128]{1,0:T(8,128)S(1)} %get-tuple-element.60), channel_id=1, source_target_pairs={{2,0},{4,2},{6,4},{8,6},{10,8},{12,10},{14,12},{16,14},{18,16},{20... | collective-permute-start | bytes 98312 | tf_op jit(solution)/shard_map/ppermute | solution.py:24
  29.4 11.1 %collective-permute-start.7 = (f32[968,128]{1,0:T(8,128)S(1)}, f32[968,128]{1,0:T(8,128)S(1)}, u32[]{:S(2)}, u32[]{:S(2)}) collective-permute-start(f32[968,128]{1,0:T(8,128)S(1)} %get-tuple-element.70), channel_id=1, source_target_pairs={{0,2},{2,4},{4,6},{6,8},{8,10},{10,12},{12,14},{14,16},{16,18},{18... | collective-permute-start | bytes 1486856 | tf_op jit(solution)/shard_map/ppermute | solution.py:24
  33.2 12.5 %collective-permute-start.8 = (f32[968,128]{1,0:T(8,128)S(1)}, f32[968,128]{1,0:T(8,128)S(1)}, u32[]{:S(2)}, u32[]{:S(2)}) collective-permute-start(f32[968,128]{1,0:T(8,128)S(1)} %get-tuple-element.72), channel_id=1, source_target_pairs={{0,2},{2,4},{4,6},{6,8},{8,10},{10,12},{12,14},{14,16},{16,18},{18... | collective-permute-start | bytes 1486856 | tf_op jit(solution)/shard_map/ppermute | solution.py:24
  36.7 11.6 %collective-permute-start.6 = (f32[32,2048]{1,0:T(8,128)S(1)}, f32[32,2048]{1,0:T(8,128)S(1)}, u32[]{:S(2)}, u32[]{:S(2)}) collective-permute-start(f32[32,2048]{1,0:T(8,128)S(1)} %shard_map.106.own_ref), channel_id=1, source_target_pairs={{0,1},{1,0},{2,3},{3,2},{4,5},{5,4},{6,7},{7,6},{8,9},{9,8},{10,11... | collective-permute-start | bytes 786440 | tf_op jit(solution)/shard_map/ppermute | solution.py:29
  46.7 4.3 %collective-permute-start.9 = (f32[128,128]{1,0:T(8,128)S(1)}, f32[128,128]{1,0:T(8,128)S(1)}, u32[]{:S(2)}, u32[]{:S(2)}) collective-permute-start(f32[128,128]{1,0:T(8,128)S(1)} %get-tuple-element.75.refs_3_), channel_id=1, source_target_pairs={{0,1},{1,0},{2,3},{3,2},{4,5},{5,4},{6,7},{7,6},{8,9},{9,8},{10,11... | collective-permute-start | bytes 196616 | tf_op jit(solution)/shard_map/ppermute | solution.py:29

commit v7 on v6

--- a/solution.py
+++ b/solution.py
@@ -75,9 +75,13 @@
     return jnp.dot(lhs, rhs, preferred_element_type=F32)
 
 
+def met_rows(bases, height):
+    return [min(height, 8 * (2 * basis // 8 + 1)) for basis in range(bases)]
+
+
 def setup_kernel(
     filters_ref, bounds_ref, margin_ref, loading_ref,
-    lift_ref, next_ref, interior_ref, border_ref, coef_ref, spectral_ref, limits_ref,
+    lift_ref, inner_ref, outer_ref, next_ref, interior_ref, border_ref, coef_ref, spectral_ref, limits_ref,
 ):
     bases, taps = filters_ref.shape
     height = taps
@@ -117,7 +121,13 @@
     tap_of = target - source + height
     below = toeplitz(bases * bases, reaching, jnp.where((source >= height) | (height - source <= next_margin), tap_of, -1))
 
-    lift_ref[...] = three_lhs(DUAL * own.T)
+    lift = DUAL * own.T
+    lift_ref[...] = three_lhs(lift)
+    inner_ref[...] = three_lhs(lift[:, height:])
+    met = [
+        lift[basis * height : basis * height + count, :height] for basis, count in enumerate(met_rows(bases, height))
+    ]
+    outer_ref[...] = three_lhs(jnp.concatenate(met, axis=0))
     next_ref[...] = three_lhs(DUAL * below.T)
     interior_ref[...] = two_lhs(own[height:])
     border_ref[...] = two_lhs(below[:height])
@@ -204,20 +214,18 @@
         out_ref[pl.ds(row + 1, channels, stride=height), :] = both[:, lanes:]
 
 
+def scale_of(weights, own_ref, other_ref):
+    return weights / jnp.maximum(jnp.sqrt(own_ref[...] + other_ref[...]), weights)
+
+
 def scale_kernel(height, weights_ref, own_ref, other_ref, scale_ref, above_ref):
-    weights = weights_ref[...]
-    scale_ref[...] = weights / jnp.maximum(jnp.sqrt(own_ref[...] + other_ref[...]), weights)
-    for basis in range(weights.shape[0] // height):
+    scale_ref[...] = scale_of(weights_ref[...], own_ref, other_ref)
+    for basis in range(weights_ref.shape[0] // height):
         count = 2 * basis + 1
         above_ref[pl.ds(basis * basis, count), :] = scale_ref[pl.ds(basis * height, count), :]
 
 
-def lift_kernel(height, kind, *refs):
-    if kind == "first":
-        halo_ref, own_ref, lhs_ref, before_ref, out_ref, squares_ref = refs
-    else:
-        halo_ref, own_ref, lhs_ref, before_ref, dual_ref, scale_ref, out_ref, squares_ref = refs
-        scale = scale_ref[...]
+def lift_kernel(height, halo_ref, own_ref, lhs_ref, before_ref, out_ref, squares_ref):
     lhs = lhs_ref[...]
     size = lhs.shape[0]
     lanes = own_ref.shape[1]
@@ -238,13 +246,57 @@
         )
         both = dot(lhs, three_rhs(value))
         for half in range(2):
-            rows = pl.ds((pair + half) * size, size)
             lifted = both[:, half * lanes : (half + 1) * lanes]
-            if kind == "second":
-                lifted = lifted + dual_ref[rows, :] * scale
+            out_ref[pl.ds((pair + half) * size, size), :] = lifted
+            total = total + lifted * lifted
+    squares_ref[...] = total
+
+
+def inner_kernel(height, own_ref, lhs_ref, dual_ref, scale_ref, before_ref, met_ref, free_ref, squares_ref):
+    lhs = lhs_ref[...]
+    size, lanes = scale_ref.shape
+    scale = scale_ref[...]
+    counts = met_rows(size // height, height)
+    many = sum(counts)
+    total = before_ref[...]
+    for pair in range(0, own_ref.shape[0] // height, 2):
+        value = jnp.concatenate(
+            [own_ref[pl.ds(channel * height, height), :] for channel in (pair, pair + 1)], axis=1
+        )
+        both = dot(lhs, three_rhs(value))
+        for half in range(2):
+            channel = pair + half
+            lifted = both[:, half * lanes : (half + 1) * lanes] + dual_ref[pl.ds(channel * size, size), :] * scale
+            met = [lifted[basis * height : basis * height + count] for basis, count in enumerate(counts)]
+            free = [
+                lifted[basis * height + count : (basis + 1) * height]
+                for basis, count in enumerate(counts)
+                if count < height
+            ]
+            met_ref[pl.ds(channel * many, many), :] = jnp.concatenate(met, axis=0)
+            free = jnp.concatenate(free, axis=0)
+            free_ref[pl.ds(channel * (size - many), size - many), :] = free
+            total = total + free * free
+    squares_ref[...] = total
+
+
+def outer_kernel(height, halo_ref, lhs_ref, met_ref, before_ref, free_ref, out_ref, squares_ref):
+    lhs = lhs_ref[...]
+    many = lhs.shape[0]
+    lanes = met_ref.shape[1]
+    total = before_ref[:many, :]
+    for pair in range(0, met_ref.shape[0] // many, 2):
+        value = jnp.concatenate(
+            [halo_ref[pl.ds(channel * (height - 1), height), :] for channel in (pair, pair + 1)], axis=1
+        )
+        both = dot(lhs, three_rhs(value))
+        for half in range(2):
+            rows = pl.ds((pair + half) * many, many)
+            lifted = both[:, half * lanes : (half + 1) * lanes] + met_ref[rows, :]
             out_ref[rows, :] = lifted
             total = total + lifted * lifted
-    squares_ref[...] = total
+    squares_ref[:many, :] = total
+    squares_ref[many:, :] = free_ref[...]
 
 
 def adjoint_kernel(height, start, dual_ref, lhs_ref, scale_ref, s_ref, x_ref, d_ref, partial_ref):
@@ -314,39 +366,48 @@
 
 
 def wavelet_kernel(chunks, height, *refs):
-    dual_refs = refs[:chunks]
-    weights_ref, mine_ref, other_ref, out_ref, buffer, sems = refs[chunks:]
-    size = weights_ref.shape[0]
-    bases = size // height
-    weights = weights_ref[...]
-    scale = weights / jnp.maximum(jnp.sqrt(mine_ref[...] + other_ref[...]), weights)
-    block = buffer.shape[2]
-    slots = buffer.shape[0]
-    pending = [None] * slots
+    met_refs, free_refs = refs[:chunks], refs[chunks : 2 * chunks]
+    weights_ref, mine_ref, other_ref, out_ref, buffer, sems = refs[2 * chunks :]
+    bases = weights_ref.shape[0] // height
+    counts = met_rows(bases, height)
+    many = sum(counts)
+    parts = [weights_ref[pl.ds(basis * height, count), :] for basis, count in enumerate(counts)]
+    parts += [
+        weights_ref[pl.ds(basis * height + count, height - count), :]
+        for basis, count in enumerate(counts)
+        if count < height
+    ]
+    scale = scale_of(jnp.concatenate(parts, axis=0), mine_ref, other_ref)
+    rest = scale.shape[0] - many
+    slots, block = buffer.shape[0], buffer.shape[2]
+    pending = [()] * slots
     turn = 0
-    for index, dual_ref in enumerate(dual_refs):
-        channels = dual_ref.shape[0] // size
+    for index, (met_ref, free_ref) in enumerate(zip(met_refs, free_refs)):
+        channels = met_ref.shape[0] // many
         for start in range(0, channels, block):
             slot = turn % slots
-            if pending[slot] is not None:
-                pending[slot].wait()
-
-            def step(channel, carry):
-                rows = pl.ds(pl.multiple_of((start + channel) * size, size), size)
-                value = dual_ref[rows, :] * scale
-                for basis in range(bases):
-                    buffer[slot, basis, channel] = value[basis * height : (basis + 1) * height]
-                return carry
-
-            lax.fori_loop(0, block, step, 0, unroll=2)
-            copy = pltpu.make_async_copy(
-                buffer.at[slot], out_ref.at[:, pl.ds(index * channels + start, block)], sems.at[slot]
-            )
-            copy.start()
-            pending[slot] = copy
+            for copy in pending[slot]:
+                copy.wait()
+            for channel in range(block):
+                met = met_ref[pl.ds((start + channel) * many, many), :] * scale[:many]
+                free = free_ref[pl.ds((start + channel) * rest, rest), :] * scale[many:]
+                first = second = 0
+                for basis, count in enumerate(counts):
+                    buffer[slot, basis, channel, :count] = met[first : first + count]
+                    first += count
+                    if count < height:
+                        buffer[slot, basis, channel, count:] = free[second : second + height - count]
+                        second += height - count
+            place = pl.ds(index * channels + start, block)
+            pending[slot] = [
+                pltpu.make_async_copy(buffer.at[slot, basis], out_ref.at[basis, place], sems.at[slot, basis])
+                for basis in range(bases)
+            ]
+            for copy in pending[slot]:
+                copy.start()
             turn += 1
-    for copy in pending:
-        if copy is not None:
+    for copies in pending:
+        for copy in copies:
             copy.wait()
 
 
@@ -354,13 +415,14 @@
     return pl.BlockSpec(memory_space=pltpu.VMEM)
 
 
-def call(kernel, outs, ins, operands, flops, nbytes, scratch=(), out_specs=None, limit=VMEM_LIMIT):
+def call(kernel, outs, ins, operands, flops, nbytes, scratch=(), out_specs=None, limit=VMEM_LIMIT, aliases=None):
     return pl.pallas_call(
         kernel,
         out_shape=outs,
         in_specs=ins,
         out_specs=out_specs if out_specs is not None else jax.tree.map(lambda _: whole(), outs),
         scratch_shapes=scratch,
+        input_output_aliases=aliases or {},
         compiler_params=pltpu.CompilerParams(vmem_limit_bytes=limit),
         cost_estimate=pl.CostEstimate(flops=flops, bytes_accessed=nbytes, transcendentals=0),
     )(*operands)
@@ -373,6 +435,9 @@
     assert taps == height
     size = bases * height
     reaching = bases * bases
+    counts = met_rows(bases, height)
+    met = sum(counts)
+    free = size - met
     chunks = CHUNKS if channels >= 8 * CHUNKS else 1
     per = channels // chunks
     block = per * height
@@ -403,10 +468,12 @@
         reflected.append(r)
         halos.append(shift(ahead, "facet", 1))
 
-    lift_lhs, next_lhs, interior_lhs, border_lhs, coef_lhs, spectral_lhs, limits = call(
+    lift_lhs, inner_lhs, outer_lhs, next_lhs, interior_lhs, border_lhs, coef_lhs, spectral_lhs, limits = call(
         setup_kernel,
         [
             jax.ShapeDtypeStruct((size, 6 * height), BF16),
+            jax.ShapeDtypeStruct((size, 3 * height), BF16),
+            jax.ShapeDtypeStruct((met, 3 * height), BF16),
             jax.ShapeDtypeStruct((reaching, 6 * height), BF16),
             jax.ShapeDtypeStruct((2 * height, 2 * size), BF16),
             jax.ShapeDtypeStruct((2 * height, 2 * reaching), BF16),
@@ -438,14 +505,13 @@
     lifted = []
     for index in range(chunks):
         out, squares = call(
-            functools.partial(lift_kernel, height, "first"), [flat(per * size), flat(size)], [whole()] * 4,
+            functools.partial(lift_kernel, height), [flat(per * size), flat(size)], [whole()] * 4,
             (halos[index], reflected[index], lift_lhs, squares), work, duals,
         )
         lifted.append(out)
         if index == 0:
             tied, _ = lax.optimization_barrier((everything, squares))
             below = shift(tied, "facet", -1)
-            squares, *terms = lax.optimization_barrier((squares, *terms))
     own, other = chan_terms(squares)
     (spectral,) = synthesis(*terms)
     other, spectral = lax.optimization_barrier((other, spectral))
@@ -473,14 +539,25 @@
         halos.append(shift(ahead, "facet", 1))
     terms = chan_terms(*coefficients(again, spectral))
 
+    squares = jnp.zeros((free, lanes), F32)
+    inner, early = [], []
+    for index in range(chunks):
+        for_halo, done, squares = call(
+            functools.partial(inner_kernel, height), [flat(per * met), flat(per * free), flat(free)], [whole()] * 5,
+            (again[index], inner_lhs, lifted[index], scale, squares), work, 2 * duals,
+        )
+        inner.append(for_halo)
+        early.append(done)
+    apart = squares
+
     squares = jnp.zeros((size, lanes), F32)
-    final = []
+    late = []
     for index in range(chunks):
         out, squares = call(
-            functools.partial(lift_kernel, height, "second"), [flat(per * size), flat(size)], [whole()] * 6,
-            (halos[index], again[index], lift_lhs, squares, lifted[index], scale), work, 2 * duals,
-        )
-        final.append(out)
+            functools.partial(outer_kernel, height), [flat(per * met), flat(size)], [whole()] * 5,
+            (halos[index], outer_lhs, inner[index], squares, apart), work, 2 * duals,
+        )
+        late.append(out)
     own, other = chan_terms(squares)
     image, spectral = synthesis(*terms, image)
 
@@ -488,8 +565,8 @@
     wavelet = call(
         functools.partial(wavelet_kernel, chunks, height),
         jax.ShapeDtypeStruct((bases, channels, height, lanes), F32),
-        [whole()] * (chunks + 3), (*final, w, own, other), rows * lanes * bases, 2 * cubes * bases,
-        scratch=[pltpu.VMEM((3, bases, slab, height, lanes), F32), pltpu.SemaphoreType.DMA((3,))],
+        [whole()] * (2 * chunks + 3), (*late, *early, w, own, other), rows * lanes * bases, 2 * cubes * bases,
+        scratch=[pltpu.VMEM((3, bases, slab, height, lanes), F32), pltpu.SemaphoreType.DMA((3, bases))],
         out_specs=distant,
     )
     return (

time: 54.9 us -> 54.4 us (level)
  waiting for transfers between devices: 13.9 us -> 12.8 us
  Pallas kernels: 18.6 us -> 19.2 us
    ppermute x4, waiting for transfers between devices: 6.29 us -> 3.23 us  [chan_pairs(): lax.ppermute(value, 'chan', [(source, source ^ stride) for source in rang...]
    ppermute x6, waiting for transfers between devices: 7.59 us -> 9.6 us  [shift(): lax.ppermute(value, axis, [(source, source + steps) for source in range(i...]
    pallas_call x17 -> x19, Pallas kernels: 18.6 us -> 19.2 us  [call(): pl.pallas_call(kernel, out_shape=outs, in_specs=ins, out_specs=out_specs...]
  transfers between devices with their start and end apart: 10 -> 10, of which waited for: 6 -> 7; matrix products, arithmetic and copies ran while one was open for 0% -> 0% of each run, Pallas kernels for 23% -> 24%
where the time goes in v7:
time: 54.4 us; the launch traced here: 54 us
  starting transfers between devices  21.1 us (39%)
  Pallas kernels  19.2 us (35%)
  waiting for transfers between devices  12.8 us (24%)
  between operations  0.88 us (2%)
    pallas_call x19, Pallas kernels, call(): pl.pallas_call(kernel, out_shape=outs, in_specs=ins, out_specs=out_specs...  19.2 us
    ppermute x6, starting transfers between devices, shift(): lax.ppermute(value, axis, [(source, source + steps) for source in range(i...  14.8 us
    ppermute x6, waiting for transfers between devices, shift(): lax.ppermute(value, axis, [(source, source + steps) for source in range(i...  9.6 us
    ppermute x4, starting transfers between devices, chan_pairs(): lax.ppermute(value, 'chan', [(source, source ^ stride) for source in rang...  6.35 us
    ppermute x4, waiting for transfers between devices, chan_pairs(): lax.ppermute(value, 'chan', [(source, source ^ stride) for source in rang...  3.23 us
  transfers between devices with their start and end apart: 10, of which 7 were waited for; matrix products, arithmetic and copies ran while one was open for 0% of the time, Pallas kernels for 24%

profile of v7, /device:TPU:16, one launch (start us, length us, event | category | flops | bytes accessed | tf_op | source)
XLA Modules:
  0.0 54.0 jit_solution(11142345891974829158)
XLA Ops:
  0.7 1.5 %shard_map.96 = (f32[1024,128]{1,0:T(8,128)S(1)}, f32[968,128]{1,0:T(8,128)S(1)}) custom-call(f32[2048,128]{1,0:T(8,128)} %bitcast.8, f32[2048,128]{1,0:T(8,128)} %bitcast.14), custom_call_target="tpu_custom_call" | custom-call | flops 524288 | bytes 1572864 | tf_op jit(solution)/shard_map/pallas_call | solution.py:419
  2.2 2.1 %collective-permute-start.1 = (f32[968,128]{1,0:T(8,128)S(1)}, f32[968,128]{1,0:T(8,128)S(1)}, u32[]{:S(2)}, u32[]{:S(2)}) collective-permute-start(f32[968,128]{1,0:T(8,128)S(1)} %get-tuple-element.50), channel_id=1, source_target_pairs={{0,2},{2,4},{4,6},{6,8},{8,10},{10,12},{12,14},{14,16},{16,18},{18... | collective-permute-start | bytes 1486856 | tf_op jit(solution)/shard_map/ppermute | solution.py:24
  4.2 1.5 %shard_map.95 = (f32[1024,128]{1,0:T(8,128)S(1)}, f32[968,128]{1,0:T(8,128)S(1)}) custom-call(f32[2048,128]{1,0:T(8,128)} %bitcast.9, f32[2048,128]{1,0:T(8,128)} %bitcast.15), custom_call_target="tpu_custom_call" | custom-call | flops 524288 | bytes 1572864 | tf_op jit(solution)/shard_map/pallas_call | solution.py:419
  5.7 3.6 %collective-permute-start = (f32[968,128]{1,0:T(8,128)S(1)}, f32[968,128]{1,0:T(8,128)S(1)}, u32[]{:S(2)}, u32[]{:S(2)}) collective-permute-start(f32[968,128]{1,0:T(8,128)S(1)} %get-tuple-element.47), channel_id=1, source_target_pairs={{0,2},{2,4},{4,6},{6,8},{8,10},{10,12},{12,14},{14,16},{16,18},{18... | collective-permute-start | bytes 1486856 | tf_op jit(solution)/shard_map/ppermute | solution.py:24
  9.4 0.9 %shard_map.94 = (bf16[128,96]{1,0:T(8,128)(2,1)S(1)}, bf16[128,48]{1,0:T(8,128)(2,1)S(1)}, bf16[96,48]{1,0:T(8,128)(2,1)S(1)}, bf16[64,96]{1,0:T(8,128)(2,1)S(1)...) custom-call(f32[8,16]{1,0:T(8,128)S(1)} %copy-done.4, ...), custom_call_target="tpu_custom_call" | custom-call | flops 100000 | bytes 100000 | tf_op jit(solution)/shard_map/pallas_call | solution.py:419
  11.0 1.6 %collective-permute-start.3 = (f32[32,2048]{1,0:T(8,128)S(1)}, f32[32,2048]{1,0:T(8,128)S(1)}, u32[]{:S(2)}, u32[]{:S(2)}) collective-permute-start(f32[32,2048]{1,0:T(8,128)S(1)} %get-tuple-element.54.own_ref), channel_id=1, source_target_pairs={{0,1},{1,0},{2,3},{3,2},{4,5},{5,4},{6,7},{7,6},{8,9},{9,8},{10,11... | collective-permute-start | bytes 786440 | tf_op jit(solution)/shard_map/ppermute | solution.py:29
  14.1 1.9 %collective-permute-start.4 = (f32[1928,128]{1,0:T(8,128)S(1)}, f32[1928,128]{1,0:T(8,128)S(1)}, u32[]{:S(2)}, u32[]{:S(2)}) collective-permute-start(f32[1928,128]{1,0:T(8,128)S(1)} %get-tuple-element.58), channel_id=1, source_target_pairs={{2,0},{4,2},{6,4},{8,6},{10,8},{12,10},{14,12},{16,14},{18,16},{20... | collective-permute-start | bytes 2961416 | tf_op jit(solution)/shard_map/ppermute | solution.py:24
  16.0 2.7 %collective-permute-done.halo_ref = f32[968,128]{1,0:T(8,128)S(1)} collective-permute-done((f32[968,128]{1,0:T(8,128)S(1)}, f32[968,128]{1,0:T(8,128)S(1)}, u32[]{:S(2)}, u32[]{:S(2)}) %collective-permute-start) | collective-permute-done | bytes 495648 | tf_op jit(solution)/shard_map/ppermute | solution.py:24
  19.5 1.6 %collective-permute-start.2 = (f32[128,128]{1,0:T(8,128)S(1)}, f32[128,128]{1,0:T(8,128)S(1)}, u32[]{:S(2)}, u32[]{:S(2)}) collective-permute-start(f32[128,128]{1,0:T(8,128)S(1)} %get-tuple-element.53.own_ref), channel_id=1, source_target_pairs={{0,1},{1,0},{2,3},{3,2},{4,5},{5,4},{6,7},{7,6},{8,9},{9,8},{10,11... | collective-permute-start | bytes 196616 | tf_op jit(solution)/shard_map/ppermute | solution.py:29
  21.5 2.3 %collective-permute-done.2.other_ref = f32[128,128]{1,0:T(8,128)S(1)} collective-permute-done((f32[128,128]{1,0:T(8,128)S(1)}, f32[128,128]{1,0:T(8,128)S(1)}, u32[]{:S(2)}, u32[]{:S(2)}) %collective-permute-start.2) | collective-permute-done | bytes 65568 | tf_op jit(solution)/shard_map/ppermute | solution.py:29
  23.8 1.9 %collective-permute-start.5 = (f32[64,128]{1,0:T(8,128)S(1)}, f32[64,128]{1,0:T(8,128)S(1)}, u32[]{:S(2)}, u32[]{:S(2)}) collective-permute-start(f32[64,128]{1,0:T(8,128)S(1)} %get-tuple-element.62), channel_id=1, source_target_pairs={{2,0},{4,2},{6,4},{8,6},{10,8},{12,10},{14,12},{16,14},{18,16},{20... | collective-permute-start | bytes 98312 | tf_op jit(solution)/shard_map/ppermute | solution.py:24
  25.8 1.1 %shard_map.104.partial_ref = f32[1024,128]{1,0:T(8,128)S(1)} custom-call(f32[8192,128]{1,0:T(8,128)S(1)} %get-tuple-element.67.dual_ref, bf16[32,256]{1,0:T(8,128)(2,1)S(1)} %get-tuple-element.64.lhs_ref, f32[128,128]{1,0:T(8,128)S(1)} %get-tuple-element.65.scale_ref, f32[2048,128]{1,0:T(8,128)S(1)} %shard_map.100.s_ref.refs_0_, f32[2048,128]{1,0:T(8,128)S(1)} %bitcast.10, ...), custom_call_target="tpu_custom_call" | custom-call | flops 4429185024 | bytes 92274688 | tf_op jit(solution)/shard_map/pallas_call | solution.py:419
  26.9 1.1 %shard_map.102.partial_ref = f32[1024,128]{1,0:T(8,128)S(1)} custom-call(f32[8192,128]{1,0:T(8,128)S(1)} %get-tuple-element.63.dual_ref, bf16[32,256]{1,0:T(8,128)(2,1)S(1)} %get-tuple-element.64.lhs_ref, f32[128,128]{1,0:T(8,128)S(1)} %get-tuple-element.65.scale_ref, f32[2048,128]{1,0:T(8,128)S(1)} %shard_map.100.s_ref.refs_0_, f32[2048,128]{1,0:T(8,128)S(1)} %bitcast.11, ...), custom_call_target="tpu_custom_call" | custom-call | flops 4429185024 | bytes 92274688 | tf_op jit(solution)/shard_map/pallas_call | solution.py:419
  28.0 0.9 %shard_map.103 = (f32[1024,128]{1,0:T(8,128)S(1)}, f32[1024,128]{1,0:T(8,128)S(1)}, f32[968,128]{1,0:T(8,128)S(1)}) custom-call(f32[1024,128]{1,0:T(8,128)S(1)} %get-tuple-element.51.own_ref.refs_0_, f32[1928,128]{1,0:T(8,128)S(1)} %collective-permute-done.4.below_ref, bf16[64,96]{1,0:T(8,128)(2,1)S(1)} %get-tuple-element.59.next_ref, ...), custom_call_target="tpu_custom_call" | custom-call | flops 4429185024 | bytes 92274688 | tf_op jit(solution)/shard_map/pallas_call | solution.py:419
  28.9 3.3 %collective-permute-start.7 = (f32[968,128]{1,0:T(8,128)S(1)}, f32[968,128]{1,0:T(8,128)S(1)}, u32[]{:S(2)}, u32[]{:S(2)}) collective-permute-start(f32[968,128]{1,0:T(8,128)S(1)} %get-tuple-element.72), channel_id=1, source_target_pairs={{0,2},{2,4},{4,6},{6,8},{8,10},{10,12},{12,14},{14,16},{16,18},{18... | collective-permute-start | bytes 1486856 | tf_op jit(solution)/shard_map/ppermute | solution.py:24
  32.3 0.9 %shard_map.105 = (f32[1024,128]{1,0:T(8,128)S(1)}, f32[1024,128]{1,0:T(8,128)S(1)}, f32[968,128]{1,0:T(8,128)S(1)}) custom-call(f32[1024,128]{1,0:T(8,128)S(1)} %get-tuple-element.48.own_ref.refs_1_, f32[1928,128]{1,0:T(8,128)S(1)} %collective-permute-done.4.below_ref, bf16[64,96]{1,0:T(8,128)(2,1)S(1)} %get-tuple-element.59.next_ref, ...), custom_call_target="tpu_custom_call" | custom-call | flops 4429185024 | bytes 92274688 | tf_op jit(solution)/shard_map/pallas_call | solution.py:419
  33.2 1.9 %collective-permute-start.8 = (f32[968,128]{1,0:T(8,128)S(1)}, f32[968,128]{1,0:T(8,128)S(1)}, u32[]{:S(2)}, u32[]{:S(2)}) collective-permute-start(f32[968,128]{1,0:T(8,128)S(1)} %get-tuple-element.79), channel_id=1, source_target_pairs={{0,2},{2,4},{4,6},{6,8},{8,10},{10,12},{12,14},{14,16},{16,18},{18... | collective-permute-start | bytes 1486856 | tf_op jit(solution)/shard_map/ppermute | solution.py:24
  36.0 1.6 %collective-permute-start.6 = (f32[32,2048]{1,0:T(8,128)S(1)}, f32[32,2048]{1,0:T(8,128)S(1)}, u32[]{:S(2)}, u32[]{:S(2)}) collective-permute-start(f32[32,2048]{1,0:T(8,128)S(1)} %shard_map.106.own_ref), channel_id=1, source_target_pairs={{0,1},{1,0},{2,3},{3,2},{4,5},{5,4},{6,7},{7,6},{8,9},{9,8},{10,11... | collective-permute-start | bytes 786440 | tf_op jit(solution)/shard_map/ppermute | solution.py:29
  39.0 1.2 %collective-permute-done.7.halo_ref = f32[968,128]{1,0:T(8,128)S(1)} collective-permute-done((f32[968,128]{1,0:T(8,128)S(1)}, f32[968,128]{1,0:T(8,128)S(1)}, u32[]{:S(2)}, u32[]{:S(2)}) %collective-permute-start.7) | collective-permute-done | bytes 495648 | tf_op jit(solution)/shard_map/ppermute | solution.py:24
  40.8 4.7 %collective-permute-done.8.halo_ref = f32[968,128]{1,0:T(8,128)S(1)} collective-permute-done((f32[968,128]{1,0:T(8,128)S(1)}, f32[968,128]{1,0:T(8,128)S(1)}, u32[]{:S(2)}, u32[]{:S(2)}) %collective-permute-start.8) | collective-permute-done | bytes 495648 | tf_op jit(solution)/shard_map/ppermute | solution.py:24
  46.1 1.6 %collective-permute-start.9 = (f32[128,128]{1,0:T(8,128)S(1)}, f32[128,128]{1,0:T(8,128)S(1)}, u32[]{:S(2)}, u32[]{:S(2)}) collective-permute-start(f32[128,128]{1,0:T(8,128)S(1)} %get-tuple-element.85.refs_5_), channel_id=1, source_target_pairs={{0,1},{1,0},{2,3},{3,2},{4,5},{5,4},{6,7},{7,6},{8,9},{9,8},{10,11... | collective-permute-start | bytes 196616 | tf_op jit(solution)/shard_map/ppermute | solution.py:29
  47.7 1.8 %shard_map.107 = (f32[2048,128]{1,0:T(8,128)}, f32[2048,128]{1,0:T(8,128)}) custom-call(bf16[128,96]{1,0:T(8,128)(2,1)S(1)} %get-tuple-element.45.lhs_ref, f32[32,2048]{1,0:T(8,128)S(1)} %shard_map.106.own_ref, f32[32,2048]{1,0:T(8,128)S(1)} %collective-permute-done.6.other_ref, f32[32,128]{1,0:T(8,128)S(1)} %get-tuple-element.55.bounds_ref, ...), custom_call_target="tpu_custom_call" | custom-call | flops 50331648 | bytes 2097152 | tf_op jit(solution)/shard_map/pallas_call | solution.py:419
  49.4 1.0 %collective-permute-done.9.refs_6_ = f32[128,128]{1,0:T(8,128)S(1)} collective-permute-done((f32[128,128]{1,0:T(8,128)S(1)}, f32[128,128]{1,0:T(8,128)S(1)}, u32[]{:S(2)}, u32[]{:S(2)}) %collective-permute-start.9) | collective-permute-done | bytes 65568 | tf_op jit(solution)/shard_map/ppermute | solution.py:29
  50.4 3.6 %shard_map.112 = f32[8,128,16,128]{3,2,1,0:T(8,128)} custom-call(f32[6144,128]{1,0:T(8,128)S(1)} %get-tuple-element.78.refs_0_, f32[6144,128]{1,0:T(8,128)S(1)} %get-tuple-element.82.refs_1_, f32[2048,128]{1,0:T(8,128)S(1)} %get-tuple-element.83.refs_2_, f32[2048,128]{1,0:T(8,128)S(1)} %get-tuple-element.84.refs_3_, f32[128,128]{1,0:T(8,128)S(1)} %bitcast.21, ...), custom_call_target="tpu_custom_call" | custom-call | flops 2097152 | bytes 16777216 | tf_op jit(solution)/shard_map/pallas_call | solution.py:419
  (31 shorter events, 6.9 us)
Async XLA Ops:
  0.6 8.7 %copy-start.6 = (s32[16]{0:T(128)S(1)}, s32[16]{0:T(128)}, u32[]{:S(2)}) copy-start(s32[16]{0:T(128)} %margin_ref.1) | copy-start | bytes 196
  0.6 8.7 %copy-start.5 = (f32[32]{0:T(128)S(1)}, f32[32]{0:T(128)}, u32[]{:S(2)}) copy-start(f32[32]{0:T(128)} %bounds_ref.1) | copy-start | bytes 388
  0.7 8.7 %copy-start.3 = (f32[1,128,32]{1,2,0:T(8,128)S(1)}, f32[1,128,32]{1,2,0:T(8,128)}, u32[]{:S(2)}) copy-start(f32[1,128,32]{1,2,0:T(8,128)} %param.11) | copy-start | bytes 49156
  0.7 8.7 %copy-start.4 = (f32[8,16]{1,0:T(8,128)S(1)}, f32[8,16]{1,0:T(8,128)}, u32[]{:S(2)}) copy-start(f32[8,16]{1,0:T(8,128)} %filters_ref.1) | copy-start | bytes 1540
  2.2 21.6 %copy-start.2 = (f32[8,16,128]{2,1,0:T(8,128)S(1)}, f32[8,16,128]{2,1,0:T(8,128)}, u32[]{:S(2)}) copy-start(f32[8,16,128]{2,1,0:T(8,128)} %param.9) | copy-start | bytes 196612
  2.2 11.2 %collective-permute-start.1 = (f32[968,128]{1,0:T(8,128)S(1)}, f32[968,128]{1,0:T(8,128)S(1)}, u32[]{:S(2)}, u32[]{:S(2)}) collective-permute-start(f32[968,128]{1,0:T(8,128)S(1)} %get-tuple-element.50), channel_id=1, source_target_pairs={{0,2},{2,4},{4,6},{6,8},{8,10},{10,12},{12,14},{14,16},{16,18},{18... | collective-permute-start | bytes 1486856 | tf_op jit(solution)/shard_map/ppermute | solution.py:24
  5.7 20.1 %copy-start = (f32[128,16,128]{2,1,0:T(8,128)S(1)}, f32[128,16,128]{2,1,0:T(8,128)}, u32[]{:S(2)}) copy-start(f32[128,16,128]{2,1,0:T(8,128)} %param.7) | copy-start | bytes 3145732
  5.7 20.1 %copy-start.1 = (f32[128,16,128]{2,1,0:T(8,128)S(1)}, f32[128,16,128]{2,1,0:T(8,128)}, u32[]{:S(2)}) copy-start(f32[128,16,128]{2,1,0:T(8,128)} %param.8) | copy-start | bytes 3145732
  5.7 13.0 %collective-permute-start = (f32[968,128]{1,0:T(8,128)S(1)}, f32[968,128]{1,0:T(8,128)S(1)}, u32[]{:S(2)}, u32[]{:S(2)}) collective-permute-start(f32[968,128]{1,0:T(8,128)S(1)} %get-tuple-element.47), channel_id=1, source_target_pairs={{0,2},{2,4},{4,6},{6,8},{8,10},{10,12},{12,14},{14,16},{16,18},{18... | collective-permute-start | bytes 1486856 | tf_op jit(solution)/shard_map/ppermute | solution.py:24
  11.0 10.1 %collective-permute-start.3 = (f32[32,2048]{1,0:T(8,128)S(1)}, f32[32,2048]{1,0:T(8,128)S(1)}, u32[]{:S(2)}, u32[]{:S(2)}) collective-permute-start(f32[32,2048]{1,0:T(8,128)S(1)} %get-tuple-element.54.own_ref), channel_id=1, source_target_pairs={{0,1},{1,0},{2,3},{3,2},{4,5},{5,4},{6,7},{7,6},{8,9},{9,8},{10,11... | collective-permute-start | bytes 786440 | tf_op jit(solution)/shard_map/ppermute | solution.py:29
  14.1 13.9 %collective-permute-start.4 = (f32[1928,128]{1,0:T(8,128)S(1)}, f32[1928,128]{1,0:T(8,128)S(1)}, u32[]{:S(2)}, u32[]{:S(2)}) collective-permute-start(f32[1928,128]{1,0:T(8,128)S(1)} %get-tuple-element.58), channel_id=1, source_target_pairs={{2,0},{4,2},{6,4},{8,6},{10,8},{12,10},{14,12},{16,14},{18,16},{20... | collective-permute-start | bytes 2961416 | tf_op jit(solution)/shard_map/ppermute | solution.py:24
  19.5 4.3 %collective-permute-start.2 = (f32[128,128]{1,0:T(8,128)S(1)}, f32[128,128]{1,0:T(8,128)S(1)}, u32[]{:S(2)}, u32[]{:S(2)}) collective-permute-start(f32[128,128]{1,0:T(8,128)S(1)} %get-tuple-element.53.own_ref), channel_id=1, source_target_pairs={{0,1},{1,0},{2,3},{3,2},{4,5},{5,4},{6,7},{7,6},{8,9},{9,8},{10,11... | collective-permute-start | bytes 196616 | tf_op jit(solution)/shard_map/ppermute | solution.py:29
  23.8 4.2 %collective-permute-start.5 = (f32[64,128]{1,0:T(8,128)S(1)}, f32[64,128]{1,0:T(8,128)S(1)}, u32[]{:S(2)}, u32[]{:S(2)}) collective-permute-start(f32[64,128]{1,0:T(8,128)S(1)} %get-tuple-element.62), channel_id=1, source_target_pairs={{2,0},{4,2},{6,4},{8,6},{10,8},{12,10},{14,12},{16,14},{18,16},{20... | collective-permute-start | bytes 98312 | tf_op jit(solution)/shard_map/ppermute | solution.py:24
  28.9 11.3 %collective-permute-start.7 = (f32[968,128]{1,0:T(8,128)S(1)}, f32[968,128]{1,0:T(8,128)S(1)}, u32[]{:S(2)}, u32[]{:S(2)}) collective-permute-start(f32[968,128]{1,0:T(8,128)S(1)} %get-tuple-element.72), channel_id=1, source_target_pairs={{0,2},{2,4},{4,6},{6,8},{8,10},{10,12},{12,14},{14,16},{16,18},{18... | collective-permute-start | bytes 1486856 | tf_op jit(solution)/shard_map/ppermute | solution.py:24
  33.2 12.3 %collective-permute-start.8 = (f32[968,128]{1,0:T(8,128)S(1)}, f32[968,128]{1,0:T(8,128)S(1)}, u32[]{:S(2)}, u32[]{:S(2)}) collective-permute-start(f32[968,128]{1,0:T(8,128)S(1)} %get-tuple-element.79), channel_id=1, source_target_pairs={{0,2},{2,4},{4,6},{6,8},{8,10},{10,12},{12,14},{14,16},{16,18},{18... | collective-permute-start | bytes 1486856 | tf_op jit(solution)/shard_map/ppermute | solution.py:24
  36.0 11.7 %collective-permute-start.6 = (f32[32,2048]{1,0:T(8,128)S(1)}, f32[32,2048]{1,0:T(8,128)S(1)}, u32[]{:S(2)}, u32[]{:S(2)}) collective-permute-start(f32[32,2048]{1,0:T(8,128)S(1)} %shard_map.106.own_ref), channel_id=1, source_target_pairs={{0,1},{1,0},{2,3},{3,2},{4,5},{5,4},{6,7},{7,6},{8,9},{9,8},{10,11... | collective-permute-start | bytes 786440 | tf_op jit(solution)/shard_map/ppermute | solution.py:29
  46.1 4.3 %collective-permute-start.9 = (f32[128,128]{1,0:T(8,128)S(1)}, f32[128,128]{1,0:T(8,128)S(1)}, u32[]{:S(2)}, u32[]{:S(2)}) collective-permute-start(f32[128,128]{1,0:T(8,128)S(1)} %get-tuple-element.85.refs_5_), channel_id=1, source_target_pairs={{0,1},{1,0},{2,3},{3,2},{4,5},{5,4},{6,7},{7,6},{8,9},{9,8},{10,11... | collective-permute-start | bytes 196616 | tf_op jit(solution)/shard_map/ppermute | solution.py:29

commit v8 on v7

--- a/solution.py
+++ b/solution.py
@@ -14,6 +14,7 @@
 CHUNKS = 2
 GROUP = 32
 PAD = 8
+STEPS = 2
 VMEM_LIMIT = 24 << 20
 REFLECT_LIMIT = 55000000
 
@@ -152,20 +153,29 @@
 
 
 def reflect_kernel(height, start, x_ref, d_ref, r_ref, packed_ref, x_buffer, d_buffer, sems):
-    rows = pl.ds(start, r_ref.shape[0])
-    copies = [
-        pltpu.make_async_copy(source.at[rows], target, sems.at[turn])
-        for turn, (source, target) in enumerate(((x_ref, x_buffer), (d_ref, d_buffer)))
-    ]
-    for copy in copies:
-        copy.start()
-    for copy in copies:
-        copy.wait()
-    x = x_buffer[...]
-    updated = jnp.maximum(x - PRIMAL * (x - d_buffer[...]), 0.0)
-    r_ref[...] = 2.0 * updated - x
-    pack(r_ref, packed_ref, height, 1)
+    steps = sems.shape[0]
+    block = r_ref.shape[0] // steps
+    copies = []
+    for step in range(steps):
+        here = pl.ds(step * block, block)
+        there = pl.ds(start + step * block, block)
+        copies.append(
+            [
+                pltpu.make_async_copy(source.at[there], target.at[here], sems.at[step, turn])
+                for turn, (source, target) in enumerate(((x_ref, x_buffer), (d_ref, d_buffer)))
+            ]
+        )
+        for copy in copies[-1]:
+            copy.start()
     clear_tail(packed_ref)
+    for step in range(steps):
+        for copy in copies[step]:
+            copy.wait()
+        here = pl.ds(step * block, block)
+        x = x_buffer[here, :]
+        updated = jnp.maximum(x - PRIMAL * (x - d_buffer[here, :]), 0.0)
+        r_ref[here, :] = 2.0 * updated - x
+        pack(r_ref.at[here], packed_ref, height, 1, step * (block // height) * (height - 1))
 
 
 def coef_kernel(height, spectral, lhs_ref, *refs):
@@ -463,7 +473,7 @@
         r, ahead = call(
             functools.partial(reflect_kernel, height, index * block), [flat(block), flat(packed)], [distant] * 2, (x, d),
             4 * block * lanes, 12 * block * lanes,
-            scratch=[pltpu.VMEM((block, lanes), F32)] * 2 + [pltpu.SemaphoreType.DMA((2,))], limit=REFLECT_LIMIT,
+            scratch=[pltpu.VMEM((block, lanes), F32)] * 2 + [pltpu.SemaphoreType.DMA((STEPS, 2))], limit=REFLECT_LIMIT,
         )
         reflected.append(r)
         halos.append(shift(ahead, "facet", 1))

time: 54.4 us -> 54.2 us (level)
  no operation moved by 1% of the time
where the time goes in v8:
time: 54.2 us; the launch traced here: 53.9 us
  starting transfers between devices  21.1 us (39%)
  Pallas kernels  18.9 us (35%)
  waiting for transfers between devices  13 us (24%)
  between operations  0.88 us (2%)
    pallas_call x19, Pallas kernels, call(): pl.pallas_call(kernel, out_shape=outs, in_specs=ins, out_specs=out_specs...  18.9 us
    ppermute x6, starting transfers between devices, shift(): lax.ppermute(value, axis, [(source, source + steps) for source in range(i...  14.8 us
    ppermute x6, waiting for transfers between devices, shift(): lax.ppermute(value, axis, [(source, source + steps) for source in range(i...  9.74 us
    ppermute x4, starting transfers between devices, chan_pairs(): lax.ppermute(value, 'chan', [(source, source ^ stride) for source in rang...  6.34 us
    ppermute x4, waiting for transfers between devices, chan_pairs(): lax.ppermute(value, 'chan', [(source, source ^ stride) for source in rang...  3.24 us
  transfers between devices with their start and end apart: 10, of which 7 were waited for; matrix products, arithmetic and copies ran while one was open for 0% of the time, Pallas kernels for 24%

profile of v8, /device:TPU:16, one launch (start us, length us, event | category | flops | bytes accessed | tf_op | source)
XLA Modules:
  0.0 53.9 jit_solution(766055293772852083)
XLA Ops:
  0.7 1.4 %shard_map.96 = (f32[1024,128]{1,0:T(8,128)S(1)}, f32[968,128]{1,0:T(8,128)S(1)}) custom-call(f32[2048,128]{1,0:T(8,128)} %bitcast.8, f32[2048,128]{1,0:T(8,128)} %bitcast.14), custom_call_target="tpu_custom_call" | custom-call | flops 524288 | bytes 1572864 | tf_op jit(solution)/shard_map/pallas_call | solution.py:429
  2.0 2.1 %collective-permute-start.1 = (f32[968,128]{1,0:T(8,128)S(1)}, f32[968,128]{1,0:T(8,128)S(1)}, u32[]{:S(2)}, u32[]{:S(2)}) collective-permute-start(f32[968,128]{1,0:T(8,128)S(1)} %get-tuple-element.50), channel_id=1, source_target_pairs={{0,2},{2,4},{4,6},{6,8},{8,10},{10,12},{12,14},{14,16},{16,18},{18... | collective-permute-start | bytes 1486856 | tf_op jit(solution)/shard_map/ppermute | solution.py:25
  4.1 1.3 %shard_map.95 = (f32[1024,128]{1,0:T(8,128)S(1)}, f32[968,128]{1,0:T(8,128)S(1)}) custom-call(f32[2048,128]{1,0:T(8,128)} %bitcast.9, f32[2048,128]{1,0:T(8,128)} %bitcast.15), custom_call_target="tpu_custom_call" | custom-call | flops 524288 | bytes 1572864 | tf_op jit(solution)/shard_map/pallas_call | solution.py:429
  5.5 3.6 %collective-permute-start = (f32[968,128]{1,0:T(8,128)S(1)}, f32[968,128]{1,0:T(8,128)S(1)}, u32[]{:S(2)}, u32[]{:S(2)}) collective-permute-start(f32[968,128]{1,0:T(8,128)S(1)} %get-tuple-element.47), channel_id=1, source_target_pairs={{0,2},{2,4},{4,6},{6,8},{8,10},{10,12},{12,14},{14,16},{16,18},{18... | collective-permute-start | bytes 1486856 | tf_op jit(solution)/shard_map/ppermute | solution.py:25
  9.2 0.9 %shard_map.94 = (bf16[128,96]{1,0:T(8,128)(2,1)S(1)}, bf16[128,48]{1,0:T(8,128)(2,1)S(1)}, bf16[96,48]{1,0:T(8,128)(2,1)S(1)}, bf16[64,96]{1,0:T(8,128)(2,1)S(1)...) custom-call(f32[8,16]{1,0:T(8,128)S(1)} %copy-done.4, ...), custom_call_target="tpu_custom_call" | custom-call | flops 100000 | bytes 100000 | tf_op jit(solution)/shard_map/pallas_call | solution.py:429
  10.7 1.6 %collective-permute-start.3 = (f32[32,2048]{1,0:T(8,128)S(1)}, f32[32,2048]{1,0:T(8,128)S(1)}, u32[]{:S(2)}, u32[]{:S(2)}) collective-permute-start(f32[32,2048]{1,0:T(8,128)S(1)} %get-tuple-element.54.own_ref), channel_id=1, source_target_pairs={{0,1},{1,0},{2,3},{3,2},{4,5},{5,4},{6,7},{7,6},{8,9},{9,8},{10,11... | collective-permute-start | bytes 786440 | tf_op jit(solution)/shard_map/ppermute | solution.py:30
  12.3 1.0 %collective-permute-done.1.halo_ref = f32[968,128]{1,0:T(8,128)S(1)} collective-permute-done((f32[968,128]{1,0:T(8,128)S(1)}, f32[968,128]{1,0:T(8,128)S(1)}, u32[]{:S(2)}, u32[]{:S(2)}) %collective-permute-start.1) | collective-permute-done | bytes 495648 | tf_op jit(solution)/shard_map/ppermute | solution.py:25
  14.0 1.9 %collective-permute-start.4 = (f32[1928,128]{1,0:T(8,128)S(1)}, f32[1928,128]{1,0:T(8,128)S(1)}, u32[]{:S(2)}, u32[]{:S(2)}) collective-permute-start(f32[1928,128]{1,0:T(8,128)S(1)} %get-tuple-element.58), channel_id=1, source_target_pairs={{2,0},{4,2},{6,4},{8,6},{10,8},{12,10},{14,12},{16,14},{18,16},{20... | collective-permute-start | bytes 2961416 | tf_op jit(solution)/shard_map/ppermute | solution.py:25
  15.9 2.7 %collective-permute-done.halo_ref = f32[968,128]{1,0:T(8,128)S(1)} collective-permute-done((f32[968,128]{1,0:T(8,128)S(1)}, f32[968,128]{1,0:T(8,128)S(1)}, u32[]{:S(2)}, u32[]{:S(2)}) %collective-permute-start) | collective-permute-done | bytes 495648 | tf_op jit(solution)/shard_map/ppermute | solution.py:25
  19.3 1.6 %collective-permute-start.2 = (f32[128,128]{1,0:T(8,128)S(1)}, f32[128,128]{1,0:T(8,128)S(1)}, u32[]{:S(2)}, u32[]{:S(2)}) collective-permute-start(f32[128,128]{1,0:T(8,128)S(1)} %get-tuple-element.53.own_ref), channel_id=1, source_target_pairs={{0,1},{1,0},{2,3},{3,2},{4,5},{5,4},{6,7},{7,6},{8,9},{9,8},{10,11... | collective-permute-start | bytes 196616 | tf_op jit(solution)/shard_map/ppermute | solution.py:30
  21.4 2.3 %collective-permute-done.2.other_ref = f32[128,128]{1,0:T(8,128)S(1)} collective-permute-done((f32[128,128]{1,0:T(8,128)S(1)}, f32[128,128]{1,0:T(8,128)S(1)}, u32[]{:S(2)}, u32[]{:S(2)}) %collective-permute-start.2) | collective-permute-done | bytes 65568 | tf_op jit(solution)/shard_map/ppermute | solution.py:30
  23.7 1.9 %collective-permute-start.5 = (f32[64,128]{1,0:T(8,128)S(1)}, f32[64,128]{1,0:T(8,128)S(1)}, u32[]{:S(2)}, u32[]{:S(2)}) collective-permute-start(f32[64,128]{1,0:T(8,128)S(1)} %get-tuple-element.62), channel_id=1, source_target_pairs={{2,0},{4,2},{6,4},{8,6},{10,8},{12,10},{14,12},{16,14},{18,16},{20... | collective-permute-start | bytes 98312 | tf_op jit(solution)/shard_map/ppermute | solution.py:25
  25.7 1.1 %shard_map.104.partial_ref = f32[1024,128]{1,0:T(8,128)S(1)} custom-call(f32[8192,128]{1,0:T(8,128)S(1)} %get-tuple-element.67.dual_ref, bf16[32,256]{1,0:T(8,128)(2,1)S(1)} %get-tuple-element.64.lhs_ref, f32[128,128]{1,0:T(8,128)S(1)} %get-tuple-element.65.scale_ref, f32[2048,128]{1,0:T(8,128)S(1)} %shard_map.100.s_ref.refs_0_, f32[2048,128]{1,0:T(8,128)S(1)} %bitcast.10, ...), custom_call_target="tpu_custom_call" | custom-call | flops 4429185024 | bytes 92274688 | tf_op jit(solution)/shard_map/pallas_call | solution.py:429
  26.7 1.1 %shard_map.102.partial_ref = f32[1024,128]{1,0:T(8,128)S(1)} custom-call(f32[8192,128]{1,0:T(8,128)S(1)} %get-tuple-element.63.dual_ref, bf16[32,256]{1,0:T(8,128)(2,1)S(1)} %get-tuple-element.64.lhs_ref, f32[128,128]{1,0:T(8,128)S(1)} %get-tuple-element.65.scale_ref, f32[2048,128]{1,0:T(8,128)S(1)} %shard_map.100.s_ref.refs_0_, f32[2048,128]{1,0:T(8,128)S(1)} %bitcast.11, ...), custom_call_target="tpu_custom_call" | custom-call | flops 4429185024 | bytes 92274688 | tf_op jit(solution)/shard_map/pallas_call | solution.py:429
  27.9 0.9 %shard_map.103 = (f32[1024,128]{1,0:T(8,128)S(1)}, f32[1024,128]{1,0:T(8,128)S(1)}, f32[968,128]{1,0:T(8,128)S(1)}) custom-call(f32[1024,128]{1,0:T(8,128)S(1)} %get-tuple-element.51.own_ref.refs_0_, f32[1928,128]{1,0:T(8,128)S(1)} %collective-permute-done.4.below_ref, bf16[64,96]{1,0:T(8,128)(2,1)S(1)} %get-tuple-element.59.next_ref, ...), custom_call_target="tpu_custom_call" | custom-call | flops 4429185024 | bytes 92274688 | tf_op jit(solution)/shard_map/pallas_call | solution.py:429
  28.8 3.3 %collective-permute-start.7 = (f32[968,128]{1,0:T(8,128)S(1)}, f32[968,128]{1,0:T(8,128)S(1)}, u32[]{:S(2)}, u32[]{:S(2)}) collective-permute-start(f32[968,128]{1,0:T(8,128)S(1)} %get-tuple-element.72), channel_id=1, source_target_pairs={{0,2},{2,4},{4,6},{6,8},{8,10},{10,12},{12,14},{14,16},{16,18},{18... | collective-permute-start | bytes 1486856 | tf_op jit(solution)/shard_map/ppermute | solution.py:25
  33.0 1.9 %collective-permute-start.8 = (f32[968,128]{1,0:T(8,128)S(1)}, f32[968,128]{1,0:T(8,128)S(1)}, u32[]{:S(2)}, u32[]{:S(2)}) collective-permute-start(f32[968,128]{1,0:T(8,128)S(1)} %get-tuple-element.79), channel_id=1, source_target_pairs={{0,2},{2,4},{4,6},{6,8},{8,10},{10,12},{12,14},{14,16},{16,18},{18... | collective-permute-start | bytes 1486856 | tf_op jit(solution)/shard_map/ppermute | solution.py:25
  35.9 1.6 %collective-permute-start.6 = (f32[32,2048]{1,0:T(8,128)S(1)}, f32[32,2048]{1,0:T(8,128)S(1)}, u32[]{:S(2)}, u32[]{:S(2)}) collective-permute-start(f32[32,2048]{1,0:T(8,128)S(1)} %shard_map.106.own_ref), channel_id=1, source_target_pairs={{0,1},{1,0},{2,3},{3,2},{4,5},{5,4},{6,7},{7,6},{8,9},{9,8},{10,11... | collective-permute-start | bytes 786440 | tf_op jit(solution)/shard_map/ppermute | solution.py:30
  38.9 1.2 %collective-permute-done.7.halo_ref = f32[968,128]{1,0:T(8,128)S(1)} collective-permute-done((f32[968,128]{1,0:T(8,128)S(1)}, f32[968,128]{1,0:T(8,128)S(1)}, u32[]{:S(2)}, u32[]{:S(2)}) %collective-permute-start.7) | collective-permute-done | bytes 495648 | tf_op jit(solution)/shard_map/ppermute | solution.py:25
  40.6 4.7 %collective-permute-done.8.halo_ref = f32[968,128]{1,0:T(8,128)S(1)} collective-permute-done((f32[968,128]{1,0:T(8,128)S(1)}, f32[968,128]{1,0:T(8,128)S(1)}, u32[]{:S(2)}, u32[]{:S(2)}) %collective-permute-start.8) | collective-permute-done | bytes 495648 | tf_op jit(solution)/shard_map/ppermute | solution.py:25
  46.0 1.6 %collective-permute-start.9 = (f32[128,128]{1,0:T(8,128)S(1)}, f32[128,128]{1,0:T(8,128)S(1)}, u32[]{:S(2)}, u32[]{:S(2)}) collective-permute-start(f32[128,128]{1,0:T(8,128)S(1)} %get-tuple-element.85.refs_5_), channel_id=1, source_target_pairs={{0,1},{1,0},{2,3},{3,2},{4,5},{5,4},{6,7},{7,6},{8,9},{9,8},{10,11... | collective-permute-start | bytes 196616 | tf_op jit(solution)/shard_map/ppermute | solution.py:30
  47.5 1.8 %shard_map.107 = (f32[2048,128]{1,0:T(8,128)}, f32[2048,128]{1,0:T(8,128)}) custom-call(bf16[128,96]{1,0:T(8,128)(2,1)S(1)} %get-tuple-element.45.lhs_ref, f32[32,2048]{1,0:T(8,128)S(1)} %shard_map.106.own_ref, f32[32,2048]{1,0:T(8,128)S(1)} %collective-permute-done.6.other_ref, f32[32,128]{1,0:T(8,128)S(1)} %get-tuple-element.55.bounds_ref, ...), custom_call_target="tpu_custom_call" | custom-call | flops 50331648 | bytes 2097152 | tf_op jit(solution)/shard_map/pallas_call | solution.py:429
  49.3 1.0 %collective-permute-done.9.refs_6_ = f32[128,128]{1,0:T(8,128)S(1)} collective-permute-done((f32[128,128]{1,0:T(8,128)S(1)}, f32[128,128]{1,0:T(8,128)S(1)}, u32[]{:S(2)}, u32[]{:S(2)}) %collective-permute-start.9) | collective-permute-done | bytes 65568 | tf_op jit(solution)/shard_map/ppermute | solution.py:30
  50.3 3.6 %shard_map.112 = f32[8,128,16,128]{3,2,1,0:T(8,128)} custom-call(f32[6144,128]{1,0:T(8,128)S(1)} %get-tuple-element.78.refs_0_, f32[6144,128]{1,0:T(8,128)S(1)} %get-tuple-element.82.refs_1_, f32[2048,128]{1,0:T(8,128)S(1)} %get-tuple-element.83.refs_2_, f32[2048,128]{1,0:T(8,128)S(1)} %get-tuple-element.84.refs_3_, f32[128,128]{1,0:T(8,128)S(1)} %bitcast.21, ...), custom_call_target="tpu_custom_call" | custom-call | flops 2097152 | bytes 16777216 | tf_op jit(solution)/shard_map/pallas_call | solution.py:429
  (31 shorter events, 7.0 us)
Async XLA Ops:
  0.6 8.5 %copy-start.6 = (s32[16]{0:T(128)S(1)}, s32[16]{0:T(128)}, u32[]{:S(2)}) copy-start(s32[16]{0:T(128)} %margin_ref.1) | copy-start | bytes 196
  0.6 8.5 %copy-start.5 = (f32[32]{0:T(128)S(1)}, f32[32]{0:T(128)}, u32[]{:S(2)}) copy-start(f32[32]{0:T(128)} %bounds_ref.1) | copy-start | bytes 388
  0.7 8.5 %copy-start.3 = (f32[1,128,32]{1,2,0:T(8,128)S(1)}, f32[1,128,32]{1,2,0:T(8,128)}, u32[]{:S(2)}) copy-start(f32[1,128,32]{1,2,0:T(8,128)} %param.11) | copy-start | bytes 49156
  0.7 8.5 %copy-start.4 = (f32[8,16]{1,0:T(8,128)S(1)}, f32[8,16]{1,0:T(8,128)}, u32[]{:S(2)}) copy-start(f32[8,16]{1,0:T(8,128)} %filters_ref.1) | copy-start | bytes 1540
  2.0 21.6 %copy-start.2 = (f32[8,16,128]{2,1,0:T(8,128)S(1)}, f32[8,16,128]{2,1,0:T(8,128)}, u32[]{:S(2)}) copy-start(f32[8,16,128]{2,1,0:T(8,128)} %param.9) | copy-start | bytes 196612
  2.0 11.2 %collective-permute-start.1 = (f32[968,128]{1,0:T(8,128)S(1)}, f32[968,128]{1,0:T(8,128)S(1)}, u32[]{:S(2)}, u32[]{:S(2)}) collective-permute-start(f32[968,128]{1,0:T(8,128)S(1)} %get-tuple-element.50), channel_id=1, source_target_pairs={{0,2},{2,4},{4,6},{6,8},{8,10},{10,12},{12,14},{14,16},{16,18},{18... | collective-permute-start | bytes 1486856 | tf_op jit(solution)/shard_map/ppermute | solution.py:25
  5.4 20.2 %copy-start = (f32[128,16,128]{2,1,0:T(8,128)S(1)}, f32[128,16,128]{2,1,0:T(8,128)}, u32[]{:S(2)}) copy-start(f32[128,16,128]{2,1,0:T(8,128)} %param.7) | copy-start | bytes 3145732
  5.5 20.2 %copy-start.1 = (f32[128,16,128]{2,1,0:T(8,128)S(1)}, f32[128,16,128]{2,1,0:T(8,128)}, u32[]{:S(2)}) copy-start(f32[128,16,128]{2,1,0:T(8,128)} %param.8) | copy-start | bytes 3145732
  5.5 13.2 %collective-permute-start = (f32[968,128]{1,0:T(8,128)S(1)}, f32[968,128]{1,0:T(8,128)S(1)}, u32[]{:S(2)}, u32[]{:S(2)}) collective-permute-start(f32[968,128]{1,0:T(8,128)S(1)} %get-tuple-element.47), channel_id=1, source_target_pairs={{0,2},{2,4},{4,6},{6,8},{8,10},{10,12},{12,14},{14,16},{16,18},{18... | collective-permute-start | bytes 1486856 | tf_op jit(solution)/shard_map/ppermute | solution.py:25
  10.7 10.2 %collective-permute-start.3 = (f32[32,2048]{1,0:T(8,128)S(1)}, f32[32,2048]{1,0:T(8,128)S(1)}, u32[]{:S(2)}, u32[]{:S(2)}) collective-permute-start(f32[32,2048]{1,0:T(8,128)S(1)} %get-tuple-element.54.own_ref), channel_id=1, source_target_pairs={{0,1},{1,0},{2,3},{3,2},{4,5},{5,4},{6,7},{7,6},{8,9},{9,8},{10,11... | collective-permute-start | bytes 786440 | tf_op jit(solution)/shard_map/ppermute | solution.py:30
  14.0 13.9 %collective-permute-start.4 = (f32[1928,128]{1,0:T(8,128)S(1)}, f32[1928,128]{1,0:T(8,128)S(1)}, u32[]{:S(2)}, u32[]{:S(2)}) collective-permute-start(f32[1928,128]{1,0:T(8,128)S(1)} %get-tuple-element.58), channel_id=1, source_target_pairs={{2,0},{4,2},{6,4},{8,6},{10,8},{12,10},{14,12},{16,14},{18,16},{20... | collective-permute-start | bytes 2961416 | tf_op jit(solution)/shard_map/ppermute | solution.py:25
  19.3 4.3 %collective-permute-start.2 = (f32[128,128]{1,0:T(8,128)S(1)}, f32[128,128]{1,0:T(8,128)S(1)}, u32[]{:S(2)}, u32[]{:S(2)}) collective-permute-start(f32[128,128]{1,0:T(8,128)S(1)} %get-tuple-element.53.own_ref), channel_id=1, source_target_pairs={{0,1},{1,0},{2,3},{3,2},{4,5},{5,4},{6,7},{7,6},{8,9},{9,8},{10,11... | collective-permute-start | bytes 196616 | tf_op jit(solution)/shard_map/ppermute | solution.py:30
  23.7 4.2 %collective-permute-start.5 = (f32[64,128]{1,0:T(8,128)S(1)}, f32[64,128]{1,0:T(8,128)S(1)}, u32[]{:S(2)}, u32[]{:S(2)}) collective-permute-start(f32[64,128]{1,0:T(8,128)S(1)} %get-tuple-element.62), channel_id=1, source_target_pairs={{2,0},{4,2},{6,4},{8,6},{10,8},{12,10},{14,12},{16,14},{18,16},{20... | collective-permute-start | bytes 98312 | tf_op jit(solution)/shard_map/ppermute | solution.py:25
  28.8 11.3 %collective-permute-start.7 = (f32[968,128]{1,0:T(8,128)S(1)}, f32[968,128]{1,0:T(8,128)S(1)}, u32[]{:S(2)}, u32[]{:S(2)}) collective-permute-start(f32[968,128]{1,0:T(8,128)S(1)} %get-tuple-element.72), channel_id=1, source_target_pairs={{0,2},{2,4},{4,6},{6,8},{8,10},{10,12},{12,14},{14,16},{16,18},{18... | collective-permute-start | bytes 1486856 | tf_op jit(solution)/shard_map/ppermute | solution.py:25
  33.0 12.3 %collective-permute-start.8 = (f32[968,128]{1,0:T(8,128)S(1)}, f32[968,128]{1,0:T(8,128)S(1)}, u32[]{:S(2)}, u32[]{:S(2)}) collective-permute-start(f32[968,128]{1,0:T(8,128)S(1)} %get-tuple-element.79), channel_id=1, source_target_pairs={{0,2},{2,4},{4,6},{6,8},{8,10},{10,12},{12,14},{14,16},{16,18},{18... | collective-permute-start | bytes 1486856 | tf_op jit(solution)/shard_map/ppermute | solution.py:25
  35.9 11.7 %collective-permute-start.6 = (f32[32,2048]{1,0:T(8,128)S(1)}, f32[32,2048]{1,0:T(8,128)S(1)}, u32[]{:S(2)}, u32[]{:S(2)}) collective-permute-start(f32[32,2048]{1,0:T(8,128)S(1)} %shard_map.106.own_ref), channel_id=1, source_target_pairs={{0,1},{1,0},{2,3},{3,2},{4,5},{5,4},{6,7},{7,6},{8,9},{9,8},{10,11... | collective-permute-start | bytes 786440 | tf_op jit(solution)/shard_map/ppermute | solution.py:30
  46.0 4.3 %collective-permute-start.9 = (f32[128,128]{1,0:T(8,128)S(1)}, f32[128,128]{1,0:T(8,128)S(1)}, u32[]{:S(2)}, u32[]{:S(2)}) collective-permute-start(f32[128,128]{1,0:T(8,128)S(1)} %get-tuple-element.85.refs_5_), channel_id=1, source_target_pairs={{0,1},{1,0},{2,3},{3,2},{4,5},{5,4},{6,7},{7,6},{8,9},{9,8},{10,11... | collective-permute-start | bytes 196616 | tf_op jit(solution)/shard_map/ppermute | solution.py:30

commit v9 on v8

--- a/solution.py
+++ b/solution.py
@@ -12,7 +12,7 @@
 F32 = jnp.float32
 BF16 = jnp.bfloat16
 CHUNKS = 2
-GROUP = 32
+GROUP = 64
 PAD = 8
 STEPS = 2
 VMEM_LIMIT = 24 << 20

time: 54.2 us -> 54.4 us (level)
  no operation moved by 1% of the time
where the time goes in v9:
time: 54.4 us; the launch traced here: 54.1 us
  starting transfers between devices  21.3 us (39%)
  Pallas kernels  18.7 us (34%)
  waiting for transfers between devices  12.9 us (24%)
  between operations  1.04 us (2%)
    pallas_call x19, Pallas kernels, call(): pl.pallas_call(kernel, out_shape=outs, in_specs=ins, out_specs=out_specs...  18.7 us
    ppermute x6, starting transfers between devices, shift(): lax.ppermute(value, axis, [(source, source + steps) for source in range(i...  15 us
    ppermute x6, waiting for transfers between devices, shift(): lax.ppermute(value, axis, [(source, source + steps) for source in range(i...  9.72 us
    ppermute x4, starting transfers between devices, chan_pairs(): lax.ppermute(value, 'chan', [(source, source ^ stride) for source in rang...  6.35 us
    ppermute x4, waiting for transfers between devices, chan_pairs(): lax.ppermute(value, 'chan', [(source, source ^ stride) for source in rang...  3.23 us
  transfers between devices with their start and end apart: 10, of which 7 were waited for; matrix products, arithmetic and copies ran while one was open for 0% of the time, Pallas kernels for 24%

profile of v9, /device:TPU:16, one launch (start us, length us, event | category | flops | bytes accessed | tf_op | source)
XLA Modules:
  0.0 54.1 jit_solution(16856496739714359907)
XLA Ops:
  0.7 1.4 %shard_map.96 = (f32[1024,128]{1,0:T(8,128)S(1)}, f32[968,128]{1,0:T(8,128)S(1)}) custom-call(f32[2048,128]{1,0:T(8,128)} %bitcast.8, f32[2048,128]{1,0:T(8,128)} %bitcast.14), custom_call_target="tpu_custom_call" | custom-call | flops 524288 | bytes 1572864 | tf_op jit(solution)/shard_map/pallas_call | solution.py:429
  2.0 2.1 %collective-permute-start.1 = (f32[968,128]{1,0:T(8,128)S(1)}, f32[968,128]{1,0:T(8,128)S(1)}, u32[]{:S(2)}, u32[]{:S(2)}) collective-permute-start(f32[968,128]{1,0:T(8,128)S(1)} %get-tuple-element.50), channel_id=1, source_target_pairs={{0,2},{2,4},{4,6},{6,8},{8,10},{10,12},{12,14},{14,16},{16,18},{18... | collective-permute-start | bytes 1486856 | tf_op jit(solution)/shard_map/ppermute | solution.py:25
  4.1 1.3 %shard_map.95 = (f32[1024,128]{1,0:T(8,128)S(1)}, f32[968,128]{1,0:T(8,128)S(1)}) custom-call(f32[2048,128]{1,0:T(8,128)} %bitcast.9, f32[2048,128]{1,0:T(8,128)} %bitcast.15), custom_call_target="tpu_custom_call" | custom-call | flops 524288 | bytes 1572864 | tf_op jit(solution)/shard_map/pallas_call | solution.py:429
  5.5 3.6 %collective-permute-start = (f32[968,128]{1,0:T(8,128)S(1)}, f32[968,128]{1,0:T(8,128)S(1)}, u32[]{:S(2)}, u32[]{:S(2)}) collective-permute-start(f32[968,128]{1,0:T(8,128)S(1)} %get-tuple-element.47), channel_id=1, source_target_pairs={{0,2},{2,4},{4,6},{6,8},{8,10},{10,12},{12,14},{14,16},{16,18},{18... | collective-permute-start | bytes 1486856 | tf_op jit(solution)/shard_map/ppermute | solution.py:25
  9.2 0.9 %shard_map.94 = (bf16[128,96]{1,0:T(8,128)(2,1)S(1)}, bf16[128,48]{1,0:T(8,128)(2,1)S(1)}, bf16[96,48]{1,0:T(8,128)(2,1)S(1)}, bf16[64,96]{1,0:T(8,128)(2,1)S(1)...) custom-call(f32[8,16]{1,0:T(8,128)S(1)} %copy-done.4, ...), custom_call_target="tpu_custom_call" | custom-call | flops 100000 | bytes 100000 | tf_op jit(solution)/shard_map/pallas_call | solution.py:429
  10.7 1.6 %collective-permute-start.3 = (f32[32,2048]{1,0:T(8,128)S(1)}, f32[32,2048]{1,0:T(8,128)S(1)}, u32[]{:S(2)}, u32[]{:S(2)}) collective-permute-start(f32[32,2048]{1,0:T(8,128)S(1)} %get-tuple-element.54.own_ref), channel_id=1, source_target_pairs={{0,1},{1,0},{2,3},{3,2},{4,5},{5,4},{6,7},{7,6},{8,9},{9,8},{10,11... | collective-permute-start | bytes 786440 | tf_op jit(solution)/shard_map/ppermute | solution.py:30
  12.3 1.0 %collective-permute-done.1.halo_ref = f32[968,128]{1,0:T(8,128)S(1)} collective-permute-done((f32[968,128]{1,0:T(8,128)S(1)}, f32[968,128]{1,0:T(8,128)S(1)}, u32[]{:S(2)}, u32[]{:S(2)}) %collective-permute-start.1) | collective-permute-done | bytes 495648 | tf_op jit(solution)/shard_map/ppermute | solution.py:25
  14.0 1.9 %collective-permute-start.4 = (f32[1928,128]{1,0:T(8,128)S(1)}, f32[1928,128]{1,0:T(8,128)S(1)}, u32[]{:S(2)}, u32[]{:S(2)}) collective-permute-start(f32[1928,128]{1,0:T(8,128)S(1)} %get-tuple-element.58), channel_id=1, source_target_pairs={{2,0},{4,2},{6,4},{8,6},{10,8},{12,10},{14,12},{16,14},{18,16},{20... | collective-permute-start | bytes 2961416 | tf_op jit(solution)/shard_map/ppermute | solution.py:25
  15.9 2.7 %collective-permute-done.halo_ref = f32[968,128]{1,0:T(8,128)S(1)} collective-permute-done((f32[968,128]{1,0:T(8,128)S(1)}, f32[968,128]{1,0:T(8,128)S(1)}, u32[]{:S(2)}, u32[]{:S(2)}) %collective-permute-start) | collective-permute-done | bytes 495648 | tf_op jit(solution)/shard_map/ppermute | solution.py:25
  19.3 1.6 %collective-permute-start.2 = (f32[128,128]{1,0:T(8,128)S(1)}, f32[128,128]{1,0:T(8,128)S(1)}, u32[]{:S(2)}, u32[]{:S(2)}) collective-permute-start(f32[128,128]{1,0:T(8,128)S(1)} %get-tuple-element.53.own_ref), channel_id=1, source_target_pairs={{0,1},{1,0},{2,3},{3,2},{4,5},{5,4},{6,7},{7,6},{8,9},{9,8},{10,11... | collective-permute-start | bytes 196616 | tf_op jit(solution)/shard_map/ppermute | solution.py:30
  21.4 2.3 %collective-permute-done.2.other_ref = f32[128,128]{1,0:T(8,128)S(1)} collective-permute-done((f32[128,128]{1,0:T(8,128)S(1)}, f32[128,128]{1,0:T(8,128)S(1)}, u32[]{:S(2)}, u32[]{:S(2)}) %collective-permute-start.2) | collective-permute-done | bytes 65568 | tf_op jit(solution)/shard_map/ppermute | solution.py:30
  23.7 1.9 %collective-permute-start.5 = (f32[64,128]{1,0:T(8,128)S(1)}, f32[64,128]{1,0:T(8,128)S(1)}, u32[]{:S(2)}, u32[]{:S(2)}) collective-permute-start(f32[64,128]{1,0:T(8,128)S(1)} %get-tuple-element.62), channel_id=1, source_target_pairs={{2,0},{4,2},{6,4},{8,6},{10,8},{12,10},{14,12},{16,14},{18,16},{20... | collective-permute-start | bytes 98312 | tf_op jit(solution)/shard_map/ppermute | solution.py:25
  25.7 1.0 %shard_map.104.partial_ref = f32[1024,128]{1,0:T(8,128)S(1)} custom-call(f32[8192,128]{1,0:T(8,128)S(1)} %get-tuple-element.67.dual_ref, bf16[32,256]{1,0:T(8,128)(2,1)S(1)} %get-tuple-element.64.lhs_ref, f32[128,128]{1,0:T(8,128)S(1)} %get-tuple-element.65.scale_ref, f32[2048,128]{1,0:T(8,128)S(1)} %shard_map.100.s_ref.refs_0_, f32[2048,128]{1,0:T(8,128)S(1)} %bitcast.10, ...), custom_call_target="tpu_custom_call" | custom-call | flops 4429185024 | bytes 92274688 | tf_op jit(solution)/shard_map/pallas_call | solution.py:429
  26.7 1.0 %shard_map.102.partial_ref = f32[1024,128]{1,0:T(8,128)S(1)} custom-call(f32[8192,128]{1,0:T(8,128)S(1)} %get-tuple-element.63.dual_ref, bf16[32,256]{1,0:T(8,128)(2,1)S(1)} %get-tuple-element.64.lhs_ref, f32[128,128]{1,0:T(8,128)S(1)} %get-tuple-element.65.scale_ref, f32[2048,128]{1,0:T(8,128)S(1)} %shard_map.100.s_ref.refs_0_, f32[2048,128]{1,0:T(8,128)S(1)} %bitcast.11, ...), custom_call_target="tpu_custom_call" | custom-call | flops 4429185024 | bytes 92274688 | tf_op jit(solution)/shard_map/pallas_call | solution.py:429
  27.9 0.9 %shard_map.103 = (f32[1024,128]{1,0:T(8,128)S(1)}, f32[1024,128]{1,0:T(8,128)S(1)}, f32[968,128]{1,0:T(8,128)S(1)}) custom-call(f32[1024,128]{1,0:T(8,128)S(1)} %get-tuple-element.51.own_ref.refs_0_, f32[1928,128]{1,0:T(8,128)S(1)} %collective-permute-done.4.below_ref, bf16[64,96]{1,0:T(8,128)(2,1)S(1)} %get-tuple-element.59.next_ref, ...), custom_call_target="tpu_custom_call" | custom-call | flops 4429185024 | bytes 92274688 | tf_op jit(solution)/shard_map/pallas_call | solution.py:429
  28.8 3.3 %collective-permute-start.7 = (f32[968,128]{1,0:T(8,128)S(1)}, f32[968,128]{1,0:T(8,128)S(1)}, u32[]{:S(2)}, u32[]{:S(2)}) collective-permute-start(f32[968,128]{1,0:T(8,128)S(1)} %get-tuple-element.72), channel_id=1, source_target_pairs={{0,2},{2,4},{4,6},{6,8},{8,10},{10,12},{12,14},{14,16},{16,18},{18... | collective-permute-start | bytes 1486856 | tf_op jit(solution)/shard_map/ppermute | solution.py:25
  33.0 2.1 %collective-permute-start.8 = (f32[968,128]{1,0:T(8,128)S(1)}, f32[968,128]{1,0:T(8,128)S(1)}, u32[]{:S(2)}, u32[]{:S(2)}) collective-permute-start(f32[968,128]{1,0:T(8,128)S(1)} %get-tuple-element.79), channel_id=1, source_target_pairs={{0,2},{2,4},{4,6},{6,8},{8,10},{10,12},{12,14},{14,16},{16,18},{18... | collective-permute-start | bytes 1486856 | tf_op jit(solution)/shard_map/ppermute | solution.py:25
  36.0 1.6 %collective-permute-start.6 = (f32[32,2048]{1,0:T(8,128)S(1)}, f32[32,2048]{1,0:T(8,128)S(1)}, u32[]{:S(2)}, u32[]{:S(2)}) collective-permute-start(f32[32,2048]{1,0:T(8,128)S(1)} %shard_map.106.own_ref), channel_id=1, source_target_pairs={{0,1},{1,0},{2,3},{3,2},{4,5},{5,4},{6,7},{7,6},{8,9},{9,8},{10,11... | collective-permute-start | bytes 786440 | tf_op jit(solution)/shard_map/ppermute | solution.py:30
  39.0 1.0 %collective-permute-done.7.halo_ref = f32[968,128]{1,0:T(8,128)S(1)} collective-permute-done((f32[968,128]{1,0:T(8,128)S(1)}, f32[968,128]{1,0:T(8,128)S(1)}, u32[]{:S(2)}, u32[]{:S(2)}) %collective-permute-start.7) | collective-permute-done | bytes 495648 | tf_op jit(solution)/shard_map/ppermute | solution.py:25
  40.6 4.7 %collective-permute-done.8.halo_ref = f32[968,128]{1,0:T(8,128)S(1)} collective-permute-done((f32[968,128]{1,0:T(8,128)S(1)}, f32[968,128]{1,0:T(8,128)S(1)}, u32[]{:S(2)}, u32[]{:S(2)}) %collective-permute-start.8) | collective-permute-done | bytes 495648 | tf_op jit(solution)/shard_map/ppermute | solution.py:25
  45.9 1.6 %collective-permute-start.9 = (f32[128,128]{1,0:T(8,128)S(1)}, f32[128,128]{1,0:T(8,128)S(1)}, u32[]{:S(2)}, u32[]{:S(2)}) collective-permute-start(f32[128,128]{1,0:T(8,128)S(1)} %get-tuple-element.85.refs_5_), channel_id=1, source_target_pairs={{0,1},{1,0},{2,3},{3,2},{4,5},{5,4},{6,7},{7,6},{8,9},{9,8},{10,11... | collective-permute-start | bytes 196616 | tf_op jit(solution)/shard_map/ppermute | solution.py:30
  47.5 1.8 %shard_map.107 = (f32[2048,128]{1,0:T(8,128)}, f32[2048,128]{1,0:T(8,128)}) custom-call(bf16[128,96]{1,0:T(8,128)(2,1)S(1)} %get-tuple-element.45.lhs_ref, f32[32,2048]{1,0:T(8,128)S(1)} %shard_map.106.own_ref, f32[32,2048]{1,0:T(8,128)S(1)} %collective-permute-done.6.other_ref, f32[32,128]{1,0:T(8,128)S(1)} %get-tuple-element.55.bounds_ref, ...), custom_call_target="tpu_custom_call" | custom-call | flops 50331648 | bytes 2097152 | tf_op jit(solution)/shard_map/pallas_call | solution.py:429
  49.3 1.0 %collective-permute-done.9.refs_6_ = f32[128,128]{1,0:T(8,128)S(1)} collective-permute-done((f32[128,128]{1,0:T(8,128)S(1)}, f32[128,128]{1,0:T(8,128)S(1)}, u32[]{:S(2)}, u32[]{:S(2)}) %collective-permute-start.9) | collective-permute-done | bytes 65568 | tf_op jit(solution)/shard_map/ppermute | solution.py:30
  50.3 3.6 %shard_map.112 = f32[8,128,16,128]{3,2,1,0:T(8,128)} custom-call(f32[6144,128]{1,0:T(8,128)S(1)} %get-tuple-element.78.refs_0_, f32[6144,128]{1,0:T(8,128)S(1)} %get-tuple-element.82.refs_1_, f32[2048,128]{1,0:T(8,128)S(1)} %get-tuple-element.83.refs_2_, f32[2048,128]{1,0:T(8,128)S(1)} %get-tuple-element.84.refs_3_, f32[128,128]{1,0:T(8,128)S(1)} %bitcast.21, ...), custom_call_target="tpu_custom_call" | custom-call | flops 2097152 | bytes 16777216 | tf_op jit(solution)/shard_map/pallas_call | solution.py:429
  (31 shorter events, 7.1 us)
Async XLA Ops:
  0.6 8.5 %copy-start.6 = (s32[16]{0:T(128)S(1)}, s32[16]{0:T(128)}, u32[]{:S(2)}) copy-start(s32[16]{0:T(128)} %margin_ref.1) | copy-start | bytes 196
  0.6 8.5 %copy-start.5 = (f32[32]{0:T(128)S(1)}, f32[32]{0:T(128)}, u32[]{:S(2)}) copy-start(f32[32]{0:T(128)} %bounds_ref.1) | copy-start | bytes 388
  0.7 8.5 %copy-start.3 = (f32[1,128,32]{1,2,0:T(8,128)S(1)}, f32[1,128,32]{1,2,0:T(8,128)}, u32[]{:S(2)}) copy-start(f32[1,128,32]{1,2,0:T(8,128)} %param.11) | copy-start | bytes 49156
  0.7 8.5 %copy-start.4 = (f32[8,16]{1,0:T(8,128)S(1)}, f32[8,16]{1,0:T(8,128)}, u32[]{:S(2)}) copy-start(f32[8,16]{1,0:T(8,128)} %filters_ref.1) | copy-start | bytes 1540
  2.0 21.6 %copy-start.2 = (f32[8,16,128]{2,1,0:T(8,128)S(1)}, f32[8,16,128]{2,1,0:T(8,128)}, u32[]{:S(2)}) copy-start(f32[8,16,128]{2,1,0:T(8,128)} %param.9) | copy-start | bytes 196612
  2.0 11.2 %collective-permute-start.1 = (f32[968,128]{1,0:T(8,128)S(1)}, f32[968,128]{1,0:T(8,128)S(1)}, u32[]{:S(2)}, u32[]{:S(2)}) collective-permute-start(f32[968,128]{1,0:T(8,128)S(1)} %get-tuple-element.50), channel_id=1, source_target_pairs={{0,2},{2,4},{4,6},{6,8},{8,10},{10,12},{12,14},{14,16},{16,18},{18... | collective-permute-start | bytes 1486856 | tf_op jit(solution)/shard_map/ppermute | solution.py:25
  5.4 20.2 %copy-start = (f32[128,16,128]{2,1,0:T(8,128)S(1)}, f32[128,16,128]{2,1,0:T(8,128)}, u32[]{:S(2)}) copy-start(f32[128,16,128]{2,1,0:T(8,128)} %param.7) | copy-start | bytes 3145732
  5.5 20.2 %copy-start.1 = (f32[128,16,128]{2,1,0:T(8,128)S(1)}, f32[128,16,128]{2,1,0:T(8,128)}, u32[]{:S(2)}) copy-start(f32[128,16,128]{2,1,0:T(8,128)} %param.8) | copy-start | bytes 3145732
  5.5 13.2 %collective-permute-start = (f32[968,128]{1,0:T(8,128)S(1)}, f32[968,128]{1,0:T(8,128)S(1)}, u32[]{:S(2)}, u32[]{:S(2)}) collective-permute-start(f32[968,128]{1,0:T(8,128)S(1)} %get-tuple-element.47), channel_id=1, source_target_pairs={{0,2},{2,4},{4,6},{6,8},{8,10},{10,12},{12,14},{14,16},{16,18},{18... | collective-permute-start | bytes 1486856 | tf_op jit(solution)/shard_map/ppermute | solution.py:25
  10.7 10.2 %collective-permute-start.3 = (f32[32,2048]{1,0:T(8,128)S(1)}, f32[32,2048]{1,0:T(8,128)S(1)}, u32[]{:S(2)}, u32[]{:S(2)}) collective-permute-start(f32[32,2048]{1,0:T(8,128)S(1)} %get-tuple-element.54.own_ref), channel_id=1, source_target_pairs={{0,1},{1,0},{2,3},{3,2},{4,5},{5,4},{6,7},{7,6},{8,9},{9,8},{10,11... | collective-permute-start | bytes 786440 | tf_op jit(solution)/shard_map/ppermute | solution.py:30
  14.0 13.9 %collective-permute-start.4 = (f32[1928,128]{1,0:T(8,128)S(1)}, f32[1928,128]{1,0:T(8,128)S(1)}, u32[]{:S(2)}, u32[]{:S(2)}) collective-permute-start(f32[1928,128]{1,0:T(8,128)S(1)} %get-tuple-element.58), channel_id=1, source_target_pairs={{2,0},{4,2},{6,4},{8,6},{10,8},{12,10},{14,12},{16,14},{18,16},{20... | collective-permute-start | bytes 2961416 | tf_op jit(solution)/shard_map/ppermute | solution.py:25
  19.3 4.3 %collective-permute-start.2 = (f32[128,128]{1,0:T(8,128)S(1)}, f32[128,128]{1,0:T(8,128)S(1)}, u32[]{:S(2)}, u32[]{:S(2)}) collective-permute-start(f32[128,128]{1,0:T(8,128)S(1)} %get-tuple-element.53.own_ref), channel_id=1, source_target_pairs={{0,1},{1,0},{2,3},{3,2},{4,5},{5,4},{6,7},{7,6},{8,9},{9,8},{10,11... | collective-permute-start | bytes 196616 | tf_op jit(solution)/shard_map/ppermute | solution.py:30
  23.7 4.2 %collective-permute-start.5 = (f32[64,128]{1,0:T(8,128)S(1)}, f32[64,128]{1,0:T(8,128)S(1)}, u32[]{:S(2)}, u32[]{:S(2)}) collective-permute-start(f32[64,128]{1,0:T(8,128)S(1)} %get-tuple-element.62), channel_id=1, source_target_pairs={{2,0},{4,2},{6,4},{8,6},{10,8},{12,10},{14,12},{16,14},{18,16},{20... | collective-permute-start | bytes 98312 | tf_op jit(solution)/shard_map/ppermute | solution.py:25
  28.8 11.3 %collective-permute-start.7 = (f32[968,128]{1,0:T(8,128)S(1)}, f32[968,128]{1,0:T(8,128)S(1)}, u32[]{:S(2)}, u32[]{:S(2)}) collective-permute-start(f32[968,128]{1,0:T(8,128)S(1)} %get-tuple-element.72), channel_id=1, source_target_pairs={{0,2},{2,4},{4,6},{6,8},{8,10},{10,12},{12,14},{14,16},{16,18},{18... | collective-permute-start | bytes 1486856 | tf_op jit(solution)/shard_map/ppermute | solution.py:25
  33.0 12.3 %collective-permute-start.8 = (f32[968,128]{1,0:T(8,128)S(1)}, f32[968,128]{1,0:T(8,128)S(1)}, u32[]{:S(2)}, u32[]{:S(2)}) collective-permute-start(f32[968,128]{1,0:T(8,128)S(1)} %get-tuple-element.79), channel_id=1, source_target_pairs={{0,2},{2,4},{4,6},{6,8},{8,10},{10,12},{12,14},{14,16},{16,18},{18... | collective-permute-start | bytes 1486856 | tf_op jit(solution)/shard_map/ppermute | solution.py:25
  36.0 11.5 %collective-permute-start.6 = (f32[32,2048]{1,0:T(8,128)S(1)}, f32[32,2048]{1,0:T(8,128)S(1)}, u32[]{:S(2)}, u32[]{:S(2)}) collective-permute-start(f32[32,2048]{1,0:T(8,128)S(1)} %shard_map.106.own_ref), channel_id=1, source_target_pairs={{0,1},{1,0},{2,3},{3,2},{4,5},{5,4},{6,7},{7,6},{8,9},{9,8},{10,11... | collective-permute-start | bytes 786440 | tf_op jit(solution)/shard_map/ppermute | solution.py:30
  45.9 4.3 %collective-permute-start.9 = (f32[128,128]{1,0:T(8,128)S(1)}, f32[128,128]{1,0:T(8,128)S(1)}, u32[]{:S(2)}, u32[]{:S(2)}) collective-permute-start(f32[128,128]{1,0:T(8,128)S(1)} %get-tuple-element.85.refs_5_), channel_id=1, source_target_pairs={{0,1},{1,0},{2,3},{3,2},{4,5},{5,4},{6,7},{7,6},{8,9},{9,8},{10,11... | collective-permute-start | bytes 196616 | tf_op jit(solution)/shard_map/ppermute | solution.py:30

commit v10 on v8

--- a/solution.py
+++ b/solution.py
@@ -394,11 +394,13 @@
     turn = 0
     for index, (met_ref, free_ref) in enumerate(zip(met_refs, free_refs)):
         channels = met_ref.shape[0] // many
-        for start in range(0, channels, block):
+        opening = block // 2 if index == 0 else block
+        starts = [0, *range(opening, channels, block)]
+        for start, stop in zip(starts, [*starts[1:], channels]):
             slot = turn % slots
             for copy in pending[slot]:
                 copy.wait()
-            for channel in range(block):
+            for channel in range(stop - start):
                 met = met_ref[pl.ds((start + channel) * many, many), :] * scale[:many]
                 free = free_ref[pl.ds((start + channel) * rest, rest), :] * scale[many:]
                 first = second = 0
@@ -408,9 +410,9 @@
                     if count < height:
                         buffer[slot, basis, channel, count:] = free[second : second + height - count]
                         second += height - count
-            place = pl.ds(index * channels + start, block)
+            place = pl.ds(index * channels + start, stop - start)
             pending[slot] = [
-                pltpu.make_async_copy(buffer.at[slot, basis], out_ref.at[basis, place], sems.at[slot, basis])
+                pltpu.make_async_copy(buffer.at[slot, basis, pl.ds(0, stop - start)], out_ref.at[basis, place], sems.at[slot, basis])
                 for basis in range(bases)
             ]
             for copy in pending[slot]:

time: 54.2 us -> 54.4 us (level)
  no operation moved by 1% of the time
where the time goes in v10:
time: 54.4 us; the launch traced here: 54 us
  starting transfers between devices  21.1 us (39%)
  Pallas kernels  19 us (35%)
  waiting for transfers between devices  13 us (24%)
  between operations  0.88 us (2%)
    pallas_call x19, Pallas kernels, call(): pl.pallas_call(kernel, out_shape=outs, in_specs=ins, out_specs=out_specs...  19 us
    ppermute x6, starting transfers between devices, shift(): lax.ppermute(value, axis, [(source, source + steps) for source in range(i...  14.8 us
    ppermute x6, waiting for transfers between devices, shift(): lax.ppermute(value, axis, [(source, source + steps) for source in range(i...  9.74 us
    ppermute x4, starting transfers between devices, chan_pairs(): lax.ppermute(value, 'chan', [(source, source ^ stride) for source in rang...  6.34 us
    ppermute x4, waiting for transfers between devices, chan_pairs(): lax.ppermute(value, 'chan', [(source, source ^ stride) for source in rang...  3.24 us
  transfers between devices with their start and end apart: 10, of which 7 were waited for; matrix products, arithmetic and copies ran while one was open for 0% of the time, Pallas kernels for 24%

profile of v10, /device:TPU:16, one launch (start us, length us, event | category | flops | bytes accessed | tf_op | source)
XLA Modules:
  0.0 54.0 jit_solution(9276916393303720790)
XLA Ops:
  0.7 1.4 %shard_map.96 = (f32[1024,128]{1,0:T(8,128)S(1)}, f32[968,128]{1,0:T(8,128)S(1)}) custom-call(f32[2048,128]{1,0:T(8,128)} %bitcast.8, f32[2048,128]{1,0:T(8,128)} %bitcast.14), custom_call_target="tpu_custom_call" | custom-call | flops 524288 | bytes 1572864 | tf_op jit(solution)/shard_map/pallas_call | solution.py:431
  2.0 2.1 %collective-permute-start.1 = (f32[968,128]{1,0:T(8,128)S(1)}, f32[968,128]{1,0:T(8,128)S(1)}, u32[]{:S(2)}, u32[]{:S(2)}) collective-permute-start(f32[968,128]{1,0:T(8,128)S(1)} %get-tuple-element.50), channel_id=1, source_target_pairs={{0,2},{2,4},{4,6},{6,8},{8,10},{10,12},{12,14},{14,16},{16,18},{18... | collective-permute-start | bytes 1486856 | tf_op jit(solution)/shard_map/ppermute | solution.py:25
  4.1 1.3 %shard_map.95 = (f32[1024,128]{1,0:T(8,128)S(1)}, f32[968,128]{1,0:T(8,128)S(1)}) custom-call(f32[2048,128]{1,0:T(8,128)} %bitcast.9, f32[2048,128]{1,0:T(8,128)} %bitcast.15), custom_call_target="tpu_custom_call" | custom-call | flops 524288 | bytes 1572864 | tf_op jit(solution)/shard_map/pallas_call | solution.py:431
  5.5 3.6 %collective-permute-start = (f32[968,128]{1,0:T(8,128)S(1)}, f32[968,128]{1,0:T(8,128)S(1)}, u32[]{:S(2)}, u32[]{:S(2)}) collective-permute-start(f32[968,128]{1,0:T(8,128)S(1)} %get-tuple-element.47), channel_id=1, source_target_pairs={{0,2},{2,4},{4,6},{6,8},{8,10},{10,12},{12,14},{14,16},{16,18},{18... | collective-permute-start | bytes 1486856 | tf_op jit(solution)/shard_map/ppermute | solution.py:25
  9.2 0.9 %shard_map.94 = (bf16[128,96]{1,0:T(8,128)(2,1)S(1)}, bf16[128,48]{1,0:T(8,128)(2,1)S(1)}, bf16[96,48]{1,0:T(8,128)(2,1)S(1)}, bf16[64,96]{1,0:T(8,128)(2,1)S(1)...) custom-call(f32[8,16]{1,0:T(8,128)S(1)} %copy-done.4, ...), custom_call_target="tpu_custom_call" | custom-call | flops 100000 | bytes 100000 | tf_op jit(solution)/shard_map/pallas_call | solution.py:431
  10.7 1.6 %collective-permute-start.3 = (f32[32,2048]{1,0:T(8,128)S(1)}, f32[32,2048]{1,0:T(8,128)S(1)}, u32[]{:S(2)}, u32[]{:S(2)}) collective-permute-start(f32[32,2048]{1,0:T(8,128)S(1)} %get-tuple-element.54.own_ref), channel_id=1, source_target_pairs={{0,1},{1,0},{2,3},{3,2},{4,5},{5,4},{6,7},{7,6},{8,9},{9,8},{10,11... | collective-permute-start | bytes 786440 | tf_op jit(solution)/shard_map/ppermute | solution.py:30
  12.3 1.0 %collective-permute-done.1.halo_ref = f32[968,128]{1,0:T(8,128)S(1)} collective-permute-done((f32[968,128]{1,0:T(8,128)S(1)}, f32[968,128]{1,0:T(8,128)S(1)}, u32[]{:S(2)}, u32[]{:S(2)}) %collective-permute-start.1) | collective-permute-done | bytes 495648 | tf_op jit(solution)/shard_map/ppermute | solution.py:25
  14.0 1.9 %collective-permute-start.4 = (f32[1928,128]{1,0:T(8,128)S(1)}, f32[1928,128]{1,0:T(8,128)S(1)}, u32[]{:S(2)}, u32[]{:S(2)}) collective-permute-start(f32[1928,128]{1,0:T(8,128)S(1)} %get-tuple-element.58), channel_id=1, source_target_pairs={{2,0},{4,2},{6,4},{8,6},{10,8},{12,10},{14,12},{16,14},{18,16},{20... | collective-permute-start | bytes 2961416 | tf_op jit(solution)/shard_map/ppermute | solution.py:25
  15.9 2.7 %collective-permute-done.halo_ref = f32[968,128]{1,0:T(8,128)S(1)} collective-permute-done((f32[968,128]{1,0:T(8,128)S(1)}, f32[968,128]{1,0:T(8,128)S(1)}, u32[]{:S(2)}, u32[]{:S(2)}) %collective-permute-start) | collective-permute-done | bytes 495648 | tf_op jit(solution)/shard_map/ppermute | solution.py:25
  19.3 1.6 %collective-permute-start.2 = (f32[128,128]{1,0:T(8,128)S(1)}, f32[128,128]{1,0:T(8,128)S(1)}, u32[]{:S(2)}, u32[]{:S(2)}) collective-permute-start(f32[128,128]{1,0:T(8,128)S(1)} %get-tuple-element.53.own_ref), channel_id=1, source_target_pairs={{0,1},{1,0},{2,3},{3,2},{4,5},{5,4},{6,7},{7,6},{8,9},{9,8},{10,11... | collective-permute-start | bytes 196616 | tf_op jit(solution)/shard_map/ppermute | solution.py:30
  21.4 2.3 %collective-permute-done.2.other_ref = f32[128,128]{1,0:T(8,128)S(1)} collective-permute-done((f32[128,128]{1,0:T(8,128)S(1)}, f32[128,128]{1,0:T(8,128)S(1)}, u32[]{:S(2)}, u32[]{:S(2)}) %collective-permute-start.2) | collective-permute-done | bytes 65568 | tf_op jit(solution)/shard_map/ppermute | solution.py:30
  23.7 1.9 %collective-permute-start.5 = (f32[64,128]{1,0:T(8,128)S(1)}, f32[64,128]{1,0:T(8,128)S(1)}, u32[]{:S(2)}, u32[]{:S(2)}) collective-permute-start(f32[64,128]{1,0:T(8,128)S(1)} %get-tuple-element.62), channel_id=1, source_target_pairs={{2,0},{4,2},{6,4},{8,6},{10,8},{12,10},{14,12},{16,14},{18,16},{20... | collective-permute-start | bytes 98312 | tf_op jit(solution)/shard_map/ppermute | solution.py:25
  25.7 1.1 %shard_map.104.partial_ref = f32[1024,128]{1,0:T(8,128)S(1)} custom-call(f32[8192,128]{1,0:T(8,128)S(1)} %get-tuple-element.67.dual_ref, bf16[32,256]{1,0:T(8,128)(2,1)S(1)} %get-tuple-element.64.lhs_ref, f32[128,128]{1,0:T(8,128)S(1)} %get-tuple-element.65.scale_ref, f32[2048,128]{1,0:T(8,128)S(1)} %shard_map.100.s_ref.refs_0_, f32[2048,128]{1,0:T(8,128)S(1)} %bitcast.10, ...), custom_call_target="tpu_custom_call" | custom-call | flops 4429185024 | bytes 92274688 | tf_op jit(solution)/shard_map/pallas_call | solution.py:431
  26.7 1.1 %shard_map.102.partial_ref = f32[1024,128]{1,0:T(8,128)S(1)} custom-call(f32[8192,128]{1,0:T(8,128)S(1)} %get-tuple-element.63.dual_ref, bf16[32,256]{1,0:T(8,128)(2,1)S(1)} %get-tuple-element.64.lhs_ref, f32[128,128]{1,0:T(8,128)S(1)} %get-tuple-element.65.scale_ref, f32[2048,128]{1,0:T(8,128)S(1)} %shard_map.100.s_ref.refs_0_, f32[2048,128]{1,0:T(8,128)S(1)} %bitcast.11, ...), custom_call_target="tpu_custom_call" | custom-call | flops 4429185024 | bytes 92274688 | tf_op jit(solution)/shard_map/pallas_call | solution.py:431
  27.9 0.9 %shard_map.103 = (f32[1024,128]{1,0:T(8,128)S(1)}, f32[1024,128]{1,0:T(8,128)S(1)}, f32[968,128]{1,0:T(8,128)S(1)}) custom-call(f32[1024,128]{1,0:T(8,128)S(1)} %get-tuple-element.51.own_ref.refs_0_, f32[1928,128]{1,0:T(8,128)S(1)} %collective-permute-done.4.below_ref, bf16[64,96]{1,0:T(8,128)(2,1)S(1)} %get-tuple-element.59.next_ref, ...), custom_call_target="tpu_custom_call" | custom-call | flops 4429185024 | bytes 92274688 | tf_op jit(solution)/shard_map/pallas_call | solution.py:431
  28.8 3.3 %collective-permute-start.7 = (f32[968,128]{1,0:T(8,128)S(1)}, f32[968,128]{1,0:T(8,128)S(1)}, u32[]{:S(2)}, u32[]{:S(2)}) collective-permute-start(f32[968,128]{1,0:T(8,128)S(1)} %get-tuple-element.72), channel_id=1, source_target_pairs={{0,2},{2,4},{4,6},{6,8},{8,10},{10,12},{12,14},{14,16},{16,18},{18... | collective-permute-start | bytes 1486856 | tf_op jit(solution)/shard_map/ppermute | solution.py:25
  33.0 1.9 %collective-permute-start.8 = (f32[968,128]{1,0:T(8,128)S(1)}, f32[968,128]{1,0:T(8,128)S(1)}, u32[]{:S(2)}, u32[]{:S(2)}) collective-permute-start(f32[968,128]{1,0:T(8,128)S(1)} %get-tuple-element.79), channel_id=1, source_target_pairs={{0,2},{2,4},{4,6},{6,8},{8,10},{10,12},{12,14},{14,16},{16,18},{18... | collective-permute-start | bytes 1486856 | tf_op jit(solution)/shard_map/ppermute | solution.py:25
  35.9 1.6 %collective-permute-start.6 = (f32[32,2048]{1,0:T(8,128)S(1)}, f32[32,2048]{1,0:T(8,128)S(1)}, u32[]{:S(2)}, u32[]{:S(2)}) collective-permute-start(f32[32,2048]{1,0:T(8,128)S(1)} %shard_map.106.own_ref), channel_id=1, source_target_pairs={{0,1},{1,0},{2,3},{3,2},{4,5},{5,4},{6,7},{7,6},{8,9},{9,8},{10,11... | collective-permute-start | bytes 786440 | tf_op jit(solution)/shard_map/ppermute | solution.py:30
  38.9 1.2 %collective-permute-done.7.halo_ref = f32[968,128]{1,0:T(8,128)S(1)} collective-permute-done((f32[968,128]{1,0:T(8,128)S(1)}, f32[968,128]{1,0:T(8,128)S(1)}, u32[]{:S(2)}, u32[]{:S(2)}) %collective-permute-start.7) | collective-permute-done | bytes 495648 | tf_op jit(solution)/shard_map/ppermute | solution.py:25
  40.6 4.7 %collective-permute-done.8.halo_ref = f32[968,128]{1,0:T(8,128)S(1)} collective-permute-done((f32[968,128]{1,0:T(8,128)S(1)}, f32[968,128]{1,0:T(8,128)S(1)}, u32[]{:S(2)}, u32[]{:S(2)}) %collective-permute-start.8) | collective-permute-done | bytes 495648 | tf_op jit(solution)/shard_map/ppermute | solution.py:25
  46.0 1.6 %collective-permute-start.9 = (f32[128,128]{1,0:T(8,128)S(1)}, f32[128,128]{1,0:T(8,128)S(1)}, u32[]{:S(2)}, u32[]{:S(2)}) collective-permute-start(f32[128,128]{1,0:T(8,128)S(1)} %get-tuple-element.85.refs_5_), channel_id=1, source_target_pairs={{0,1},{1,0},{2,3},{3,2},{4,5},{5,4},{6,7},{7,6},{8,9},{9,8},{10,11... | collective-permute-start | bytes 196616 | tf_op jit(solution)/shard_map/ppermute | solution.py:30
  47.5 1.8 %shard_map.107 = (f32[2048,128]{1,0:T(8,128)}, f32[2048,128]{1,0:T(8,128)}) custom-call(bf16[128,96]{1,0:T(8,128)(2,1)S(1)} %get-tuple-element.45.lhs_ref, f32[32,2048]{1,0:T(8,128)S(1)} %shard_map.106.own_ref, f32[32,2048]{1,0:T(8,128)S(1)} %collective-permute-done.6.other_ref, f32[32,128]{1,0:T(8,128)S(1)} %get-tuple-element.55.bounds_ref, ...), custom_call_target="tpu_custom_call" | custom-call | flops 50331648 | bytes 2097152 | tf_op jit(solution)/shard_map/pallas_call | solution.py:431
  49.3 1.0 %collective-permute-done.9.refs_6_ = f32[128,128]{1,0:T(8,128)S(1)} collective-permute-done((f32[128,128]{1,0:T(8,128)S(1)}, f32[128,128]{1,0:T(8,128)S(1)}, u32[]{:S(2)}, u32[]{:S(2)}) %collective-permute-start.9) | collective-permute-done | bytes 65568 | tf_op jit(solution)/shard_map/ppermute | solution.py:30
  50.3 3.8 %shard_map.112 = f32[8,128,16,128]{3,2,1,0:T(8,128)} custom-call(f32[6144,128]{1,0:T(8,128)S(1)} %get-tuple-element.78.refs_0_, f32[6144,128]{1,0:T(8,128)S(1)} %get-tuple-element.82.refs_1_, f32[2048,128]{1,0:T(8,128)S(1)} %get-tuple-element.83.refs_2_, f32[2048,128]{1,0:T(8,128)S(1)} %get-tuple-element.84.refs_3_, f32[128,128]{1,0:T(8,128)S(1)} %bitcast.21, ...), custom_call_target="tpu_custom_call" | custom-call | flops 2097152 | bytes 16777216 | tf_op jit(solution)/shard_map/pallas_call | solution.py:431
  (31 shorter events, 7.0 us)
Async XLA Ops:
  0.6 8.5 %copy-start.6 = (s32[16]{0:T(128)S(1)}, s32[16]{0:T(128)}, u32[]{:S(2)}) copy-start(s32[16]{0:T(128)} %margin_ref.1) | copy-start | bytes 196
  0.6 8.5 %copy-start.5 = (f32[32]{0:T(128)S(1)}, f32[32]{0:T(128)}, u32[]{:S(2)}) copy-start(f32[32]{0:T(128)} %bounds_ref.1) | copy-start | bytes 388
  0.7 8.5 %copy-start.3 = (f32[1,128,32]{1,2,0:T(8,128)S(1)}, f32[1,128,32]{1,2,0:T(8,128)}, u32[]{:S(2)}) copy-start(f32[1,128,32]{1,2,0:T(8,128)} %param.11) | copy-start | bytes 49156
  0.7 8.5 %copy-start.4 = (f32[8,16]{1,0:T(8,128)S(1)}, f32[8,16]{1,0:T(8,128)}, u32[]{:S(2)}) copy-start(f32[8,16]{1,0:T(8,128)} %filters_ref.1) | copy-start | bytes 1540
  2.0 21.6 %copy-start.2 = (f32[8,16,128]{2,1,0:T(8,128)S(1)}, f32[8,16,128]{2,1,0:T(8,128)}, u32[]{:S(2)}) copy-start(f32[8,16,128]{2,1,0:T(8,128)} %param.9) | copy-start | bytes 196612
  2.0 11.2 %collective-permute-start.1 = (f32[968,128]{1,0:T(8,128)S(1)}, f32[968,128]{1,0:T(8,128)S(1)}, u32[]{:S(2)}, u32[]{:S(2)}) collective-permute-start(f32[968,128]{1,0:T(8,128)S(1)} %get-tuple-element.50), channel_id=1, source_target_pairs={{0,2},{2,4},{4,6},{6,8},{8,10},{10,12},{12,14},{14,16},{16,18},{18... | collective-permute-start | bytes 1486856 | tf_op jit(solution)/shard_map/ppermute | solution.py:25
  5.4 20.2 %copy-start = (f32[128,16,128]{2,1,0:T(8,128)S(1)}, f32[128,16,128]{2,1,0:T(8,128)}, u32[]{:S(2)}) copy-start(f32[128,16,128]{2,1,0:T(8,128)} %param.7) | copy-start | bytes 3145732
  5.5 20.2 %copy-start.1 = (f32[128,16,128]{2,1,0:T(8,128)S(1)}, f32[128,16,128]{2,1,0:T(8,128)}, u32[]{:S(2)}) copy-start(f32[128,16,128]{2,1,0:T(8,128)} %param.8) | copy-start | bytes 3145732
  5.5 13.2 %collective-permute-start = (f32[968,128]{1,0:T(8,128)S(1)}, f32[968,128]{1,0:T(8,128)S(1)}, u32[]{:S(2)}, u32[]{:S(2)}) collective-permute-start(f32[968,128]{1,0:T(8,128)S(1)} %get-tuple-element.47), channel_id=1, source_target_pairs={{0,2},{2,4},{4,6},{6,8},{8,10},{10,12},{12,14},{14,16},{16,18},{18... | collective-permute-start | bytes 1486856 | tf_op jit(solution)/shard_map/ppermute | solution.py:25
  10.7 10.2 %collective-permute-start.3 = (f32[32,2048]{1,0:T(8,128)S(1)}, f32[32,2048]{1,0:T(8,128)S(1)}, u32[]{:S(2)}, u32[]{:S(2)}) collective-permute-start(f32[32,2048]{1,0:T(8,128)S(1)} %get-tuple-element.54.own_ref), channel_id=1, source_target_pairs={{0,1},{1,0},{2,3},{3,2},{4,5},{5,4},{6,7},{7,6},{8,9},{9,8},{10,11... | collective-permute-start | bytes 786440 | tf_op jit(solution)/shard_map/ppermute | solution.py:30
  14.0 13.9 %collective-permute-start.4 = (f32[1928,128]{1,0:T(8,128)S(1)}, f32[1928,128]{1,0:T(8,128)S(1)}, u32[]{:S(2)}, u32[]{:S(2)}) collective-permute-start(f32[1928,128]{1,0:T(8,128)S(1)} %get-tuple-element.58), channel_id=1, source_target_pairs={{2,0},{4,2},{6,4},{8,6},{10,8},{12,10},{14,12},{16,14},{18,16},{20... | collective-permute-start | bytes 2961416 | tf_op jit(solution)/shard_map/ppermute | solution.py:25
  19.3 4.3 %collective-permute-start.2 = (f32[128,128]{1,0:T(8,128)S(1)}, f32[128,128]{1,0:T(8,128)S(1)}, u32[]{:S(2)}, u32[]{:S(2)}) collective-permute-start(f32[128,128]{1,0:T(8,128)S(1)} %get-tuple-element.53.own_ref), channel_id=1, source_target_pairs={{0,1},{1,0},{2,3},{3,2},{4,5},{5,4},{6,7},{7,6},{8,9},{9,8},{10,11... | collective-permute-start | bytes 196616 | tf_op jit(solution)/shard_map/ppermute | solution.py:30
  23.7 4.2 %collective-permute-start.5 = (f32[64,128]{1,0:T(8,128)S(1)}, f32[64,128]{1,0:T(8,128)S(1)}, u32[]{:S(2)}, u32[]{:S(2)}) collective-permute-start(f32[64,128]{1,0:T(8,128)S(1)} %get-tuple-element.62), channel_id=1, source_target_pairs={{2,0},{4,2},{6,4},{8,6},{10,8},{12,10},{14,12},{16,14},{18,16},{20... | collective-permute-start | bytes 98312 | tf_op jit(solution)/shard_map/ppermute | solution.py:25
  28.8 11.3 %collective-permute-start.7 = (f32[968,128]{1,0:T(8,128)S(1)}, f32[968,128]{1,0:T(8,128)S(1)}, u32[]{:S(2)}, u32[]{:S(2)}) collective-permute-start(f32[968,128]{1,0:T(8,128)S(1)} %get-tuple-element.72), channel_id=1, source_target_pairs={{0,2},{2,4},{4,6},{6,8},{8,10},{10,12},{12,14},{14,16},{16,18},{18... | collective-permute-start | bytes 1486856 | tf_op jit(solution)/shard_map/ppermute | solution.py:25
  33.0 12.3 %collective-permute-start.8 = (f32[968,128]{1,0:T(8,128)S(1)}, f32[968,128]{1,0:T(8,128)S(1)}, u32[]{:S(2)}, u32[]{:S(2)}) collective-permute-start(f32[968,128]{1,0:T(8,128)S(1)} %get-tuple-element.79), channel_id=1, source_target_pairs={{0,2},{2,4},{4,6},{6,8},{8,10},{10,12},{12,14},{14,16},{16,18},{18... | collective-permute-start | bytes 1486856 | tf_op jit(solution)/shard_map/ppermute | solution.py:25
  35.9 11.7 %collective-permute-start.6 = (f32[32,2048]{1,0:T(8,128)S(1)}, f32[32,2048]{1,0:T(8,128)S(1)}, u32[]{:S(2)}, u32[]{:S(2)}) collective-permute-start(f32[32,2048]{1,0:T(8,128)S(1)} %shard_map.106.own_ref), channel_id=1, source_target_pairs={{0,1},{1,0},{2,3},{3,2},{4,5},{5,4},{6,7},{7,6},{8,9},{9,8},{10,11... | collective-permute-start | bytes 786440 | tf_op jit(solution)/shard_map/ppermute | solution.py:30
  46.0 4.3 %collective-permute-start.9 = (f32[128,128]{1,0:T(8,128)S(1)}, f32[128,128]{1,0:T(8,128)S(1)}, u32[]{:S(2)}, u32[]{:S(2)}) collective-permute-start(f32[128,128]{1,0:T(8,128)S(1)} %get-tuple-element.85.refs_5_), channel_id=1, source_target_pairs={{0,1},{1,0},{2,3},{3,2},{4,5},{5,4},{6,7},{7,6},{8,9},{9,8},{10,11... | collective-permute-start | bytes 196616 | tf_op jit(solution)/shard_map/ppermute | solution.py:30
